TPU v7x, 256 devices: a whole 4x4x8 slice. The times are simulated.
256 devices in a mesh: lon: 64 (over y_hi, x, z), lat: 4 (over y_lo, core).
Axes of the slice: x: 4, y: 4 (y_hi: 2, y_lo: 2; y = y_hi * 2 + y_lo), z: 8, core: 2. Of those that a mesh axis runs over, the one named last changes fastest.
Arguments:
- expanded: bfloat16 [32, 1024, 3072], P('lat', 'lon'), may hold values from -6 to 6
- stream: bfloat16 [32, 1024, 768], P('lat', 'lon'), may hold values from -6 to 6
- land: int32 [32, 1024], P('lat', 'lon'), may hold values 0 or 1
- polar: int32 [32], replicated, may hold values from 0 to 1, as said below
- land_shift: float32 [3072], replicated, may hold values from -4 to 4
- dw_kernel: float32 [3, 3, 3072], replicated, may hold values from -2 to 2
- w_proj: bfloat16 [3072, 768], replicated, may hold values from -0.109375 to 0.109375
- w_qkv: bfloat16 [768, 2304], replicated, may hold values from -0.21875 to 0.21875
- w_out: bfloat16 [768, 768], replicated, may hold values from -0.21875 to 0.21875
- rel_bias: float32 [24, 15, 8], replicated, may hold values from -2 to 250
Outputs:
- mixed_out: bfloat16 [32, 1024, 768], P('lat', 'lon')
Inputs may be any that keep to these rules, and one draw needn't show every extreme that they name: `polar`: 1 marks the first a and the last b token rows, 1 <= a, b <= 4, at least one of a, b equal to 4; all other rows are 0.
All inputs are finite; a program needn't handle non-finite values. No bound on the sum of `land` on one device may be relied on, other than what follows from the above.
Results may differ from a plain program's by a relative error of at most 0.0075.
Values may be sent and summed in bfloat16 or wider, within the bound.
No kernel may reach another device: no remote copies, remote signals or barrier semaphores. Data moves between devices by JAX's collectives and lax.ppermute only.
A program may use at most 128 MiB of HBM per device.

v0:
```python
import functools

import jax
import jax.numpy as jnp
import numpy as np
from jax import lax
from jax.experimental import pallas as pl
from jax.experimental.pallas import tpu as pltpu
from jax.sharding import Mesh
from jax.sharding import PartitionSpec as P

GRID = 8
EPS = 1e-05
NEG = -1e30
F32 = jnp.float32
BF16 = jnp.bfloat16
VM = pl.BlockSpec(memory_space=pltpu.VMEM)
SM = pl.BlockSpec(memory_space=pltpu.SMEM)
HBM = pl.BlockSpec(memory_space=pl.ANY)


def send_order(rows, cols):
    strips = rows // 2
    order = []
    for s in range(strips):
        for c2 in range(cols // 2):
            for m in range(2):
                for c1 in range(2):
                    order.append((m * strips + s) * cols + 2 * c2 + c1)
    return np.array(order)


def pack_columns(flags, e_ref, ra_ref, rb_ref, ca_ref, cb_ref, first, last):
    lat_even = flags[0] == 1
    lon_even = flags[1] == 1
    rows, cols, _ = e_ref.shape
    ra = ra_ref[...].astype(F32)
    rb = rb_ref[...].astype(F32)
    top = jnp.where(lat_even, rb, ra)
    bottom = jnp.where(lat_even, ra, rb)
    for r in range(rows + 2):
        line = top if r == 0 else bottom if r == rows + 1 else e_ref[r - 1].astype(F32)
        first[r : r + 1, :] = line[0:1]
        last[r : r + 1, :] = line[cols - 1 : cols]
    a = jnp.where(lon_even, last[...], first[...])
    b = jnp.where(lon_even, first[...], last[...])
    ca_ref[...] = a.astype(BF16)
    cb_ref[...] = b.astype(BF16)


def gelu(x):
    inner = np.float32(np.sqrt(2 / np.pi)) * (x + np.float32(0.044715) * (x * x * x))
    return x * (np.float32(0.5) * (np.float32(1.0) + jnp.tanh(inner)))


def mix_kernel(
    flags, e_ref, ra_ref, rb_ref, ca_ref, cb_ref, land_ref, taps_ref, w_hbm, stream_ref, perm_ref,
    mixed_ref, out_ref, w_buf, act, total, sem, *, chunk,
):
    rows, cols, width_exp = e_ref.shape
    tokens = rows * cols
    steps = width_exp // chunk

    def fetch(i):
        return pltpu.make_async_copy(
            w_hbm.at[pl.ds(i * chunk, chunk), :], w_buf.at[pl.ds(i * chunk, chunk), :], sem.at[i]
        )

    for i in range(steps):
        fetch(i).start()
    lat_even = flags[0] == 1
    lon_even = flags[1] == 1
    sub = lax.broadcasted_iota(jnp.int32, (cols, 128), 0)
    is_first = sub == 0
    is_last = sub == cols - 1

    def depthwise(at):
        lanes = pl.ds(at, 128)
        ra = ra_ref[:, lanes].astype(F32)
        rb = rb_ref[:, lanes].astype(F32)
        x = [jnp.where(lat_even, rb, ra)]
        x += [e_ref[r, :, lanes].astype(F32) for r in range(rows)]
        x += [jnp.where(lat_even, ra, rb)]
        ca = ca_ref[:, lanes].astype(F32)
        cb = cb_ref[:, lanes].astype(F32)
        left = jnp.where(lon_even, cb, ca)
        right = jnp.where(lon_even, ca, cb)
        tap = [[taps_ref[3 * a + b : 3 * a + b + 1, lanes] for b in range(3)] for a in range(3)]
        shift = taps_ref[9:10, lanes]
        from_left = sum(tap[a][0] * left[a : a + rows] for a in range(3))
        from_right = sum(tap[a][2] * right[a : a + rows] for a in range(3))
        for r in range(rows):
            y = [tap[0][b] * x[r] + tap[1][b] * x[r + 1] + tap[2][b] * x[r + 2] for b in range(3)]
            y0 = jnp.where(is_first, from_left[r : r + 1], pltpu.roll(y[0], 1, 0))
            y2 = jnp.where(is_last, from_right[r : r + 1], pltpu.roll(y[2], cols - 1, 0))
            filtered = land_ref[r] * shift + y[1] + (y0 + y2)
            act[r * cols : (r + 1) * cols, lanes] = gelu(filtered).astype(BF16)

    def conv(i):
        for k in range(chunk // 128):
            depthwise(pl.multiple_of(i * chunk + k * 128, 128))

    def project(i):
        at = pl.multiple_of(i * chunk, chunk)
        return jnp.dot(
            act[:, pl.ds(at, chunk)], w_buf[pl.ds(at, chunk), :], preferred_element_type=F32
        )

    total[...] = stream_ref[...].astype(F32)
    conv(0)

    def step(i, carry):
        fetch(i - 1).wait()
        conv(i)
        total[...] += project(i - 1)
        return carry

    lax.fori_loop(1, steps, step, 0)
    fetch(steps - 1).wait()
    mixed = (total[...] + project(steps - 1)).astype(BF16)
    mixed_ref[...] = mixed
    flat = mixed.astype(F32)
    centred = flat - jnp.mean(flat, axis=1, keepdims=True)
    spread = jnp.mean(centred * centred, axis=1, keepdims=True)
    normed = (centred * lax.rsqrt(spread + EPS)).astype(BF16)
    sent = jnp.dot(perm_ref[...], normed, preferred_element_type=F32)
    for k in range(tokens // 4):
        out_ref[k] = sent[4 * k : 4 * k + 4].astype(BF16)


def attend_kernel(x_ref, w_ref, bias_ref, out_ref, x_buf, o_buf, *, heads):
    tokens = 4 * x_ref.shape[0]
    width = x_ref.shape[2]
    head_dim = width // heads
    for k in range(tokens // 4):
        x_buf[4 * k : 4 * k + 4, :] = x_ref[k].astype(F32)
    x = x_buf[...].astype(BF16)
    scale = np.float32(head_dim**-0.5)
    per = 128 // head_dim
    lane_head = lax.broadcasted_iota(jnp.int32, (tokens, 128), 1) // head_dim
    ones = jnp.ones((16, tokens), BF16)

    def project(col):
        return jnp.dot(x, w_ref[:, col : col + 128], preferred_element_type=F32)

    for p in range(heads // per):
        q = project(128 * p)
        k = project(width + 128 * p).astype(BF16)
        v = project(2 * width + 128 * p)
        v_t = jnp.concatenate([jnp.transpose(v).astype(BF16), ones], axis=0)
        queries = jnp.concatenate(
            [jnp.where(lane_head == j, q, 0.0).astype(BF16) for j in range(per)], axis=0
        )
        scores = lax.dot_general(
            k, queries, (((1,), (1,)), ((), ())), preferred_element_type=F32
        )
        weights = []
        for j in range(per):
            base = bias_ref[p * per + j]
            bias = jnp.concatenate(
                [base if n == 0 else pltpu.roll(base, 16 * n, 1) for n in range(GRID)], axis=0
            )
            s = scores[:, tokens * j : tokens * (j + 1)] * scale + bias
            weights.append(jnp.exp(s - jnp.max(s, axis=0, keepdims=True)).astype(BF16))
        summed = jnp.dot(v_t, jnp.concatenate(weights, axis=1), preferred_element_type=F32)
        parts = []
        for j in range(per):
            block = summed[:, tokens * j : tokens * (j + 1)]
            parts.append(
                block[head_dim * j : head_dim * (j + 1)] * (1.0 / block[128 : 129])
            )
        o_buf[:, 128 * p : 128 * (p + 1)] = jnp.transpose(jnp.concatenate(parts, axis=0))
    for k in range(tokens // 4):
        out_ref[k] = o_buf[4 * k : 4 * k + 4, :].astype(BF16)


def out_kernel(a_ref, w_ref, mixed_ref, perm_ref, out_ref, a_buf):
    tokens = 4 * a_ref.shape[0]
    for k in range(tokens // 4):
        a_buf[4 * k : 4 * k + 4, :] = a_ref[k].astype(F32)
    attended = jnp.dot(
        perm_ref[...], a_buf[...].astype(BF16), preferred_element_type=F32
    ).astype(BF16)
    result = mixed_ref[...].astype(F32) + jnp.dot(
        attended, w_ref[...], preferred_element_type=F32
    )
    out_ref[...] = result.astype(BF16)


def bias_choice():
    side = 2 * GRID - 1
    choose = np.zeros((side * GRID, 2 * GRID, 128), np.float32)
    block = np.full((2 * GRID, 128), NEG, np.float32)
    for mk in range(GRID):
        for gk in range(2):
            for nq in range(GRID):
                for mq in range(GRID):
                    for gq in range(2):
                        r, q = 2 * mk + gk, 16 * nq + 2 * mq + gq
                        choose[(mk - mq + GRID - 1) * GRID + (-nq) % GRID, r, q] = 1.0
                        if gk == gq:
                            block[r, q] = 0.0
    return choose, block


def local(expanded, stream, land, polar, land_shift, dw_kernel, w_proj, w_qkv, w_out, rel_bias):
    rows, cols, width_exp = expanded.shape
    width = stream.shape[2]
    heads = rel_bias.shape[0]
    tokens = rows * cols
    lon, lat = ("nhi", "nlo"), "lat"
    lons, lats = lax.axis_size(lon), lax.axis_size(lat)
    everyone = lon + (lat,)
    lat_at = lax.axis_index(lat)
    lon_at = lax.axis_index(lon)
    lat_even = lat_at % 2 == 0
    lon_even = lon_at % 2 == 0
    flags = jnp.stack([lat_even, lon_even]).astype(jnp.int32)
    top_row, bottom_row = expanded[0], expanded[rows - 1]
    row_a = jnp.where(lat_even, bottom_row, top_row)
    row_b = jnp.where(lat_even, top_row, bottom_row)
    got_a = lax.ppermute(row_a, lat, [(i, i ^ 1) for i in range(lats)])
    got_b = lax.ppermute(
        row_b, lat, [(i, j) for k in range(1, lats - 1, 2) for i, j in ((k, k + 1), (k + 1, k))]
    )
    col_shape = jax.ShapeDtypeStruct((rows + 2, width_exp), BF16)
    col_a, col_b = pl.pallas_call(
        pack_columns,
        name="pack_columns",
        out_shape=(col_shape, col_shape),
        in_specs=[SM, VM, VM, VM],
        out_specs=(VM, VM),
        scratch_shapes=[pltpu.VMEM((rows + 2, width_exp), F32)] * 2,
    )(flags, expanded, got_a, got_b)
    seen_b = lax.ppermute(
        col_b, lon, [(i, (i + 1) % lons if i % 2 else (i - 1) % lons) for i in range(lons)]
    )
    seen_a = lax.ppermute(col_a, lon, [(i, i ^ 1) for i in range(lons)])

    order = send_order(rows, cols)
    perm = np.zeros((tokens, tokens), np.float32)
    perm[np.arange(tokens), order] = 1.0
    perm_send = jnp.asarray(perm, BF16)
    perm_back = jnp.asarray(perm.T, BF16)
    taps = jnp.concatenate([dw_kernel.reshape(9, width_exp), land_shift[None]], axis=0)
    land_lanes = jnp.broadcast_to(land.astype(F32)[:, :, None], (rows, cols, 128))
    chunk = 256
    steps = width_exp // chunk
    mixed, sent = pl.pallas_call(
        functools.partial(mix_kernel, chunk=chunk),
        name="mix",
        out_shape=(
            jax.ShapeDtypeStruct((tokens, width), BF16),
            jax.ShapeDtypeStruct((tokens // 4, 4, width), BF16),
        ),
        in_specs=[SM] + [VM] * 7 + [HBM] + [VM] * 2,
        out_specs=(VM, VM),
        scratch_shapes=[
            pltpu.VMEM((width_exp, width), BF16),
            pltpu.VMEM((tokens, width_exp), BF16),
            pltpu.VMEM((tokens, width), F32),
            pltpu.SemaphoreType.DMA((steps,)),
        ],
        compiler_params=pltpu.CompilerParams(vmem_limit_bytes=24 << 20),
    )(
        flags, expanded, got_a, got_b, seen_a, seen_b, land_lanes, taps, w_proj,
        stream.reshape(tokens, width), perm_send,
    )
    choose, block = bias_choice()
    strips = rows // 2
    strip = lax.axis_index("nhi") * strips // lax.axis_size("nhi")
    capped = lax.dynamic_index_in_dim(polar.reshape(GRID, strips), strip, 1, keepdims=False)
    bias = jnp.einsum(
        "hs,srq->hrq", rel_bias.reshape(heads, -1), choose, precision=lax.Precision.HIGHEST
    )
    hidden = jnp.where(jnp.repeat(capped, 2)[:, None] == 1, np.float32(NEG), block)
    bias = bias + hidden[None]

    group = ("nhi", lat)
    mine = lax.all_to_all(sent, group, 0, 0, tiled=True)
    attended = pl.pallas_call(
        functools.partial(attend_kernel, heads=heads),
        name="attend",
        out_shape=jax.ShapeDtypeStruct((tokens // 4, 4, width), BF16),
        in_specs=[VM] * 3,
        out_specs=VM,
        scratch_shapes=[pltpu.VMEM((tokens, width), F32)] * 2,
        compiler_params=pltpu.CompilerParams(vmem_limit_bytes=24 << 20),
    )(mine, w_qkv, bias)
    back = lax.all_to_all(attended, group, 0, 0, tiled=True)
    result = pl.pallas_call(
        out_kernel,
        name="out",
        out_shape=jax.ShapeDtypeStruct((tokens, width), BF16),
        in_specs=[VM] * 4,
        out_specs=VM,
        scratch_shapes=[pltpu.VMEM((tokens, width), F32)],
    )(back, w_out, mixed, perm_back)
    return result.reshape(rows, cols, width)


def solution(mesh):
    lons, lats = mesh.shape["lon"], mesh.shape["lat"]
    fine = Mesh(mesh.devices.reshape(GRID, lons // GRID, lats), ("nhi", "nlo", "lat"))
    lon = ("nhi", "nlo")
    in_specs = (P("lat", lon, None), P("lat", lon, None), P("lat", lon)) + (P(),) * 7
    return jax.shard_map(
        local, mesh=fine, in_specs=in_specs, out_specs=P("lat", lon, None), check_vma=False
    )
```

profile of v0, /device:TPU:1, one launch (start us, length us, event | category | flops | bytes accessed | tf_op | source)
XLA Modules:
  0.0 73.5 jit_solution(11790164541139972146)
XLA Ops:
  0.0 1.0 %select_bitcast_fusion = (bf16[16,3072]{1,0:T(8,128)(2,1)S(1)}, bf16[16,3072]{1,0:T(8,128)(2,1)S(1)}) fusion(pred[]{:T(512)} %eq.24, bf16[8,16,3072]{2,1,0:T(8,128)(2,1)} %e_ref.3), kind=kLoop, calls=%fused_computation.3 | loop fusion | flops 98304 | bytes 393217 | tf_op jit(solution)/shard_map/jit(_where)/select_n | solution.py:221
  1.1 3.3 %collective-permute-start = (bf16[16,3072]{1,0:T(8,128)(2,1)S(1)}, bf16[16,3072]{1,0:T(8,128)(2,1)S(1)}, u32[]{:S(2)}, u32[]{:S(2)}) collective-permute-start(bf16[16,3072]{1,0:T(8,128)(2,1)S(1)} %get-tuple-element.14), channel_id=1, source_target_pairs={{0,1},{1,0},{2,3},{3,2},{4,5},{5,4},{6,7},{7,6},{8,9},{9,8},{10,11... | collective-permute-start | bytes 294920 | tf_op jit(solution)/shard_map/ppermute | solution.py:222
  4.4 1.9 %collective-permute-start.1 = (bf16[16,3072]{1,0:T(8,128)(2,1)S(1)}, bf16[16,3072]{1,0:T(8,128)(2,1)S(1)}, u32[]{:S(2)}, u32[]{:S(2)}) collective-permute-start(bf16[16,3072]{1,0:T(8,128)(2,1)S(1)} %get-tuple-element.13), channel_id=1, source_target_pairs={{1,2},{2,1},{5,6},{6,5},{9,10},{10,9},{13,14},{14,13},{17,18},{18,... | collective-permute-start | bytes 294920 | tf_op jit(solution)/shard_map/ppermute | solution.py:223
  6.3 1.0 %reshape.32 = f32[9,3072]{1,0:T(8,128)S(1)} reshape(f32[3,3,3072]{2,1,0:T(4,128)} %param.19) | data formatting | bytes 221184 | tf_op jit(solution)/shard_map/reshape | solution.py:245
  7.3 0.7 reshape.35
  8.1 0.2 fusion.3
  8.2 0.1 broadcast_in_dim.27
  8.3 0.1 eq.28
  8.4 0.7 %pad_maximum_fusion.taps_ref = f32[10,3072]{1,0:T(8,128)S(1)} fusion(f32[1,3072]{1,0:T(1,128)} %bitcast.18, f32[9,3072]{1,0:T(8,128)S(1)} %reshape.32), kind=kLoop, calls=%fused_computation | loop fusion | flops 30720 | bytes 245760 | tf_op jit(solution)/shard_map/concatenate | solution.py:245
  9.2 1.8 %fusion.1 = f32[16,128,24]{1,2,0:T(8,128)S(1)} fusion(f32[120,16,128]{2,0,1:T(8,128)} %constant.65.clone, f32[24,15,8]{0,2,1:T(8,128)S(1)} %copy-done), kind=kOutput, calls=%fused_computation.5 | convolution fusion | flops 70778880 | bytes 1191168 | tf_op jit(solution)/shard_map/hs,srq->hrq/dot_general | solution.py:273
  11.0 0.7 add_convert_fusion.flags
  11.7 0.6 copy-done.4
  12.3 0.6 copy-done.6
  12.9 2.1 %pack_columns.1 = (bf16[10,3072]{1,0:T(8,128)(2,1)}, bf16[10,3072]{1,0:T(8,128)(2,1)}) custom-call(s32[2]{0:T(128)} %add_convert_fusion.flags, bf16[8,16,3072]{2,1,0:T(8,128)(2,1)} %e_ref.3, bf16[16,3072]{1,0:T(8,128)(2,1)} %copy-done.4, bf16[16,3072]{1,0:T(8,128)(2,1)} %copy-done.6), custom_call_target="tpu_custom_call" | custom-call | tf_op jit(solution)/shard_map/pack_columns/pallas_call | solution.py:227
  15.1 1.1 %collective-permute-start.2 = (bf16[10,3072]{1,0:T(8,128)(2,1)}, bf16[10,3072]{1,0:T(8,128)(2,1)S(1)}, u32[]{:S(2)}, u32[]{:S(2)}) collective-permute-start(bf16[10,3072]{1,0:T(8,128)(2,1)} %get-tuple-element.9), channel_id=1, source_target_pairs={{0,4},{4,0},{8,12},{12,8},{16,20},{20,16},{24,28},{28,24},{32,36},... | collective-permute-start | bytes 184328 | tf_op jit(solution)/shard_map/ppermute | solution.py:238
  16.2 9.2 %collective-permute-start.3 = (bf16[10,3072]{1,0:T(8,128)(2,1)}, bf16[10,3072]{1,0:T(8,128)(2,1)S(1)}, u32[]{:S(2)}, u32[]{:S(2)}) collective-permute-start(bf16[10,3072]{1,0:T(8,128)(2,1)} %get-tuple-element.10), channel_id=1, source_target_pairs={{0,252},{4,8},{8,4},{12,16},{16,12},{20,24},{24,20},{28,32},{32,28... | collective-permute-start | bytes 184328 | tf_op jit(solution)/shard_map/ppermute | solution.py:235
  25.4 0.8 %broadcast_select_fusion = f32[16,128]{1,0:T(8,128)S(1)} fusion(f32[16,128]{1,0:T(8,128)} %constant.66.clone, pred[16]{0:T(512)(128)(4,1)S(1)} %eq.28), kind=kLoop, calls=%fused_computation.7 | loop fusion | flops 2048 | bytes 16400 | tf_op jit(solution)/shard_map/jit(_where)/select_n | solution.py:276
  26.1 0.7 convert_element_type.7
  26.8 0.8 %collective-permute-done.3.cb_ref = bf16[10,3072]{1,0:T(8,128)(2,1)S(1)} collective-permute-done((bf16[10,3072]{1,0:T(8,128)(2,1)}, bf16[10,3072]{1,0:T(8,128)(2,1)S(1)}, u32[]{:S(2)}, u32[]{:S(2)}) %collective-permute-start.3) | collective-permute-done | bytes 61472 | tf_op jit(solution)/shard_map/ppermute | solution.py:235
  27.6 0.1 broadcast_in_dim.25.land_ref
  27.7 2.3 %copy-done.1 = bf16[3072,768]{1,0:T(8,128)(2,1)S(1)} copy-done((bf16[3072,768]{1,0:T(8,128)(2,1)S(1)}, bf16[3072,768]{1,0:T(8,128)(2,1)}, u32[]{:S(2)}) %copy-start.1) | copy-done | bytes 4718616
  30.0 0.9 %copy-done.5 = bf16[16,3072]{1,0:T(8,128)(2,1)S(1)} copy-done((bf16[16,3072]{1,0:T(8,128)(2,1)S(1)}, bf16[16,3072]{1,0:T(8,128)(2,1)}, u32[]{:S(2)}) %copy-start.5) | copy-done | bytes 98328
  30.9 0.9 %copy-done.7 = bf16[16,3072]{1,0:T(8,128)(2,1)S(1)} copy-done((bf16[16,3072]{1,0:T(8,128)(2,1)S(1)}, bf16[16,3072]{1,0:T(8,128)(2,1)}, u32[]{:S(2)}) %copy-start.7) | copy-done | bytes 98328
  31.8 0.7 copy-done.11
  32.5 8.6 %mix.1 = (bf16[128,768]{1,0:T(8,128)(2,1)S(1)}, bf16[32,4,768]{2,1,0:T(4,128)(2,1)}) custom-call(s32[2]{0:T(128)S(1)} %copy-done.11, bf16[8,16,3072]{2,1,0:T(8,128)(2,1)S(1)} %copy-done.2, bf16[16,3072]{1,0:T(8,128)(2,1)S(1)} %copy-done.5, bf16[16,3072]{1,0:T(8,128)(2,1)S(1)} %copy-done.7, bf16[10,3072]{1,0:T(8,128)(2,1)S(1)} %collective-permute-done.2.ca_ref, ...), custom_call_target="tpu_custom_call" | custom-call | tf_op jit(solution)/shard_map/mix/pallas_call | solution.py:249
  41.1 0.7 copy-done.9
  41.8 3.7 %all-to-all-start = ((bf16[32,4,768]{2,1,0:T(4,128)(2,1)}), bf16[32,4,768]{2,1,0:T(4,128)(2,1)S(1)}, u32[]{:S(2)}, u32[]{:S(2)}) async-start(bf16[32,4,768]{2,1,0:T(4,128)(2,1)} %get-tuple-element.11), calls=%async_computation | async-start | bytes 393216 | tf_op jit(solution)/shard_map/all_to_all | solution.py:280
  45.5 7.9 %all-to-all-done.x_ref = bf16[32,4,768]{2,1,0:T(4,128)(2,1)S(1)} async-done(((bf16[32,4,768]{2,1,0:T(4,128)(2,1)}), bf16[32,4,768]{2,1,0:T(4,128)(2,1)S(1)}, u32[]{:S(2)}, u32[]{:S(2)}) %all-to-all-start) | async-done | bytes 196640 | tf_op jit(solution)/shard_map/all_to_all | solution.py:280
  53.4 2.0 %copy-done.3 = bf16[768,2304]{1,0:T(8,128)(2,1)S(1)} copy-done((bf16[768,2304]{1,0:T(8,128)(2,1)S(1)}, bf16[768,2304]{1,0:T(8,128)(2,1)}, u32[]{:S(2)}) %copy-start.3) | copy-done | bytes 3538968
  55.4 3.0 %attend.1 = bf16[32,4,768]{2,1,0:T(4,128)(2,1)S(1)} custom-call(bf16[32,4,768]{2,1,0:T(4,128)(2,1)S(1)} %all-to-all-done.x_ref, bf16[768,2304]{1,0:T(8,128)(2,1)S(1)} %copy-done.3, f32[24,16,128]{2,1,0:T(8,128)S(1)} %fusion.bias_ref), custom_call_target="tpu_custom_call" | custom-call | tf_op jit(solution)/shard_map/attend/pallas_call | solution.py:281
  58.5 12.5 %all_to_all.10.a_ref = bf16[32,4,768]{2,1,0:T(4,128)(2,1)} all-to-all(bf16[32,4,768]{2,1,0:T(4,128)(2,1)S(1)} %attend.1), channel_id=1, replica_groups=mesh['nhi'=8,'nlo'=8,'lat'=4] {'nhi','lat'}, dimensions={0} | all-to-all | bytes 393216 | tf_op jit(solution)/shard_map/all_to_all | solution.py:290
  71.0 2.5 %out.1 = bf16[128,768]{1,0:T(8,128)(2,1)} custom-call(bf16[32,4,768]{2,1,0:T(4,128)(2,1)} %all_to_all.10.a_ref, bf16[768,768]{1,0:T(8,128)(2,1)} %w_ref.3, bf16[128,768]{1,0:T(8,128)(2,1)} %copy-done.9, bf16[128,128]{1,0:T(8,128)(2,1)} %constant.64.clone.perm_ref), custom_call_target="tpu_custom_call" | custom-call | tf_op jit(solution)/shard_map/out/pallas_call | solution.py:291
  (20 shorter events, 0.1 us)
Async XLA Ops:
  0.0 9.2 %copy-start = (f32[24,15,8]{0,2,1:T(8,128)S(1)}, f32[24,15,8]{0,2,1:T(8,128)}, u32[]{:S(2)}) copy-start(f32[24,15,8]{0,2,1:T(8,128)} %param.23) | copy-start | bytes 34564
  0.0 27.7 %copy-start.10 = (bf16[128,128]{1,0:T(8,128)(2,1)S(1)}, bf16[128,128]{1,0:T(8,128)(2,1)}, u32[]{:S(2)}) copy-start(bf16[128,128]{1,0:T(8,128)(2,1)} %constant.63.clone.perm_ref) | copy-start | bytes 98308
  0.0 27.7 %copy-start.2 = (bf16[8,16,3072]{2,1,0:T(8,128)(2,1)S(1)}, bf16[8,16,3072]{2,1,0:T(8,128)(2,1)}, u32[]{:S(2)}) copy-start(bf16[8,16,3072]{2,1,0:T(8,128)(2,1)} %e_ref.3) | copy-start | bytes 2359300
  0.0 27.7 %copy-start.8 = (bf16[8,16,768]{2,1,0:T(8,128)(2,1)S(1)}, bf16[8,16,768]{2,1,0:T(8,128)(2,1)}, u32[]{:S(2)}) copy-start(bf16[8,16,768]{2,1,0:T(8,128)(2,1)} %param.15) | copy-start | bytes 589828
  1.1 10.6 %collective-permute-start = (bf16[16,3072]{1,0:T(8,128)(2,1)S(1)}, bf16[16,3072]{1,0:T(8,128)(2,1)S(1)}, u32[]{:S(2)}, u32[]{:S(2)}) collective-permute-start(bf16[16,3072]{1,0:T(8,128)(2,1)S(1)} %get-tuple-element.14), channel_id=1, source_target_pairs={{0,1},{1,0},{2,3},{3,2},{4,5},{5,4},{6,7},{7,6},{8,9},{9,8},{10,11... | collective-permute-start | bytes 294920 | tf_op jit(solution)/shard_map/ppermute | solution.py:222
  4.4 7.3 %collective-permute-start.1 = (bf16[16,3072]{1,0:T(8,128)(2,1)S(1)}, bf16[16,3072]{1,0:T(8,128)(2,1)S(1)}, u32[]{:S(2)}, u32[]{:S(2)}) collective-permute-start(bf16[16,3072]{1,0:T(8,128)(2,1)S(1)} %get-tuple-element.13), channel_id=1, source_target_pairs={{1,2},{2,1},{5,6},{6,5},{9,10},{10,9},{13,14},{14,13},{17,18},{18,... | collective-permute-start | bytes 294920 | tf_op jit(solution)/shard_map/ppermute | solution.py:223
  11.7 0.6 copy-start.4
  12.3 0.6 copy-start.6
  15.1 11.8 %collective-permute-start.2 = (bf16[10,3072]{1,0:T(8,128)(2,1)}, bf16[10,3072]{1,0:T(8,128)(2,1)S(1)}, u32[]{:S(2)}, u32[]{:S(2)}) collective-permute-start(bf16[10,3072]{1,0:T(8,128)(2,1)} %get-tuple-element.9), channel_id=1, source_target_pairs={{0,4},{4,0},{8,12},{12,8},{16,20},{20,16},{24,28},{28,24},{32,36},... | collective-permute-start | bytes 184328 | tf_op jit(solution)/shard_map/ppermute | solution.py:238
  16.2 11.4 %collective-permute-start.3 = (bf16[10,3072]{1,0:T(8,128)(2,1)}, bf16[10,3072]{1,0:T(8,128)(2,1)S(1)}, u32[]{:S(2)}, u32[]{:S(2)}) collective-permute-start(bf16[10,3072]{1,0:T(8,128)(2,1)} %get-tuple-element.10), channel_id=1, source_target_pairs={{0,252},{4,8},{8,4},{12,16},{16,12},{20,24},{24,20},{28,32},{32,28... | collective-permute-start | bytes 184328 | tf_op jit(solution)/shard_map/ppermute | solution.py:235
  27.7 2.3 %copy-start.1 = (bf16[3072,768]{1,0:T(8,128)(2,1)S(1)}, bf16[3072,768]{1,0:T(8,128)(2,1)}, u32[]{:S(2)}) copy-start(bf16[3072,768]{1,0:T(8,128)(2,1)} %w_hbm.1) | copy-start | bytes 14155780
  30.0 0.9 %copy-start.5 = (bf16[16,3072]{1,0:T(8,128)(2,1)S(1)}, bf16[16,3072]{1,0:T(8,128)(2,1)}, u32[]{:S(2)}) copy-start(bf16[16,3072]{1,0:T(8,128)(2,1)} %copy-done.4) | copy-start | bytes 294916
  30.9 0.9 %copy-start.7 = (bf16[16,3072]{1,0:T(8,128)(2,1)S(1)}, bf16[16,3072]{1,0:T(8,128)(2,1)}, u32[]{:S(2)}) copy-start(bf16[16,3072]{1,0:T(8,128)(2,1)} %copy-done.6) | copy-start | bytes 294916
  31.8 0.7 copy-start.11
  41.1 0.7 copy-start.9
  41.8 11.6 %all-to-all-start = ((bf16[32,4,768]{2,1,0:T(4,128)(2,1)}), bf16[32,4,768]{2,1,0:T(4,128)(2,1)S(1)}, u32[]{:S(2)}, u32[]{:S(2)}) async-start(bf16[32,4,768]{2,1,0:T(4,128)(2,1)} %get-tuple-element.11), calls=%async_computation | async-start | bytes 393216 | tf_op jit(solution)/shard_map/all_to_all | solution.py:280
  53.4 2.0 %copy-start.3 = (bf16[768,2304]{1,0:T(8,128)(2,1)S(1)}, bf16[768,2304]{1,0:T(8,128)(2,1)}, u32[]{:S(2)}) copy-start(bf16[768,2304]{1,0:T(8,128)(2,1)} %w_ref.2) | copy-start | bytes 10616836
where the time goes:
time: 74.9 us; the launch traced here: 73.5 us
  starting transfers between devices  19.2 us (26%)
  Pallas kernels  16.3 us (22%)
  blocking collectives  12.5 us (17%)
  local copies, waits for them, and re-layouts  10.7 us (14%)
  waiting for transfers between devices  8.69 us (12%)
  other arithmetic  4.13 us (6%)
  matrix products  1.83 us (2%)
    all_to_all x1, blocking collectives, local(): back = lax.all_to_all(attended, group, 0, 0, tiled=True)  12.5 us
    ppermute x1, starting transfers between devices, local(): lax.ppermute(col_b, lon, [(i, (i + 1) % lons if i % 2 else (i - 1) % lons...  9.2 us
    unnamed x24, local copies, waits for them, and re-layouts  8.75 us
    pallas_call x1, Pallas kernels, local(): pl.pallas_call(functools.partial(mix_kernel, chunk=chunk), name='mix', ou...  8.61 us
    all_to_all x1, waiting for transfers between devices, local(): mine = lax.all_to_all(sent, group, 0, 0, tiled=True)  7.93 us
    all_to_all x1, starting transfers between devices, local(): mine = lax.all_to_all(sent, group, 0, 0, tiled=True)  3.65 us
    ppermute x1, starting transfers between devices, local(): got_a = lax.ppermute(row_a, lat, [(i, i ^ 1) for i in range(lats)])  3.32 us
    pallas_call x1, Pallas kernels, local(): pl.pallas_call(functools.partial(attend_kernel, heads=heads), name='atten...  3.03 us
  transfers between devices with their start and end apart: 5, of which 2 were waited for; matrix products, arithmetic and copies ran while one was open for 9% of the time, Pallas kernels for 0%

commit v1 on v0

v1 whole, which is shorter than its diff:
```python
import functools

import jax
import jax.numpy as jnp
import numpy as np
from jax import lax
from jax.experimental import pallas as pl
from jax.experimental.pallas import tpu as pltpu
from jax.sharding import Mesh
from jax.sharding import PartitionSpec as P

GRID = 8
EPS = 1e-05
NEG = -1e30
F32 = jnp.float32
BF16 = jnp.bfloat16
VM = pl.BlockSpec(memory_space=pltpu.VMEM)
SM = pl.BlockSpec(memory_space=pltpu.SMEM)
HBM = pl.BlockSpec(memory_space=pltpu.HBM)


def in_hbm(x):
    return pltpu.with_memory_space_constraint(x, pltpu.HBM)


def send_matrix(rows, cols, back):
    tokens = rows * cols
    strips, pairs = rows // 2, cols // 2
    to = lax.broadcasted_iota(jnp.int32, (tokens, tokens), 0)
    at = lax.broadcasted_iota(jnp.int32, (tokens, tokens), 1)
    if back:
        to, at = at, to
    s, rest = to // (4 * pairs), to % (4 * pairs)
    c2, m, c1 = rest // 4, rest % 4 // 2, rest % 2
    token = (m * strips + s) * cols + 2 * c2 + c1
    return jnp.where(token == at, 1.0, 0.0).astype(BF16)


def even(axes):
    return lax.rem(lax.axis_index(axes), 2) == 0


def stage_kernel(e_hbm, row_ref, e_ref, ca_ref, cb_ref, first, last, sem, *, lon):
    rows, cols, _ = e_ref.shape
    copies = [
        pltpu.make_async_copy(e_hbm.at[r], e_ref.at[r], sem.at[r]) for r in range(rows)
    ]
    for copy in copies:
        copy.start()
    for r in range(rows):
        copies[r].wait()
        line = e_ref[r].astype(F32)
        first[r : r + 1, :] = line[0:1]
        last[r : r + 1, :] = line[cols - 1 : cols]
    lon_even = even(lon)
    ca_ref[...] = jnp.where(lon_even, last[...], first[...]).astype(BF16)
    cb_ref[...] = jnp.where(lon_even, first[...], last[...]).astype(BF16)


def pack_kernel(ca_ref, cb_ref, ra_ref, rb_ref, oa_ref, ob_ref, *, lat, lon):
    lat_even, lon_even = even(lat), even(lon)
    cols = ra_ref.shape[0]
    ra = ra_ref[...].astype(F32)
    rb = rb_ref[...].astype(F32)
    top = jnp.where(lat_even, rb, ra)
    bottom = jnp.where(lat_even, ra, rb)
    for c_ref, o_ref, is_last in ((ca_ref, oa_ref, lon_even), (cb_ref, ob_ref, ~lon_even)):
        above = jnp.where(is_last, top[cols - 1 : cols], top[0:1])
        below = jnp.where(is_last, bottom[cols - 1 : cols], bottom[0:1])
        o_ref[...] = jnp.concatenate([above, c_ref[...].astype(F32), below], axis=0).astype(BF16)


def gelu(x):
    inner = x * (np.float32(np.sqrt(2 / np.pi)) + np.float32(0.044715 * np.sqrt(2 / np.pi)) * (x * x))
    half = np.float32(0.5) * x
    return half + half * jnp.tanh(inner)


def normalize(flat):
    centred = flat - jnp.mean(flat, axis=1, keepdims=True)
    spread = jnp.mean(centred * centred, axis=1, keepdims=True)
    return centred * lax.rsqrt(spread + EPS)


def fill_bias(polar, rel, out_ref, strips, nhi):
    strip = lax.axis_index(nhi) * strips // lax.axis_size(nhi)
    high = rel.astype(BF16)
    middle = (rel - high.astype(F32)).astype(BF16)
    low = (rel - high.astype(F32) - middle.astype(F32)).astype(BF16)
    offsets = rel.shape[0]
    lane = lax.broadcasted_iota(jnp.int32, (offsets, 128), 1)
    mq = lane // 2 % GRID
    nq = lane // (2 * GRID)
    at = lax.broadcasted_iota(jnp.int32, (offsets, 128), 0)
    gq = lax.broadcasted_iota(jnp.int32, (1, 128), 1) % 2
    for mk in range(GRID):
        wanted = (mk - mq + GRID - 1) * GRID + (GRID - nq) % GRID
        choose = jnp.where(at == wanted, 1.0, 0.0).astype(BF16)
        near = sum(
            lax.dot_general(
                part, choose, (((0,), (0,)), ((), ())), preferred_element_type=F32
            )
            for part in (high, middle, low)
        )
        cap = jnp.where(polar[mk * strips + strip] == 1, np.float32(NEG), np.float32(0.0))
        for gk in range(2):
            out_ref[:, 2 * mk + gk, :] = near + jnp.where(gq == gk, cap, np.float32(NEG))


def mix_kernel(
    e_ref, ra_ref, rb_ref, land_hbm, taps_hbm, shift_hbm, w_hbm, stream_hbm, qkv_hbm, out_hbm,
    rel_hbm, polar_hbm,
    mixed_ref, sent_ref, edge_ref, taps_ref, w_ref, stream_ref, qkv_ref, wout_ref, bias_ref,
    rel_ref, polar_ref, land_ref, shift_ref, act, total, land_lanes, perm_ref, sem, *, chunk, lat,
):
    rows, cols, width_exp = e_ref.shape
    tokens = rows * cols
    steps = width_exp // chunk

    def fetch(i):
        part = pl.ds(i * chunk, chunk)
        return pltpu.make_async_copy(w_hbm.at[part], w_ref.at[part], sem.at[i])

    first = [
        pltpu.make_async_copy(src, dst, sem.at[steps + i])
        for i, (src, dst) in enumerate(
            ((land_hbm, land_ref), (taps_hbm, taps_ref), (shift_hbm, shift_ref))
        )
    ]
    later = [
        pltpu.make_async_copy(src, dst, sem.at[steps + 3 + i])
        for i, (src, dst) in enumerate(
            (
                (stream_hbm, stream_ref), (rel_hbm, rel_ref), (polar_hbm, polar_ref),
                (qkv_hbm, qkv_ref), (out_hbm, wout_ref),
            )
        )
    ]
    for copy in first:
        copy.start()
    for i in range(steps):
        fetch(i).start()
    for copy in later:
        copy.start()
    lat_even = even(lat)
    perm_ref[...] = send_matrix(rows, cols, False)
    sub = lax.broadcasted_iota(jnp.int32, (cols, 128), 0)
    is_first = sub == 0
    is_last = sub == cols - 1
    token = lax.broadcasted_iota(jnp.int32, (tokens, cols), 0)
    at = lax.broadcasted_iota(jnp.int32, (tokens, cols), 1)
    row_of = lax.broadcasted_iota(jnp.int32, (tokens, rows), 0) // cols
    pick_row = (row_of == lax.broadcasted_iota(jnp.int32, (tokens, rows), 1)).astype(F32)
    for copy in first:
        copy.wait()
    by_row = jnp.dot(pick_row, land_ref[...].astype(F32), preferred_element_type=F32)
    mine = jnp.where(lax.rem(token, cols) == at, by_row, 0.0)
    land_lanes[...] = jnp.dot(mine, jnp.ones((cols, 128), F32), preferred_element_type=F32)

    def depthwise(at):
        lanes = pl.ds(at, 128)
        ra = ra_ref[:, lanes].astype(F32)
        rb = rb_ref[:, lanes].astype(F32)
        x = [jnp.where(lat_even, rb, ra)]
        x += [e_ref[r, :, lanes].astype(F32) for r in range(rows)]
        x += [jnp.where(lat_even, ra, rb)]
        tap = [[taps_ref[a, b : b + 1, lanes] for b in range(3)] for a in range(3)]
        shift = shift_ref[:, lanes]
        for r in range(rows):
            y = [tap[0][b] * x[r] + tap[1][b] * x[r + 1] + tap[2][b] * x[r + 2] for b in range(3)]
            y0 = jnp.where(is_first, 0.0, pltpu.roll(y[0], 1, 0))
            y2 = jnp.where(is_last, 0.0, pltpu.roll(y[2], cols - 1, 0))
            filtered = land_lanes[r * cols : (r + 1) * cols] * shift + y[1] + (y0 + y2)
            edge_ref[r : r + 1, lanes] = filtered[0:1]
            edge_ref[rows + r : rows + r + 1, lanes] = filtered[cols - 1 : cols]
            act[r * cols : (r + 1) * cols, lanes] = gelu(filtered).astype(BF16)

    def conv(i):
        for k in range(chunk // 128):
            depthwise(pl.multiple_of(i * chunk + k * 128, 128))

    def project(i):
        at = pl.multiple_of(i * chunk, chunk)
        return jnp.dot(
            act[:, pl.ds(at, chunk)], w_ref[pl.ds(at, chunk), :], preferred_element_type=F32
        )

    total[...] = jnp.zeros_like(total)
    conv(0)

    def step(i, carry):
        fetch(i - 1).wait()
        conv(i)
        total[...] += project(i - 1)
        return carry

    lax.fori_loop(1, steps, step, 0)
    fetch(steps - 1).wait()
    later[0].wait()
    stream = stream_ref[...].reshape(tokens, stream_ref.shape[2]).astype(F32)
    mixed = (stream + (total[...] + project(steps - 1))).astype(BF16)
    mixed_ref[...] = mixed
    normed = normalize(mixed.astype(F32)).astype(BF16)
    sent = jnp.dot(perm_ref[...], normed, preferred_element_type=F32)
    for k in range(tokens // 4):
        sent_ref[k] = sent[4 * k : 4 * k + 4].astype(BF16)
    for copy in later[1:]:
        copy.wait()
    fill_bias(polar_ref, rel_ref[...], bias_ref, rows // 2, "nhi")


def edge_kernel(
    edge_ref, ca_ref, cb_ref, taps_ref, w_ref, stream_ref, sent_ref, inner_ref, mixed_ref, out_ref, act,
    *, lon, chunk,
):
    double, width_exp = edge_ref.shape
    rows = double // 2
    lon_even = even(lon)
    for i in range(width_exp // chunk):
        lanes = slice(i * chunk, (i + 1) * chunk)
        ca = ca_ref[:, lanes].astype(F32)
        cb = cb_ref[:, lanes].astype(F32)
        left = jnp.where(lon_even, cb, ca)
        right = jnp.where(lon_even, ca, cb)
        from_left = sum(taps_ref[a, 0:1, lanes] * left[a : a + rows] for a in range(3))
        from_right = sum(taps_ref[a, 2:3, lanes] * right[a : a + rows] for a in range(3))
        filtered = edge_ref[:, lanes] + jnp.concatenate([from_left, from_right], axis=0)
        act[:, lanes] = gelu(filtered).astype(BF16)
    projected = jnp.dot(act[...], w_ref[...], preferred_element_type=F32)
    cols = stream_ref.shape[1]
    first = jnp.concatenate([stream_ref[r, 0:1].astype(F32) for r in range(rows)], axis=0)
    last = jnp.concatenate([stream_ref[r, cols - 1 : cols].astype(F32) for r in range(rows)], axis=0)
    mixed = (jnp.concatenate([first, last], axis=0) + projected).astype(BF16)
    mixed = mixed.astype(F32)
    normed = normalize(mixed).astype(BF16).astype(F32)
    sub = lax.broadcasted_iota(jnp.int32, (cols, mixed.shape[1]), 0)
    for r in range(rows):
        part = slice(r * cols, (r + 1) * cols)
        inner = inner_ref[part].astype(F32)
        inner = jnp.where(sub == 0, mixed[r : r + 1], inner)
        inner = jnp.where(sub == cols - 1, mixed[rows + r : rows + r + 1], inner)
        mixed_ref[part] = inner.astype(BF16)
    out_ref[...] = sent_ref[...]
    pairs = cols // 2
    strips = rows // 2
    for s in range(strips):
        for side, c2 in ((0, 0), (1, pairs - 1)):
            k = s * pairs + c2
            old = sent_ref[k].astype(F32)
            keep = [old[0:1], old[1:2], old[2:3], old[3:4]]
            for m in range(2):
                at = side * rows + m * strips + s
                keep[2 * m + side] = normed[at : at + 1]
            out_ref[k] = jnp.concatenate(keep, axis=0).astype(BF16)


def attend_kernel(x_ref, w_ref, bias_ref, out_ref, x_buf, o_buf, *, heads):
    tokens = 4 * x_ref.shape[0]
    width = x_ref.shape[2]
    head_dim = width // heads
    for k in range(tokens // 4):
        x_buf[4 * k : 4 * k + 4, :] = x_ref[k].astype(F32)
    x = x_buf[...].astype(BF16)
    scale = np.float32(head_dim**-0.5)
    per = 128 // head_dim
    lane_head = lax.broadcasted_iota(jnp.int32, (tokens, 128), 1) // head_dim
    ones = jnp.ones((16, tokens), BF16)

    def project(col):
        return jnp.dot(x, w_ref[:, col : col + 128], preferred_element_type=F32)

    for p in range(heads // per):
        q = project(128 * p)
        k = project(width + 128 * p).astype(BF16)
        v = project(2 * width + 128 * p)
        v_t = jnp.concatenate([jnp.transpose(v).astype(BF16), ones], axis=0)
        queries = jnp.concatenate(
            [jnp.where(lane_head == j, q, 0.0).astype(BF16) for j in range(per)], axis=0
        )
        scores = lax.dot_general(
            k, queries, (((1,), (1,)), ((), ())), preferred_element_type=F32
        )
        weights = []
        for j in range(per):
            base = bias_ref[p * per + j]
            bias = jnp.concatenate(
                [base if n == 0 else pltpu.roll(base, 16 * n, 1) for n in range(GRID)], axis=0
            )
            s = scores[:, tokens * j : tokens * (j + 1)] * scale + bias
            weights.append(jnp.exp(s - jnp.max(s, axis=0, keepdims=True)).astype(BF16))
        summed = jnp.dot(v_t, jnp.concatenate(weights, axis=1), preferred_element_type=F32)
        parts = []
        for j in range(per):
            block = summed[:, tokens * j : tokens * (j + 1)]
            parts.append(
                block[head_dim * j : head_dim * (j + 1)] * (1.0 / block[128 : 129])
            )
        o_buf[:, 128 * p : 128 * (p + 1)] = jnp.transpose(jnp.concatenate(parts, axis=0))
    for k in range(tokens // 4):
        out_ref[k] = o_buf[4 * k : 4 * k + 4, :].astype(BF16)


def out_kernel(a_ref, w_ref, mixed_ref, out_ref, a_buf, *, rows, cols):
    tokens = rows * cols
    for k in range(tokens // 4):
        a_buf[4 * k : 4 * k + 4, :] = a_ref[k].astype(F32)
    attended = jnp.dot(
        send_matrix(rows, cols, True), a_buf[...].astype(BF16), preferred_element_type=F32
    ).astype(BF16)
    result = mixed_ref[...].astype(F32) + jnp.dot(
        attended, w_ref[...], preferred_element_type=F32
    )
    out_ref[...] = result.astype(BF16)


def local(expanded, stream, land, polar, land_shift, dw_kernel, w_proj, w_qkv, w_out, rel_bias):
    rows, cols, width_exp = expanded.shape
    width = stream.shape[2]
    heads = rel_bias.shape[0]
    tokens = rows * cols
    lon, lat = ("nhi", "nlo"), "lat"
    lons, lats = lax.axis_size(lon), lax.axis_size(lat)
    everyone = lon + (lat,)
    lat_even = lax.axis_index(lat) % 2 == 0
    top_row, bottom_row = expanded[0], expanded[rows - 1]
    row_a = jnp.where(lat_even, bottom_row, top_row)
    row_b = jnp.where(lat_even, top_row, bottom_row)
    got_a = lax.ppermute(row_a, lat, [(i, i ^ 1) for i in range(lats)])
    got_b = lax.ppermute(
        row_b, lat, [(i, j) for k in range(1, lats - 1, 2) for i, j in ((k, k + 1), (k + 1, k))]
    )
    col_shape = jax.ShapeDtypeStruct((rows, width_exp), BF16)
    e_here, own_a, own_b = pl.pallas_call(
        functools.partial(stage_kernel, lon=lon),
        name="stage",
        out_shape=(pltpu.VMEM(expanded.shape, BF16), col_shape, col_shape),
        in_specs=[HBM, VM],
        out_specs=(VM, VM, VM),
        scratch_shapes=[pltpu.VMEM((rows, width_exp), F32)] * 2 + [pltpu.SemaphoreType.DMA((rows,))],
        compiler_params=pltpu.CompilerParams(vmem_limit_bytes=4 << 20),
        cost_estimate=pl.CostEstimate(flops=10**6, bytes_accessed=2 * 10**6, transcendentals=0),
    )(in_hbm(expanded), row_b)
    col_shape = jax.ShapeDtypeStruct((rows + 2, width_exp), BF16)
    col_a, col_b = pl.pallas_call(
        functools.partial(pack_kernel, lat=lat, lon=lon),
        name="pack",
        out_shape=(col_shape, col_shape),
        in_specs=[VM] * 4,
        out_specs=(VM, VM),
        compiler_params=pltpu.CompilerParams(vmem_limit_bytes=4 << 20),
    )(own_a, own_b, got_a, got_b)
    seen_b = lax.ppermute(
        col_b, lon, [(i, (i + 1) % lons if i % 2 else (i - 1) % lons) for i in range(lons)]
    )
    seen_a = lax.ppermute(col_a, lon, [(i, i ^ 1) for i in range(lons)])

    chunk = 256
    token_shape = jax.ShapeDtypeStruct((tokens, width), BF16)
    sent_shape = jax.ShapeDtypeStruct((tokens // 4, 4, width), BF16)
    steps = width_exp // chunk
    rel = jnp.transpose(rel_bias, (1, 2, 0)).reshape(-1, heads)
    mixed, sent, edge, taps, w_proj, stream, w_qkv, w_out, bias = pl.pallas_call(
        functools.partial(mix_kernel, chunk=chunk, lat=lat),
        name="mix",
        out_shape=(
            token_shape, sent_shape, pltpu.VMEM((2 * rows, width_exp), F32),
            pltpu.VMEM(dw_kernel.shape, F32),
            pltpu.VMEM(w_proj.shape, BF16),
            pltpu.VMEM(stream.shape, BF16),
            pltpu.VMEM(w_qkv.shape, BF16),
            pltpu.VMEM(w_out.shape, BF16),
            pltpu.VMEM((heads, 2 * GRID, 128), F32),
        ),
        in_specs=[VM] * 3 + [HBM] * 9,
        out_specs=(VM,) * 9,
        scratch_shapes=[
            pltpu.VMEM(rel.shape, F32),
            pltpu.SMEM(polar.shape, jnp.int32),
            pltpu.VMEM((rows, cols), jnp.int32),
            pltpu.VMEM((1, width_exp), F32),
            pltpu.VMEM((tokens, width_exp), BF16),
            pltpu.VMEM((tokens, width), F32),
            pltpu.VMEM((tokens, 128), F32),
            pltpu.VMEM((tokens, tokens), BF16),
            pltpu.SemaphoreType.DMA((steps + 8,)),
        ],
        compiler_params=pltpu.CompilerParams(vmem_limit_bytes=20 << 20),
        cost_estimate=pl.CostEstimate(flops=10**9, bytes_accessed=10**6, transcendentals=0),
    )(
        e_here, got_a, got_b,
        *map(in_hbm, (land, dw_kernel, land_shift[None], w_proj, stream, w_qkv, w_out, rel, polar)),
    )
    mixed, sent = pl.pallas_call(
        functools.partial(edge_kernel, lon=lon, chunk=chunk),
        name="edge",
        out_shape=(token_shape, sent_shape),
        in_specs=[VM] * 8,
        out_specs=(VM, VM),
        scratch_shapes=[pltpu.VMEM((2 * rows, width_exp), BF16)],
        compiler_params=pltpu.CompilerParams(vmem_limit_bytes=8 << 20),
    )(edge, seen_a, seen_b, taps, w_proj, stream, sent, mixed)
    group = ("nhi", lat)
    mine = lax.all_to_all(sent, group, 0, 0, tiled=True)
    attended = pl.pallas_call(
        functools.partial(attend_kernel, heads=heads),
        name="attend",
        out_shape=jax.ShapeDtypeStruct((tokens // 4, 4, width), BF16),
        in_specs=[VM] * 3,
        out_specs=VM,
        scratch_shapes=[pltpu.VMEM((tokens, width), F32)] * 2,
        compiler_params=pltpu.CompilerParams(vmem_limit_bytes=8 << 20),
    )(mine, w_qkv, bias)
    back = lax.all_to_all(attended, group, 0, 0, tiled=True)
    result = pl.pallas_call(
        functools.partial(out_kernel, rows=rows, cols=cols),
        name="out",
        out_shape=jax.ShapeDtypeStruct((tokens, width), BF16),
        in_specs=[VM] * 3,
        out_specs=VM,
        scratch_shapes=[pltpu.VMEM((tokens, width), F32)],
        compiler_params=pltpu.CompilerParams(vmem_limit_bytes=8 << 20),
    )(back, w_out, mixed)
    return result.reshape(rows, cols, width)


def solution(mesh):
    lons, lats = mesh.shape["lon"], mesh.shape["lat"]
    fine = Mesh(mesh.devices.reshape(GRID, lons // GRID, lats), ("nhi", "nlo", "lat"))
    lon = ("nhi", "nlo")
    in_specs = (P("lat", lon, None), P("lat", lon, None), P("lat", lon)) + (P(),) * 7
    return jax.shard_map(
        local, mesh=fine, in_specs=in_specs, out_specs=P("lat", lon, None), check_vma=False
    )
```

time: 74.9 us -> 55 us (0.73); the launches traced: 73.5 us -> 54.7 us
  local copies, waits for them, and re-layouts: 10.7 us -> 0 us
  blocking collectives: 12.5 us -> 22.8 us
  waiting for transfers between devices: 8.69 us -> 2.97 us
  starting transfers between devices: 19.2 us -> 14.7 us
  other arithmetic: 4.13 us -> 0.96 us
  Pallas kernels: 16.3 us -> 13.2 us
  matrix products: 1.83 us -> 0 us
    all_to_all x0 -> x1, blocking collectives: none -> 10.7 us  [local(): mine = lax.all_to_all(sent, group, 0, 0, tiled=True)]
    unnamed x24 -> x0, local copies, waits for them, and re-layouts: 8.75 us -> none
    all_to_all x1 -> x0, waiting for transfers between devices: 7.93 us -> none  [local(): mine = lax.all_to_all(sent, group, 0, 0, tiled=True)]
    all_to_all x1 -> x0, starting transfers between devices: 3.65 us -> none  [local(): mine = lax.all_to_all(sent, group, 0, 0, tiled=True)]
    pallas_call x3 -> x5, Pallas kernels: 13.2 us -> 10.2 us  [the longest x1 6.52 us: local(): pl.pallas_call(functools.partial(mix_kernel, chunk=chunk, lat=lat), name=...]
    ppermute x1, waiting for transfers between devices: 0.01 us -> 2.96 us  [local(): lax.ppermute(row_b, lat, [(i, j) for k in range(1, lats - 1, 2) for i, j...]
    dot_general x1 -> x0, matrix products: 1.83 us -> none  [local(): jnp.einsum('hs,srq->hrq', rel_bias.reshape(heads, -1), choose, precision=...]
    reshape x2 -> x0, local copies, waits for them, and re-layouts: 1.7 us -> none  [the longest x1 0.97 us: local(): dw_kernel.reshape(9, width_exp)]
  transfers between devices with their start and end apart: 5 -> 4, of which waited for: 2 -> 1; matrix products, arithmetic and copies ran while one was open for 9% -> 0% of each run, Pallas kernels for 0% -> 14%
where the time goes in v1:
time: 55 us; the launch traced here: 54.7 us
  blocking collectives  22.8 us (41%)
  starting transfers between devices  14.7 us (27%)
  Pallas kernels  13.2 us (24%)
  waiting for transfers between devices  2.97 us (5%)
  other arithmetic  0.96 us (2%)
    all_to_all x1, blocking collectives, local(): back = lax.all_to_all(attended, group, 0, 0, tiled=True)  12.2 us
    all_to_all x1, blocking collectives, local(): mine = lax.all_to_all(sent, group, 0, 0, tiled=True)  10.7 us
    ppermute x1, starting transfers between devices, local(): lax.ppermute(col_b, lon, [(i, (i + 1) % lons if i % 2 else (i - 1) % lons...  9.38 us
    pallas_call x1, Pallas kernels, local(): pl.pallas_call(functools.partial(mix_kernel, chunk=chunk, lat=lat), name=...  6.52 us
    ppermute x1, starting transfers between devices, local(): got_a = lax.ppermute(row_a, lat, [(i, i ^ 1) for i in range(lats)])  3.33 us
    pallas_call x1, Pallas kernels, local(): pl.pallas_call(functools.partial(attend_kernel, heads=heads), name='atten...  3.03 us
    ppermute x1, waiting for transfers between devices, local(): lax.ppermute(row_b, lat, [(i, j) for k in range(1, lats - 1, 2) for i, j...  2.96 us
    ppermute x1, starting transfers between devices, local(): lax.ppermute(row_b, lat, [(i, j) for k in range(1, lats - 1, 2) for i, j...  1.91 us
  transfers between devices with their start and end apart: 4, of which 1 were waited for; matrix products, arithmetic and copies ran while one was open for 0% of the time, Pallas kernels for 14%

profile of v1, /device:TPU:1, one launch (start us, length us, event | category | flops | bytes accessed | tf_op | source)
XLA Modules:
  0.0 54.7 jit_solution(4378180750440763790)
XLA Ops:
  0.0 1.0 %select_bitcast_fusion = (bf16[16,3072]{1,0:T(8,128)(2,1)S(1)}, bf16[16,3072]{1,0:T(8,128)(2,1)S(1)}) fusion(pred[]{:T(512)S(6)} %eq.5, bf16[8,16,3072]{2,1,0:T(8,128)(2,1)} %e_hbm.1), kind=kLoop, calls=%fused_computation | loop fusion | flops 98304 | bytes 393217 | tf_op jit(solution)/shard_map/jit(_where)/select_n | solution.py:326
  1.0 3.3 %collective-permute-start = (bf16[16,3072]{1,0:T(8,128)(2,1)S(1)}, bf16[16,3072]{1,0:T(8,128)(2,1)S(1)}, u32[]{:S(2)}, u32[]{:S(2)}) collective-permute-start(bf16[16,3072]{1,0:T(8,128)(2,1)S(1)} %get-tuple-element.37), channel_id=1, source_target_pairs={{0,1},{1,0},{2,3},{3,2},{4,5},{5,4},{6,7},{7,6},{8,9},{9,8},{10,11... | collective-permute-start | bytes 294920 | tf_op jit(solution)/shard_map/ppermute | solution.py:328
  4.3 1.9 %collective-permute-start.1 = (bf16[16,3072]{1,0:T(8,128)(2,1)S(1)}, bf16[16,3072]{1,0:T(8,128)(2,1)S(1)}, u32[]{:S(2)}, u32[]{:S(2)}) collective-permute-start(bf16[16,3072]{1,0:T(8,128)(2,1)S(1)} %get-tuple-element.38.row_ref), channel_id=1, source_target_pairs={{1,2},{2,1},{5,6},{6,5},{9,10},{10,9},{13,14},{14,13},{17,18},{18,... | collective-permute-start | bytes 294920 | tf_op jit(solution)/shard_map/ppermute | solution.py:329
  6.2 1.3 %stage.1 = (bf16[8,16,3072]{2,1,0:T(8,128)(2,1)S(1)}, bf16[8,3072]{1,0:T(8,128)(2,1)S(1)}, bf16[8,3072]{1,0:T(8,128)(2,1)S(1)}) custom-call(bf16[8,16,3072]{2,1,0:T(8,128)(2,1)} %e_hbm.1, bf16[16,3072]{1,0:T(8,128)(2,1)S(1)} %get-tuple-element.38.row_ref), custom_call_target="tpu_custom_call" | custom-call | flops 1000000 | bytes 2000000 | tf_op jit(solution)/shard_map/stage/pallas_call | solution.py:333
  7.5 0.0 collective-permute-done.ra_ref
  7.5 3.0 %collective-permute-done.1.rb_ref = bf16[16,3072]{1,0:T(8,128)(2,1)S(1)} collective-permute-done((bf16[16,3072]{1,0:T(8,128)(2,1)S(1)}, bf16[16,3072]{1,0:T(8,128)(2,1)S(1)}, u32[]{:S(2)}, u32[]{:S(2)}) %collective-permute-start.1) | collective-permute-done | bytes 98336 | tf_op jit(solution)/shard_map/ppermute | solution.py:329
  10.5 0.1 pack.1
  10.6 0.1 collective-permute-start.2
  10.7 9.4 %collective-permute-start.3 = (bf16[10,3072]{1,0:T(8,128)(2,1)S(1)}, bf16[10,3072]{1,0:T(8,128)(2,1)S(1)}, u32[]{:S(2)}, u32[]{:S(2)}) collective-permute-start(bf16[10,3072]{1,0:T(8,128)(2,1)S(1)} %get-tuple-element.26), channel_id=1, source_target_pairs={{0,252},{4,8},{8,4},{12,16},{16,12},{20,24},{24,20},{28,32},{32,28... | collective-permute-start | bytes 184328 | tf_op jit(solution)/shard_map/ppermute | solution.py:352
  20.1 6.5 %mix.1 = (bf16[128,768]{1,0:T(8,128)(2,1)S(1)}, bf16[32,4,768]{2,1,0:T(4,128)(2,1)S(1)}, f32[16,3072]{1,0:T(8,128)S(1)}, f32[3,3,3072]{2,1,0:T(4,128)S(1)}, bf16...) custom-call(bf16[8,16,3072]{2,1,0:T(8,128)(2,1)S(1)} %get-tuple-elem, ...), custom_call_target="tpu_custom_call" | custom-call | flops 1000000000 | bytes 1000000 | tf_op jit(solution)/shard_map/mix/pallas_call | solution.py:362
  26.6 0.0 collective-permute-done.2.ca_ref
  26.6 0.0 collective-permute-done.3.cb_ref
  26.7 1.0 %edge.1 = (bf16[128,768]{1,0:T(8,128)(2,1)S(1)}, bf16[32,4,768]{2,1,0:T(4,128)(2,1)S(1)}) custom-call(f32[16,3072]{1,0:T(8,128)S(1)} %get-tuple-element.22.edge_ref, bf16[10,3072]{1,0:T(8,128)(2,1)S(1)} %collective-permute-done.2.ca_ref, bf16[10,3072]{1,0:T(8,128)(2,1)S(1)} %collective-permute-done.3.cb_ref, f32[3,3,3072]{2,1,0:T(4,128)S(1)} %get-tuple-element.27.taps_ref, ...), custom_call_target="tpu_custom_call" | custom-call | tf_op jit(solution)/shard_map/edge/pallas_call | solution.py:393
  27.7 10.7 %all_to_all.10.x_ref = bf16[32,4,768]{2,1,0:T(4,128)(2,1)S(1)} all-to-all(bf16[32,4,768]{2,1,0:T(4,128)(2,1)S(1)} %get-tuple-element.32), channel_id=1, replica_groups=mesh['nhi'=8,'nlo'=8,'lat'=4] {'nhi','lat'}, dimensions={0} | all-to-all | bytes 393216 | tf_op jit(solution)/shard_map/all_to_all | solution.py:403
  38.3 3.0 %attend.1 = bf16[32,4,768]{2,1,0:T(4,128)(2,1)S(1)} custom-call(bf16[32,4,768]{2,1,0:T(4,128)(2,1)S(1)} %all_to_all.10.x_ref, bf16[768,2304]{1,0:T(8,128)(2,1)S(1)} %get-tuple-element.33.w_ref, f32[24,16,128]{2,1,0:T(8,128)S(1)} %get-tuple-element.34.bias_ref), custom_call_target="tpu_custom_call" | custom-call | tf_op jit(solution)/shard_map/attend/pallas_call | solution.py:404
  41.4 12.2 %all_to_all.11.a_ref = bf16[32,4,768]{2,1,0:T(4,128)(2,1)S(1)} all-to-all(bf16[32,4,768]{2,1,0:T(4,128)(2,1)S(1)} %attend.1), channel_id=1, replica_groups=mesh['nhi'=8,'nlo'=8,'lat'=4] {'nhi','lat'}, dimensions={0} | all-to-all | bytes 393216 | tf_op jit(solution)/shard_map/all_to_all | solution.py:413
  53.5 1.2 %out.1 = bf16[128,768]{1,0:T(8,128)(2,1)} custom-call(bf16[32,4,768]{2,1,0:T(4,128)(2,1)S(1)} %all_to_all.11.a_ref, bf16[768,768]{1,0:T(8,128)(2,1)S(1)} %get-tuple-element.35.w_ref, bf16[128,768]{1,0:T(8,128)(2,1)S(1)} %get-tuple-element.36.mixed_ref), custom_call_target="tpu_custom_call" | custom-call | tf_op jit(solution)/shard_map/out/pallas_call | solution.py:414
Async XLA Ops:
  1.0 6.6 %collective-permute-start = (bf16[16,3072]{1,0:T(8,128)(2,1)S(1)}, bf16[16,3072]{1,0:T(8,128)(2,1)S(1)}, u32[]{:S(2)}, u32[]{:S(2)}) collective-permute-start(bf16[16,3072]{1,0:T(8,128)(2,1)S(1)} %get-tuple-element.37), channel_id=1, source_target_pairs={{0,1},{1,0},{2,3},{3,2},{4,5},{5,4},{6,7},{7,6},{8,9},{9,8},{10,11... | collective-permute-start | bytes 294920 | tf_op jit(solution)/shard_map/ppermute | solution.py:328
  4.3 6.2 %collective-permute-start.1 = (bf16[16,3072]{1,0:T(8,128)(2,1)S(1)}, bf16[16,3072]{1,0:T(8,128)(2,1)S(1)}, u32[]{:S(2)}, u32[]{:S(2)}) collective-permute-start(bf16[16,3072]{1,0:T(8,128)(2,1)S(1)} %get-tuple-element.38.row_ref), channel_id=1, source_target_pairs={{1,2},{2,1},{5,6},{6,5},{9,10},{10,9},{13,14},{14,13},{17,18},{18,... | collective-permute-start | bytes 294920 | tf_op jit(solution)/shard_map/ppermute | solution.py:329
  10.6 16.0 %collective-permute-start.2 = (bf16[10,3072]{1,0:T(8,128)(2,1)S(1)}, bf16[10,3072]{1,0:T(8,128)(2,1)S(1)}, u32[]{:S(2)}, u32[]{:S(2)}) collective-permute-start(bf16[10,3072]{1,0:T(8,128)(2,1)S(1)} %get-tuple-element.25), channel_id=1, source_target_pairs={{0,4},{4,0},{8,12},{12,8},{16,20},{20,16},{24,28},{28,24},{32,36},... | collective-permute-start | bytes 184328 | tf_op jit(solution)/shard_map/ppermute | solution.py:355
  10.7 15.9 %collective-permute-start.3 = (bf16[10,3072]{1,0:T(8,128)(2,1)S(1)}, bf16[10,3072]{1,0:T(8,128)(2,1)S(1)}, u32[]{:S(2)}, u32[]{:S(2)}) collective-permute-start(bf16[10,3072]{1,0:T(8,128)(2,1)S(1)} %get-tuple-element.26), channel_id=1, source_target_pairs={{0,252},{4,8},{8,4},{12,16},{16,12},{20,24},{24,20},{28,32},{32,28... | collective-permute-start | bytes 184328 | tf_op jit(solution)/shard_map/ppermute | solution.py:352

commit v2 on v1

v2 whole, which is shorter than its diff:
```python
import functools

import jax
import jax.numpy as jnp
import numpy as np
from jax import lax
from jax.experimental import pallas as pl
from jax.experimental.pallas import tpu as pltpu
from jax.sharding import Mesh
from jax.sharding import PartitionSpec as P

GRID = 8
EPS = 1e-05
NEG = -1e30
LOG2E = np.float32(np.log2(np.e))
F32 = jnp.float32
BF16 = jnp.bfloat16
VM = pl.BlockSpec(memory_space=pltpu.VMEM)
SM = pl.BlockSpec(memory_space=pltpu.SMEM)
HBM = pl.BlockSpec(memory_space=pltpu.HBM)


def in_hbm(x):
    return pltpu.with_memory_space_constraint(x, pltpu.HBM)


def send_matrix(rows, cols, back):
    tokens = rows * cols
    strips, pairs = rows // 2, cols // 2
    to = lax.broadcasted_iota(jnp.int32, (tokens, tokens), 0)
    at = lax.broadcasted_iota(jnp.int32, (tokens, tokens), 1)
    if back:
        to, at = at, to
    s, rest = to // (4 * pairs), to % (4 * pairs)
    c2, m, c1 = rest // 4, rest % 4 // 2, rest % 2
    token = (m * strips + s) * cols + 2 * c2 + c1
    return jnp.where(token == at, 1.0, 0.0).astype(BF16)


def even(axes):
    return lax.rem(lax.axis_index(axes), 2) == 0


def pick_kernel(*refs, lat, lon):
    ins, outs, refs = refs[:5], refs[5:10], refs[10:]
    xa_ref, xb_ref, ra_ref, rb_ref, ca_ref, cb_ref, first, last, sem = refs
    e_hbm, e_ref = ins[0], outs[0]
    rows, cols, _ = e_ref.shape
    lines = [pltpu.make_async_copy(e_hbm.at[r], e_ref.at[r], sem.at[r]) for r in range(rows)]
    rest = [
        pltpu.make_async_copy(src, dst, sem.at[rows + i])
        for i, (src, dst) in enumerate(zip(ins[1:], outs[1:]))
    ]
    for copy in lines + rest:
        copy.start()
    for r in range(rows):
        lines[r].wait()
        line = e_ref[r].astype(F32)
        first[r : r + 1, :] = line[0:1]
        last[r : r + 1, :] = line[cols - 1 : cols]
    lat_even, lon_even = even(lat), even(lon)
    top = e_ref[0].astype(F32)
    bottom = e_ref[rows - 1].astype(F32)
    ra_ref[...] = jnp.where(lat_even, bottom, top).astype(BF16)
    rb_ref[...] = jnp.where(lat_even, top, bottom).astype(BF16)
    a, b = first[...], last[...]
    ca_ref[...] = jnp.where(lon_even, b, a).astype(BF16)
    cb_ref[...] = jnp.where(lon_even, a, b).astype(BF16)
    above = jnp.concatenate([a[0:1], b[0:1]], axis=0)
    below = jnp.concatenate([a[rows - 1 : rows], b[rows - 1 : rows]], axis=0)
    xa_ref[...] = jnp.where(lat_even, below, above).astype(BF16)
    xb_ref[...] = jnp.where(lat_even, above, below).astype(BF16)
    for copy in rest:
        copy.wait()


def pack_kernel(ca_ref, cb_ref, xa_ref, xb_ref, oa_ref, ob_ref, *, lat, lon):
    lat_even, lon_even = even(lat), even(lon)
    rows, width_exp = ca_ref.shape
    half = rows // 2
    part = width_exp // half
    xa, xb = xa_ref[...].astype(F32), xb_ref[...].astype(F32)
    ends = jnp.where(lat_even, xb, xa), jnp.where(lat_even, xa, xb)
    for c_ref, o_ref, is_last in ((ca_ref, oa_ref, lon_even), (cb_ref, ob_ref, ~lon_even)):
        o_ref[:, :width_exp] = c_ref[...]
        cells = [jnp.where(is_last, end[1:2], end[0:1]) for end in ends]
        quarters = [cell[:, part * k : part * (k + 1)] for cell in cells for k in range(half)]
        o_ref[:, width_exp:] = jnp.concatenate(quarters, axis=0).astype(BF16)


def gelu(x):
    inner = x * (np.float32(np.sqrt(2 / np.pi)) + np.float32(0.044715 * np.sqrt(2 / np.pi)) * (x * x))
    half = np.float32(0.5) * x
    return half + half * jnp.tanh(inner)


def normalize(flat):
    centred = flat - jnp.mean(flat, axis=1, keepdims=True)
    spread = jnp.mean(centred * centred, axis=1, keepdims=True)
    return centred * lax.rsqrt(spread + EPS)


def fill_bias(polar, rel, out_ref, strips, nhi):
    strip = lax.axis_index(nhi) * strips // lax.axis_size(nhi)
    high = rel.astype(BF16)
    middle = (rel - high.astype(F32)).astype(BF16)
    low = (rel - high.astype(F32) - middle.astype(F32)).astype(BF16)
    offsets = rel.shape[0]
    lane = lax.broadcasted_iota(jnp.int32, (offsets, 128), 1)
    mq = lane // 2 % GRID
    nq = lane // (2 * GRID)
    at = lax.broadcasted_iota(jnp.int32, (offsets, 128), 0)
    gq = lax.broadcasted_iota(jnp.int32, (1, 128), 1) % 2
    for mk in range(GRID):
        wanted = (mk - mq + GRID - 1) * GRID + (GRID - nq) % GRID
        choose = jnp.where(at == wanted, 1.0, 0.0).astype(BF16)
        near = sum(
            lax.dot_general(
                part, choose, (((0,), (0,)), ((), ())), preferred_element_type=F32
            )
            for part in (high, middle, low)
        )
        cap = jnp.where(polar[mk * strips + strip] == 1, np.float32(NEG), np.float32(0.0))
        for gk in range(2):
            out_ref[:, 2 * mk + gk, :] = near * LOG2E + jnp.where(gq == gk, cap, np.float32(NEG))


def filter_line(x, r, lanes, taps_ref, shift_ref, land_ref, edge_ref, act_ref, rows, cols):
    sub = lax.broadcasted_iota(jnp.int32, (cols, 128), 0)
    tap = [[taps_ref[a, b : b + 1, lanes] for b in range(3)] for a in range(3)]
    y = [tap[0][b] * x[0] + tap[1][b] * x[1] + tap[2][b] * x[2] for b in range(3)]
    y0 = jnp.where(sub == 0, 0.0, pltpu.roll(y[0], 1, 0))
    y2 = jnp.where(sub == cols - 1, 0.0, pltpu.roll(y[2], cols - 1, 0))
    filtered = land_ref[r * cols : (r + 1) * cols] * shift_ref[:, lanes] + y[1] + (y0 + y2)
    edge_ref[r : r + 1, lanes] = filtered[0:1]
    edge_ref[rows + r : rows + r + 1, lanes] = filtered[cols - 1 : cols]
    act_ref[r * cols : (r + 1) * cols, lanes] = gelu(filtered).astype(BF16)


def spread_land(land, cols):
    rows = land.shape[0]
    tokens = rows * cols
    token = lax.broadcasted_iota(jnp.int32, (tokens, cols), 0)
    at = lax.broadcasted_iota(jnp.int32, (tokens, cols), 1)
    row_of = lax.broadcasted_iota(jnp.int32, (tokens, rows), 0) // cols
    pick_row = (row_of == lax.broadcasted_iota(jnp.int32, (tokens, rows), 1)).astype(F32)
    by_row = jnp.dot(pick_row, land.astype(F32), preferred_element_type=F32)
    mine = jnp.where(lax.rem(token, cols) == at, by_row, 0.0)
    return jnp.dot(mine, jnp.ones((cols, 128), F32), preferred_element_type=F32)


def inner_kernel(*refs, aliased, early, chunk):
    ins, refs = refs[:7], refs[7 + aliased :]
    outs, (rel_ref, polar_ref, sem) = refs[:-3], refs[-3:]
    e_ref, taps_ref, shift_ref, land_raw, w_hbm, rel_hbm, polar_hbm = ins
    act_ref, edge_ref, land_ref, w_ref, bias_ref = outs[:5]
    rows, cols, width_exp = e_ref.shape
    here = lax.axis_index("nlo") == 0

    @pl.when(here if early else ~here)
    def _():
        copies = [
            pltpu.make_async_copy(src, dst, sem.at[i])
            for i, (src, dst) in enumerate(
                (
                    (rel_hbm, rel_ref), (polar_hbm, polar_ref), (w_hbm, w_ref),
                )
            )
        ]
        for copy in copies:
            copy.start()
        land_ref[...] = spread_land(land_raw[...], cols)

        def step(i, carry):
            lanes = pl.ds(pl.multiple_of(i * 128, 128), 128)
            x = [e_ref[r, :, lanes].astype(F32) for r in range(rows)]
            for r in range(1, rows - 1):
                filter_line(
                    x[r - 1 : r + 2], r, lanes, taps_ref, shift_ref, land_ref, edge_ref, act_ref,
                    rows, cols,
                )
            return carry

        lax.fori_loop(0, width_exp // 128, step, 0)
        for copy in copies[:2]:
            copy.wait()
        fill_bias(polar_ref, rel_ref[...], bias_ref, rows // 2, "nhi")
        for copy in copies[2:]:
            copy.wait()


def mix_kernel(
    e_ref, ra_ref, rb_ref, taps_ref, shift_ref, land_ref, w_ref, stream_ref, qkv_hbm, out_hbm,
    act_in, edge_in, mixed_ref, sent_ref, act_ref, edge_ref, qkv_ref, wout_ref, perm_ref, sem,
    *, chunk, lat,
):
    rows, cols, width_exp = e_ref.shape
    tokens = rows * cols
    steps = width_exp // chunk
    lat_even = even(lat)
    copies = [
        pltpu.make_async_copy(src, dst, sem.at[i])
        for i, (src, dst) in enumerate(((qkv_hbm, qkv_ref), (out_hbm, wout_ref)))
    ]
    for copy in copies:
        copy.start()
    perm_ref[...] = send_matrix(rows, cols, False)

    def conv(i):
        for k in range(chunk // 128):
            lanes = pl.ds(pl.multiple_of(i * chunk + k * 128, 128), 128)
            ra = ra_ref[:, lanes].astype(F32)
            rb = rb_ref[:, lanes].astype(F32)
            top = [jnp.where(lat_even, rb, ra)] + [e_ref[r, :, lanes].astype(F32) for r in (0, 1)]
            bottom = [e_ref[r, :, lanes].astype(F32) for r in (rows - 2, rows - 1)]
            bottom += [jnp.where(lat_even, ra, rb)]
            for x, r in ((top, 0), (bottom, rows - 1)):
                filter_line(
                    x, r, lanes, taps_ref, shift_ref, land_ref, edge_ref, act_ref, rows, cols
                )

    def step(i, carry):
        conv(i)
        return carry

    lax.fori_loop(0, steps, step, 0)
    projected = jnp.dot(act_ref[...], w_ref[...], preferred_element_type=F32)
    mixed = (stream_ref[...].reshape(projected.shape).astype(F32) + projected).astype(BF16)
    mixed_ref[...] = mixed
    normed = normalize(mixed.astype(F32)).astype(BF16)
    sent = jnp.dot(perm_ref[...], normed, preferred_element_type=F32)
    for k in range(tokens // 4):
        sent_ref[k] = sent[4 * k : 4 * k + 4].astype(BF16)
    for copy in copies:
        copy.wait()


def edge_kernel(
    edge_ref, ca_ref, cb_ref, taps_ref, w_ref, stream_ref, sent_ref, inner_ref,
    mixed_ref, out_ref, act, cell_ref, *, lon, chunk,
):
    double, width_exp = edge_ref.shape
    rows = double // 2
    lon_even = even(lon)
    half = rows // 2
    part = width_exp // half
    ca, cb = ca_ref[:, width_exp:].astype(F32), cb_ref[:, width_exp:].astype(F32)
    for side, cells in enumerate((jnp.where(lon_even, cb, ca), jnp.where(lon_even, ca, cb))):
        for end in range(2):
            for k in range(half):
                at, row = 2 * side + end, half * end + k
                cell_ref[at : at + 1, part * k : part * (k + 1)] = cells[row : row + 1]
    for i in range(width_exp // chunk):
        lanes = slice(i * chunk, (i + 1) * chunk)
        ca = ca_ref[:, lanes].astype(F32)
        cb = cb_ref[:, lanes].astype(F32)
        beyond = []
        for side, own in enumerate((jnp.where(lon_even, cb, ca), jnp.where(lon_even, ca, cb))):
            above, below = (cell_ref[2 * side + end : 2 * side + end + 1, lanes] for end in range(2))
            column = jnp.concatenate([above, own, below], axis=0)
            beyond.append(
                sum(
                    taps_ref[a, 2 * side : 2 * side + 1, lanes] * column[a : a + rows]
                    for a in range(3)
                )
            )
        filtered = edge_ref[:, lanes] + jnp.concatenate(beyond, axis=0)
        act[:, lanes] = gelu(filtered).astype(BF16)
    projected = jnp.dot(act[...], w_ref[...], preferred_element_type=F32)
    cols = stream_ref.shape[1]
    first = jnp.concatenate([stream_ref[r, 0:1].astype(F32) for r in range(rows)], axis=0)
    last = jnp.concatenate([stream_ref[r, cols - 1 : cols].astype(F32) for r in range(rows)], axis=0)
    mixed = (jnp.concatenate([first, last], axis=0) + projected).astype(BF16)
    mixed = mixed.astype(F32)
    normed = normalize(mixed).astype(BF16).astype(F32)
    sub = lax.broadcasted_iota(jnp.int32, (cols, mixed.shape[1]), 0)
    for r in range(rows):
        part = slice(r * cols, (r + 1) * cols)
        inner = inner_ref[part].astype(F32)
        inner = jnp.where(sub == 0, mixed[r : r + 1], inner)
        inner = jnp.where(sub == cols - 1, mixed[rows + r : rows + r + 1], inner)
        mixed_ref[part] = inner.astype(BF16)
    out_ref[...] = sent_ref[...]
    pairs = cols // 2
    strips = rows // 2
    for s in range(strips):
        for side, c2 in ((0, 0), (1, pairs - 1)):
            k = s * pairs + c2
            old = sent_ref[k].astype(F32)
            keep = [old[0:1], old[1:2], old[2:3], old[3:4]]
            for m in range(2):
                at = side * rows + m * strips + s
                keep[2 * m + side] = normed[at : at + 1]
            out_ref[k] = jnp.concatenate(keep, axis=0).astype(BF16)


def attend_kernel(x_ref, w_ref, bias_ref, out_ref, x_buf, qk_buf, v_buf, o_buf, *, heads):
    tokens = 4 * x_ref.shape[0]
    width = x_ref.shape[2]
    head_dim = width // heads
    for k in range(tokens // 4):
        x_buf[4 * k : 4 * k + 4, :] = x_ref[k].astype(F32)
    x = x_buf[...].astype(BF16)
    scale = np.float32(head_dim**-0.5) * LOG2E
    per = 128 // head_dim
    lane_head = lax.broadcasted_iota(jnp.int32, (tokens, 128), 1) // head_dim
    ones = jnp.ones((16, tokens), BF16)
    both = 2 * width
    qk_buf[...] = jnp.dot(x, w_ref[:, :both], preferred_element_type=F32).astype(BF16)
    v_buf[...] = jnp.dot(x, w_ref[:, both:], preferred_element_type=F32)
    for p in range(heads // per):
        lanes = slice(128 * p, 128 * (p + 1))
        q = qk_buf[:, lanes]
        k = qk_buf[:, width + 128 * p : width + 128 * (p + 1)]
        v_t = jnp.concatenate([jnp.transpose(v_buf[:, lanes]).astype(BF16), ones], axis=0)
        queries = jnp.concatenate(
            [jnp.where(lane_head == j, q, jnp.zeros_like(q)) for j in range(per)], axis=0
        )
        scores = lax.dot_general(
            k, queries, (((1,), (1,)), ((), ())), preferred_element_type=F32
        )
        weights = []
        for j in range(per):
            base = bias_ref[p * per + j]
            bias = jnp.concatenate(
                [base if n == 0 else pltpu.roll(base, 16 * n, 1) for n in range(GRID)], axis=0
            )
            s = scores[:, tokens * j : tokens * (j + 1)] * scale + bias
            weights.append(jnp.exp2(s - jnp.max(s, axis=0, keepdims=True)).astype(BF16))
        summed = jnp.dot(v_t, jnp.concatenate(weights, axis=1), preferred_element_type=F32)
        parts = []
        for j in range(per):
            block = summed[:, tokens * j : tokens * (j + 1)]
            parts.append(block[head_dim * j : head_dim * (j + 1)] * (1.0 / block[128:129]))
        o_buf[:, lanes] = jnp.transpose(jnp.concatenate(parts, axis=0))
    for k in range(tokens // 4):
        out_ref[k] = o_buf[4 * k : 4 * k + 4, :].astype(BF16)


def out_kernel(a_ref, w_ref, mixed_ref, out_ref, a_buf, *, rows, cols):
    tokens = rows * cols
    for k in range(tokens // 4):
        a_buf[4 * k : 4 * k + 4, :] = a_ref[k].astype(F32)
    attended = jnp.dot(
        send_matrix(rows, cols, True), a_buf[...].astype(BF16), preferred_element_type=F32
    ).astype(BF16)
    result = mixed_ref[...].astype(F32) + jnp.dot(
        attended, w_ref[...], preferred_element_type=F32
    )
    out_ref[...] = result.astype(BF16)


def local(expanded, stream, land, polar, land_shift, dw_kernel, w_proj, w_qkv, w_out, rel_bias):
    rows, cols, width_exp = expanded.shape
    width = stream.shape[2]
    heads = rel_bias.shape[0]
    tokens = rows * cols
    lon, lat = ("nhi", "nlo"), "lat"
    lons, lats = lax.axis_size(lon), lax.axis_size(lat)
    everyone = lon + (lat,)
    swap_core = [(i, i ^ 1) for i in range(lats)]
    swap_next = [(i, j) for k in range(1, lats - 1, 2) for i, j in ((k, k + 1), (k + 1, k))]

    def call(kernel, name, ins, in_specs, outs, scratch, limit, **more):
        return pl.pallas_call(
            kernel,
            name=name,
            out_shape=tuple(pltpu.VMEM(shape, dtype) for shape, dtype in outs),
            in_specs=in_specs,
            out_specs=(VM,) * len(outs),
            scratch_shapes=scratch,
            compiler_params=pltpu.CompilerParams(vmem_limit_bytes=limit << 20),
            **more,
        )(*ins)

    row_shape, col_shape = ((cols, width_exp), BF16), ((rows, width_exp), BF16)
    end_shape = ((2, width_exp), BF16)
    small = (expanded, dw_kernel, land_shift[None], land, stream)
    e_here, taps, shift, land, stream, *picked = call(
        functools.partial(pick_kernel, lat=lat, lon=lon), "pick", map(in_hbm, small), [HBM] * 5,
        [(x.shape, x.dtype) for x in small] + [end_shape] * 2 + [row_shape] * 2 + [col_shape] * 2,
        [pltpu.VMEM((rows, width_exp), F32)] * 2 + [pltpu.SemaphoreType.DMA((rows + 4,))], 8,
    )
    rel = jnp.transpose(rel_bias, (1, 2, 0)).reshape(-1, heads)
    chunk = 256
    fixed = (e_here, taps, shift, land, *map(in_hbm, (w_proj, rel, polar)))
    inner_outs = [
        ((tokens, width_exp), BF16), ((2 * rows, width_exp), F32), ((tokens, 128), F32),
        (w_proj.shape, BF16), ((heads, 2 * GRID, 128), F32),
    ]
    inner_scratch = [
        pltpu.VMEM(rel.shape, F32), pltpu.SMEM(polar.shape, jnp.int32), pltpu.SemaphoreType.DMA((3,)),
    ]
    end_a, end_b, row_a, row_b, col_a, col_b = picked
    far_a = lax.ppermute(end_a, lat, swap_core)
    far_b = lax.ppermute(end_b, lat, swap_next)
    got_a = lax.ppermute(row_a, lat, swap_core)
    got_b = lax.ppermute(row_b, lat, swap_next)
    *inner, far_a = call(
        functools.partial(inner_kernel, aliased=1, early=True, chunk=chunk), "inner_early",
        (*fixed, far_a), [VM] * 4 + [HBM] * 3 + [VM],
        inner_outs + [end_shape], inner_scratch, 8, input_output_aliases={7: 5},
    )
    col_a, col_b = call(
        functools.partial(pack_kernel, lat=lat, lon=lon), "pack", (col_a, col_b, far_a, far_b),
        [VM] * 4, [((rows, width_exp + 2 * width_exp // rows), BF16)] * 2, [], 4,
    )
    seen_b = lax.ppermute(
        col_b, lon, [(i, (i + 1) % lons if i % 2 else (i - 1) % lons) for i in range(lons)]
    )
    seen_a = lax.ppermute(col_a, lon, [(i, i ^ 1) for i in range(lons)])
    act, edge, land_lanes, w_proj, bias, *_ = call(
        functools.partial(inner_kernel, aliased=6, early=False, chunk=chunk), "inner_late",
        (*fixed, *inner, col_a), [VM] * 4 + [HBM] * 3 + [VM] * 6, inner_outs, inner_scratch, 8,
        input_output_aliases={7 + i: i for i in range(5)},
        cost_estimate=pl.CostEstimate(flops=10**9, bytes_accessed=10**6, transcendentals=0),
    )
    token_shape, sent_shape = ((tokens, width), BF16), ((tokens // 4, 4, width), BF16)
    mixed, sent, act, edge, w_qkv, w_out = call(
        functools.partial(mix_kernel, chunk=chunk, lat=lat), "mix",
        (
            e_here, got_a, got_b, taps, shift, land_lanes, w_proj, stream,
            in_hbm(w_qkv), in_hbm(w_out), act, edge,
        ),
        [VM] * 8 + [HBM] * 2 + [VM] * 2,
        [token_shape, sent_shape] + inner_outs[:2] + [(w_qkv.shape, BF16), (w_out.shape, BF16)],
        [
            pltpu.VMEM((tokens, tokens), BF16), pltpu.SemaphoreType.DMA((2,)),
        ],
        8, input_output_aliases={10: 2, 11: 3},
        cost_estimate=pl.CostEstimate(flops=10**9, bytes_accessed=10**6, transcendentals=0),
    )
    mixed, sent = call(
        functools.partial(edge_kernel, lon=lon, chunk=chunk), "edge",
        (edge, seen_a, seen_b, taps, w_proj, stream, sent, mixed), [VM] * 8,
        [token_shape, sent_shape],
        [pltpu.VMEM((2 * rows, width_exp), BF16), pltpu.VMEM((4, width_exp), F32)], 8,
    )

    group = ("nhi", lat)
    mine = lax.all_to_all(sent, group, 0, 0, tiled=True)
    attended = pl.pallas_call(
        functools.partial(attend_kernel, heads=heads),
        name="attend",
        out_shape=jax.ShapeDtypeStruct((tokens // 4, 4, width), BF16),
        in_specs=[VM] * 3,
        out_specs=VM,
        scratch_shapes=[
            pltpu.VMEM((tokens, width), F32), pltpu.VMEM((tokens, 2 * width), BF16),
            pltpu.VMEM((tokens, width), F32), pltpu.VMEM((tokens, width), F32),
        ],
        compiler_params=pltpu.CompilerParams(vmem_limit_bytes=8 << 20),
    )(mine, w_qkv, bias)
    back = lax.all_to_all(attended, group, 0, 0, tiled=True)
    result = pl.pallas_call(
        functools.partial(out_kernel, rows=rows, cols=cols),
        name="out",
        out_shape=jax.ShapeDtypeStruct((tokens, width), BF16),
        in_specs=[VM] * 3,
        out_specs=VM,
        scratch_shapes=[pltpu.VMEM((tokens, width), F32)],
        compiler_params=pltpu.CompilerParams(vmem_limit_bytes=8 << 20),
    )(back, w_out, mixed)
    return result.reshape(rows, cols, width)


def solution(mesh):
    lons, lats = mesh.shape["lon"], mesh.shape["lat"]
    fine = Mesh(mesh.devices.reshape(GRID, lons // GRID, lats), ("nhi", "nlo", "lat"))
    lon = ("nhi", "nlo")
    in_specs = (P("lat", lon, None), P("lat", lon, None), P("lat", lon)) + (P(),) * 7
    return jax.shard_map(
        local, mesh=fine, in_specs=in_specs, out_specs=P("lat", lon, None), check_vma=False
    )
```

time: 55 us -> 51.3 us (0.933)
  Pallas kernels: 13.2 us -> 10.7 us
  waiting for transfers between devices: 2.97 us -> 0.66 us
  blocking collectives: 22.8 us -> 24 us
  other arithmetic: 0.96 us -> 0 us
  starting transfers between devices: 14.7 us -> 15.3 us
    ppermute x2 -> x4, starting transfers between devices: 5.24 us -> 8.97 us  [the longest x1 3.64 us: local(): got_b = lax.ppermute(row_b, lat, swap_next)]
    ppermute x1, starting transfers between devices: 9.38 us -> 6.36 us  [local(): lax.ppermute(col_b, lon, [(i, (i + 1) % lons if i % 2 else (i - 1) % lons...]
    ppermute x2 -> x4, waiting for transfers between devices: 2.96 us -> 0.01 us  [the longest x1 0.01 us: local(): far_a = lax.ppermute(end_a, lat, swap_core)]
    pallas_call x4 -> x6, Pallas kernels: 8.96 us -> 7.34 us  [call(): pl.pallas_call(kernel, name=name, out_shape=tuple((pltpu.VMEM(shape, dtyp...]
    all_to_all x1, blocking collectives: 10.7 us -> 11.8 us  [local(): mine = lax.all_to_all(sent, group, 0, 0, tiled=True)]
    select_n x1 -> x0, other arithmetic: 0.96 us -> none  [local(): row_a = jnp.where(lat_even, bottom_row, top_row)]
    pallas_call x1, Pallas kernels: 3.03 us -> 2.15 us  [local(): pl.pallas_call(functools.partial(attend_kernel, heads=heads), name='atten...]
    ppermute x1, waiting for transfers between devices: 0.01 us -> 0.55 us  [local(): seen_a = lax.ppermute(col_a, lon, [(i, i ^ 1) for i in range(lons)])]
  transfers between devices with their start and end apart: 4 -> 6, of which waited for: 1 -> 2; matrix products, arithmetic and copies ran while one was open for 0% -> 0% of each run, Pallas kernels for 14% -> 10%
where the time goes in v2:
time: 51.3 us; the launch traced here: 50.8 us
  blocking collectives  24 us (47%)
  starting transfers between devices  15.3 us (30%)
  Pallas kernels  10.7 us (21%)
  waiting for transfers between devices  0.66 us (1%)
    all_to_all x1, blocking collectives, local(): back = lax.all_to_all(attended, group, 0, 0, tiled=True)  12.2 us
    all_to_all x1, blocking collectives, local(): mine = lax.all_to_all(sent, group, 0, 0, tiled=True)  11.8 us
    pallas_call x6, Pallas kernels, call(): pl.pallas_call(kernel, name=name, out_shape=tuple((pltpu.VMEM(shape, dtyp...  7.34 us
    ppermute x1, starting transfers between devices, local(): lax.ppermute(col_b, lon, [(i, (i + 1) % lons if i % 2 else (i - 1) % lons...  6.36 us
    ppermute x1, starting transfers between devices, local(): got_b = lax.ppermute(row_b, lat, swap_next)  3.64 us
    ppermute x1, starting transfers between devices, local(): far_a = lax.ppermute(end_a, lat, swap_core)  3.33 us
    pallas_call x1, Pallas kernels, local(): pl.pallas_call(functools.partial(attend_kernel, heads=heads), name='atten...  2.15 us
    ppermute x1, starting transfers between devices, local(): far_b = lax.ppermute(end_b, lat, swap_next)  1.91 us
  transfers between devices with their start and end apart: 6, of which 2 were waited for; matrix products, arithmetic and copies ran while one was open for 0% of the time, Pallas kernels for 10%

profile of v2, /device:TPU:1, one launch (start us, length us, event | category | flops | bytes accessed | tf_op | source)
XLA Modules:
  0.0 50.8 jit_solution(7079089305395422238)
XLA Ops:
  0.0 1.4 %pick.1 = (bf16[8,16,3072]{2,1,0:T(8,128)(2,1)S(1)}, f32[3,3,3072]{2,1,0:T(4,128)S(1)}, f32[1,3072]{1,0:T(1,128)S(1)}, s32[8,16]{1,0:T(8,128)S(1)}, bf16[8,16,76...) custom-call(bf16[8,16,3072]{2,1,0:T(8,128)(2,1)} %refs_0_.1, ...), custom_call_target="tpu_custom_call" | custom-call | tf_op jit(solution)/shard_map/pick/pallas_call | solution.py:365
  1.4 3.3 %collective-permute-start.2 = (bf16[2,3072]{1,0:T(2,128)(2,1)S(1)}, bf16[2,3072]{1,0:T(2,128)(2,1)S(1)}, u32[]{:S(2)}, u32[]{:S(2)}) collective-permute-start(bf16[2,3072]{1,0:T(2,128)(2,1)S(1)} %get-tuple-element.42), channel_id=1, source_target_pairs={{0,1},{1,0},{2,3},{3,2},{4,5},{5,4},{6,7},{7,6},{8,9},{9,8},{10,11... | collective-permute-start | bytes 36872 | tf_op jit(solution)/shard_map/ppermute | solution.py:395
  4.8 1.9 %collective-permute-start.3 = (bf16[2,3072]{1,0:T(2,128)(2,1)S(1)}, bf16[2,3072]{1,0:T(2,128)(2,1)S(1)}, u32[]{:S(2)}, u32[]{:S(2)}) collective-permute-start(bf16[2,3072]{1,0:T(2,128)(2,1)S(1)} %get-tuple-element.51), channel_id=1, source_target_pairs={{1,2},{2,1},{5,6},{6,5},{9,10},{10,9},{13,14},{14,13},{17,18},{18,... | collective-permute-start | bytes 36872 | tf_op jit(solution)/shard_map/ppermute | solution.py:396
  6.7 0.1 collective-permute-start
  6.8 3.6 %collective-permute-start.1 = (bf16[16,3072]{1,0:T(8,128)(2,1)S(1)}, bf16[16,3072]{1,0:T(8,128)(2,1)S(1)}, u32[]{:S(2)}, u32[]{:S(2)}) collective-permute-start(bf16[16,3072]{1,0:T(8,128)(2,1)S(1)} %get-tuple-element.38), channel_id=1, source_target_pairs={{1,2},{2,1},{5,6},{6,5},{9,10},{10,9},{13,14},{14,13},{17,18},{18,... | collective-permute-start | bytes 294920 | tf_op jit(solution)/shard_map/ppermute | solution.py:398
  10.4 0.0 collective-permute-done.2.refs_7_
  10.5 2.4 %inner_early.1 = (bf16[128,3072]{1,0:T(8,128)(2,1)S(1)}, f32[16,3072]{1,0:T(8,128)S(1)}, f32[128,128]{1,0:T(8,128)S(1)}, bf16[3072,768]{1,0:T(8,128)(2,1)S(1)}, ...) custom-call(bf16[8,16,3072]{2,1,0:T(8,128)(2,1)S(1)} %get-tuple-element.36.refs_0_.e_ref, ...), custom_call_target="tpu_custom_call", output_to_operand_aliasing={{5}: (7, {})} | custom-call | tf_op jit(solution)/shard_map/inner_early/pallas_call | solution.py:365
  12.9 0.0 collective-permute-done.3.xb_ref
  12.9 0.1 pack.1
  13.0 6.4 %collective-permute-start.5 = (bf16[8,3840]{1,0:T(8,128)(2,1)S(1)}, bf16[8,3840]{1,0:T(8,128)(2,1)S(1)}, u32[]{:S(2)}, u32[]{:S(2)}) collective-permute-start(bf16[8,3840]{1,0:T(8,128)(2,1)S(1)} %get-tuple-element.59), channel_id=1, source_target_pairs={{0,252},{4,8},{8,4},{12,16},{16,12},{20,24},{24,20},{28,32},{32,28... | collective-permute-start | bytes 184328 | tf_op jit(solution)/shard_map/ppermute | solution.py:408
  19.3 0.0 collective-permute-start.4
  19.4 0.0 collective-permute-done.ra_ref
  19.4 0.0 collective-permute-done.1.rb_ref
  19.4 2.4 %mix.1 = (bf16[128,768]{1,0:T(8,128)(2,1)S(1)}, bf16[32,4,768]{2,1,0:T(4,128)(2,1)S(1)}, bf16[128,3072]{1,0:T(8,128)(2,1)S(1)}, f32[16,3072]{1,0:T(8,128)S(1)}, ...) custom-call(bf16[8,16,3072]{2,1,0:T(8,128)(2,1)S(1)} %get-tuple-elemen, ...), custom_call_target="tpu_custom_call", output_to_operand_aliasing={{2}: (10, {}), {3}: (11, {})} | custom-call | flops 1000000000 | bytes 1000000 | tf_op jit(solution)/shard_map/mix/pallas_call | solution.py:365
  21.8 0.1 collective-permute-done.5.cb_ref
  21.8 0.6 %collective-permute-done.4.ca_ref = bf16[8,3840]{1,0:T(8,128)(2,1)S(1)} collective-permute-done((bf16[8,3840]{1,0:T(8,128)(2,1)S(1)}, bf16[8,3840]{1,0:T(8,128)(2,1)S(1)}, u32[]{:S(2)}, u32[]{:S(2)}) %collective-permute-start.4) | collective-permute-done | bytes 61472 | tf_op jit(solution)/shard_map/ppermute | solution.py:411
  22.4 1.0 %edge.1 = (bf16[128,768]{1,0:T(8,128)(2,1)S(1)}, bf16[32,4,768]{2,1,0:T(4,128)(2,1)S(1)}) custom-call(f32[16,3072]{1,0:T(8,128)S(1)} %get-tuple-element.58.edge_ref, bf16[8,3840]{1,0:T(8,128)(2,1)S(1)} %collective-permute-done.4.ca_ref, bf16[8,3840]{1,0:T(8,128)(2,1)S(1)} %collective-permute-done.5.cb_ref, ...), custom_call_target="tpu_custom_call" | custom-call | tf_op jit(solution)/shard_map/edge/pallas_call | solution.py:365
  23.4 11.8 %all_to_all.10.x_ref = bf16[32,4,768]{2,1,0:T(4,128)(2,1)S(1)} all-to-all(bf16[32,4,768]{2,1,0:T(4,128)(2,1)S(1)} %get-tuple-element.62), channel_id=1, replica_groups=mesh['nhi'=8,'nlo'=8,'lat'=4] {'nhi','lat'}, dimensions={0} | all-to-all | bytes 393216 | tf_op jit(solution)/shard_map/all_to_all | solution.py:441
  35.3 2.1 %attend.1 = bf16[32,4,768]{2,1,0:T(4,128)(2,1)S(1)} custom-call(bf16[32,4,768]{2,1,0:T(4,128)(2,1)S(1)} %all_to_all.10.x_ref, bf16[768,2304]{1,0:T(8,128)(2,1)S(1)} %get-tuple-element.63.w_ref, f32[24,16,128]{2,1,0:T(8,128)S(1)} %get-tuple-element.64.bias_ref), custom_call_target="tpu_custom_call" | custom-call | tf_op jit(solution)/shard_map/attend/pallas_call | solution.py:442
  37.4 12.2 %all_to_all.11.a_ref = bf16[32,4,768]{2,1,0:T(4,128)(2,1)S(1)} all-to-all(bf16[32,4,768]{2,1,0:T(4,128)(2,1)S(1)} %attend.1), channel_id=1, replica_groups=mesh['nhi'=8,'nlo'=8,'lat'=4] {'nhi','lat'}, dimensions={0} | all-to-all | bytes 393216 | tf_op jit(solution)/shard_map/all_to_all | solution.py:454
  49.6 1.2 %out.1 = bf16[128,768]{1,0:T(8,128)(2,1)} custom-call(bf16[32,4,768]{2,1,0:T(4,128)(2,1)S(1)} %all_to_all.11.a_ref, bf16[768,768]{1,0:T(8,128)(2,1)S(1)} %get-tuple-element.65.w_ref, bf16[128,768]{1,0:T(8,128)(2,1)S(1)} %get-tuple-element.66.mixed_ref), custom_call_target="tpu_custom_call" | custom-call | tf_op jit(solution)/shard_map/out/pallas_call | solution.py:455
  (1 shorter events, 0.0 us)
Async XLA Ops:
  1.4 9.0 %collective-permute-start.2 = (bf16[2,3072]{1,0:T(2,128)(2,1)S(1)}, bf16[2,3072]{1,0:T(2,128)(2,1)S(1)}, u32[]{:S(2)}, u32[]{:S(2)}) collective-permute-start(bf16[2,3072]{1,0:T(2,128)(2,1)S(1)} %get-tuple-element.42), channel_id=1, source_target_pairs={{0,1},{1,0},{2,3},{3,2},{4,5},{5,4},{6,7},{7,6},{8,9},{9,8},{10,11... | collective-permute-start | bytes 36872 | tf_op jit(solution)/shard_map/ppermute | solution.py:395
  4.8 8.1 %collective-permute-start.3 = (bf16[2,3072]{1,0:T(2,128)(2,1)S(1)}, bf16[2,3072]{1,0:T(2,128)(2,1)S(1)}, u32[]{:S(2)}, u32[]{:S(2)}) collective-permute-start(bf16[2,3072]{1,0:T(2,128)(2,1)S(1)} %get-tuple-element.51), channel_id=1, source_target_pairs={{1,2},{2,1},{5,6},{6,5},{9,10},{10,9},{13,14},{14,13},{17,18},{18,... | collective-permute-start | bytes 36872 | tf_op jit(solution)/shard_map/ppermute | solution.py:396
  6.7 12.7 %collective-permute-start = (bf16[16,3072]{1,0:T(8,128)(2,1)S(1)}, bf16[16,3072]{1,0:T(8,128)(2,1)S(1)}, u32[]{:S(2)}, u32[]{:S(2)}) collective-permute-start(bf16[16,3072]{1,0:T(8,128)(2,1)S(1)} %get-tuple-element.37), channel_id=1, source_target_pairs={{0,1},{1,0},{2,3},{3,2},{4,5},{5,4},{6,7},{7,6},{8,9},{9,8},{10,11... | collective-permute-start | bytes 294920 | tf_op jit(solution)/shard_map/ppermute | solution.py:397
  6.8 12.6 %collective-permute-start.1 = (bf16[16,3072]{1,0:T(8,128)(2,1)S(1)}, bf16[16,3072]{1,0:T(8,128)(2,1)S(1)}, u32[]{:S(2)}, u32[]{:S(2)}) collective-permute-start(bf16[16,3072]{1,0:T(8,128)(2,1)S(1)} %get-tuple-element.38), channel_id=1, source_target_pairs={{1,2},{2,1},{5,6},{6,5},{9,10},{10,9},{13,14},{14,13},{17,18},{18,... | collective-permute-start | bytes 294920 | tf_op jit(solution)/shard_map/ppermute | solution.py:398
  13.0 8.9 %collective-permute-start.5 = (bf16[8,3840]{1,0:T(8,128)(2,1)S(1)}, bf16[8,3840]{1,0:T(8,128)(2,1)S(1)}, u32[]{:S(2)}, u32[]{:S(2)}) collective-permute-start(bf16[8,3840]{1,0:T(8,128)(2,1)S(1)} %get-tuple-element.59), channel_id=1, source_target_pairs={{0,252},{4,8},{8,4},{12,16},{16,12},{20,24},{24,20},{28,32},{32,28... | collective-permute-start | bytes 184328 | tf_op jit(solution)/shard_map/ppermute | solution.py:408
  19.3 3.1 %collective-permute-start.4 = (bf16[8,3840]{1,0:T(8,128)(2,1)S(1)}, bf16[8,3840]{1,0:T(8,128)(2,1)S(1)}, u32[]{:S(2)}, u32[]{:S(2)}) collective-permute-start(bf16[8,3840]{1,0:T(8,128)(2,1)S(1)} %get-tuple-element.52.refs_12_), channel_id=1, source_target_pairs={{0,4},{4,0},{8,12},{12,8},{16,20},{20,16},{24,28},{28,24},{32,36},... | collective-permute-start | bytes 184328 | tf_op jit(solution)/shard_map/ppermute | solution.py:411

commit v3 on v2

--- a/solution.py
+++ b/solution.py
@@ -20,17 +20,20 @@
 HBM = pl.BlockSpec(memory_space=pltpu.HBM)
 
 
+def at_pole(lat):
+    at = lax.axis_index(lat)
+    return (at == 0) | (at == lax.axis_size(lat) - 1)
+
+
 def in_hbm(x):
     return pltpu.with_memory_space_constraint(x, pltpu.HBM)
 
 
-def send_matrix(rows, cols, back):
+def send_matrix(rows, cols):
     tokens = rows * cols
     strips, pairs = rows // 2, cols // 2
     to = lax.broadcasted_iota(jnp.int32, (tokens, tokens), 0)
     at = lax.broadcasted_iota(jnp.int32, (tokens, tokens), 1)
-    if back:
-        to, at = at, to
     s, rest = to // (4 * pairs), to % (4 * pairs)
     c2, m, c1 = rest // 4, rest % 4 // 2, rest % 2
     token = (m * strips + s) * cols + 2 * c2 + c1
@@ -74,18 +77,19 @@
         copy.wait()
 
 
-def pack_kernel(ca_ref, cb_ref, xa_ref, xb_ref, oa_ref, ob_ref, *, lat, lon):
-    lat_even, lon_even = even(lat), even(lon)
-    rows, width_exp = ca_ref.shape
-    half = rows // 2
-    part = width_exp // half
-    xa, xb = xa_ref[...].astype(F32), xb_ref[...].astype(F32)
-    ends = jnp.where(lat_even, xb, xa), jnp.where(lat_even, xa, xb)
-    for c_ref, o_ref, is_last in ((ca_ref, oa_ref, lon_even), (cb_ref, ob_ref, ~lon_even)):
-        o_ref[:, :width_exp] = c_ref[...]
-        cells = [jnp.where(is_last, end[1:2], end[0:1]) for end in ends]
-        quarters = [cell[:, part * k : part * (k + 1)] for cell in cells for k in range(half)]
-        o_ref[:, width_exp:] = jnp.concatenate(quarters, axis=0).astype(BF16)
+def pack_kernel(c_ref, xa_ref, xb_ref, taps_ref, *refs, lat, lon, second):
+    o_ref = refs[-1]
+    lat_even, is_last = even(lat), even(lon) ^ second
+    rows = c_ref.shape[0]
+    xa, xb = xa_ref[...].astype(F32), jnp.where(at_pole(lat), 0.0, xb_ref[...].astype(F32))
+    above, below = jnp.where(lat_even, xb, xa), jnp.where(lat_even, xa, xb)
+    sub = lax.broadcasted_iota(jnp.int32, c_ref.shape, 0)
+    here = c_ref[...].astype(F32)
+    up, down = (jnp.where(is_last, end[1:2], end[0:1]) for end in (above, below))
+    up = jnp.where(sub == 0, up, pltpu.roll(here, 1, 0))
+    down = jnp.where(sub == rows - 1, down, pltpu.roll(here, rows - 1, 0))
+    tap = [jnp.where(is_last, taps_ref[i, 0:1], taps_ref[i, 2:3]) for i in range(3)]
+    o_ref[...] = (tap[0] * up + tap[1] * here + tap[2] * down).astype(BF16)
 
 
 def gelu(x):
@@ -197,20 +201,20 @@
     rows, cols, width_exp = e_ref.shape
     tokens = rows * cols
     steps = width_exp // chunk
-    lat_even = even(lat)
+    lat_even, pole = even(lat), at_pole(lat)
     copies = [
         pltpu.make_async_copy(src, dst, sem.at[i])
         for i, (src, dst) in enumerate(((qkv_hbm, qkv_ref), (out_hbm, wout_ref)))
     ]
     for copy in copies:
         copy.start()
-    perm_ref[...] = send_matrix(rows, cols, False)
+    perm_ref[...] = send_matrix(rows, cols)
 
     def conv(i):
         for k in range(chunk // 128):
             lanes = pl.ds(pl.multiple_of(i * chunk + k * 128, 128), 128)
             ra = ra_ref[:, lanes].astype(F32)
-            rb = rb_ref[:, lanes].astype(F32)
+            rb = jnp.where(pole, 0.0, rb_ref[:, lanes].astype(F32))
             top = [jnp.where(lat_even, rb, ra)] + [e_ref[r, :, lanes].astype(F32) for r in (0, 1)]
             bottom = [e_ref[r, :, lanes].astype(F32) for r in (rows - 2, rows - 1)]
             bottom += [jnp.where(lat_even, ra, rb)]
@@ -236,37 +240,19 @@
 
 
 def edge_kernel(
-    edge_ref, ca_ref, cb_ref, taps_ref, w_ref, stream_ref, sent_ref, inner_ref,
-    mixed_ref, out_ref, act, cell_ref, *, lon, chunk,
+    edge_ref, ca_ref, cb_ref, w_ref, stream_ref, sent_ref, inner_ref, mixed_ref, out_ref,
+    *, lon, chunk,
 ):
     double, width_exp = edge_ref.shape
     rows = double // 2
     lon_even = even(lon)
-    half = rows // 2
-    part = width_exp // half
-    ca, cb = ca_ref[:, width_exp:].astype(F32), cb_ref[:, width_exp:].astype(F32)
-    for side, cells in enumerate((jnp.where(lon_even, cb, ca), jnp.where(lon_even, ca, cb))):
-        for end in range(2):
-            for k in range(half):
-                at, row = 2 * side + end, half * end + k
-                cell_ref[at : at + 1, part * k : part * (k + 1)] = cells[row : row + 1]
-    for i in range(width_exp // chunk):
-        lanes = slice(i * chunk, (i + 1) * chunk)
-        ca = ca_ref[:, lanes].astype(F32)
-        cb = cb_ref[:, lanes].astype(F32)
-        beyond = []
-        for side, own in enumerate((jnp.where(lon_even, cb, ca), jnp.where(lon_even, ca, cb))):
-            above, below = (cell_ref[2 * side + end : 2 * side + end + 1, lanes] for end in range(2))
-            column = jnp.concatenate([above, own, below], axis=0)
-            beyond.append(
-                sum(
-                    taps_ref[a, 2 * side : 2 * side + 1, lanes] * column[a : a + rows]
-                    for a in range(3)
-                )
-            )
-        filtered = edge_ref[:, lanes] + jnp.concatenate(beyond, axis=0)
-        act[:, lanes] = gelu(filtered).astype(BF16)
-    projected = jnp.dot(act[...], w_ref[...], preferred_element_type=F32)
+    projected = 0.0
+    for at in range(0, width_exp, chunk):
+        lanes = slice(at, at + chunk)
+        ca, cb = ca_ref[:, lanes].astype(F32), cb_ref[:, lanes].astype(F32)
+        beyond = jnp.where(lon_even, cb, ca), jnp.where(lon_even, ca, cb)
+        act = gelu(edge_ref[:, lanes] + jnp.concatenate(beyond, axis=0)).astype(BF16)
+        projected += jnp.dot(act, w_ref[lanes, :], preferred_element_type=F32)
     cols = stream_ref.shape[1]
     first = jnp.concatenate([stream_ref[r, 0:1].astype(F32) for r in range(rows)], axis=0)
     last = jnp.concatenate([stream_ref[r, cols - 1 : cols].astype(F32) for r in range(rows)], axis=0)
@@ -280,7 +266,6 @@
         inner = jnp.where(sub == 0, mixed[r : r + 1], inner)
         inner = jnp.where(sub == cols - 1, mixed[rows + r : rows + r + 1], inner)
         mixed_ref[part] = inner.astype(BF16)
-    out_ref[...] = sent_ref[...]
     pairs = cols // 2
     strips = rows // 2
     for s in range(strips):
@@ -294,7 +279,7 @@
             out_ref[k] = jnp.concatenate(keep, axis=0).astype(BF16)
 
 
-def attend_kernel(x_ref, w_ref, bias_ref, out_ref, x_buf, qk_buf, v_buf, o_buf, *, heads):
+def attend_kernel(x_ref, w_ref, bias_ref, out_ref, x_buf, qk_buf, v_buf, s_buf, p_buf, t_buf, *, heads):
     tokens = 4 * x_ref.shape[0]
     width = x_ref.shape[2]
     head_dim = width // heads
@@ -303,49 +288,53 @@
     x = x_buf[...].astype(BF16)
     scale = np.float32(head_dim**-0.5) * LOG2E
     per = 128 // head_dim
-    lane_head = lax.broadcasted_iota(jnp.int32, (tokens, 128), 1) // head_dim
+    packs = heads // per
+    row_head = lax.broadcasted_iota(jnp.int32, (128, tokens), 0) // head_dim
     ones = jnp.ones((16, tokens), BF16)
     both = 2 * width
     qk_buf[...] = jnp.dot(x, w_ref[:, :both], preferred_element_type=F32).astype(BF16)
-    v_buf[...] = jnp.dot(x, w_ref[:, both:], preferred_element_type=F32)
-    for p in range(heads // per):
-        lanes = slice(128 * p, 128 * (p + 1))
-        q = qk_buf[:, lanes]
-        k = qk_buf[:, width + 128 * p : width + 128 * (p + 1)]
-        v_t = jnp.concatenate([jnp.transpose(v_buf[:, lanes]).astype(BF16), ones], axis=0)
+    v_buf[...] = jnp.dot(x, w_ref[:, both:], preferred_element_type=F32).astype(BF16)
+    for p in range(packs):
+        q = jnp.transpose(qk_buf[:, 128 * p : 128 * (p + 1)])
         queries = jnp.concatenate(
-            [jnp.where(lane_head == j, q, jnp.zeros_like(q)) for j in range(per)], axis=0
+            [jnp.where(row_head == j, q, jnp.zeros_like(q)) for j in range(per)], axis=1
         )
-        scores = lax.dot_general(
-            k, queries, (((1,), (1,)), ((), ())), preferred_element_type=F32
+        keys = qk_buf[:, width + 128 * p : width + 128 * (p + 1)]
+        span = slice(per * tokens * p, per * tokens * (p + 1))
+        s_buf[:, span] = jnp.dot(keys, queries, preferred_element_type=F32)
+    for h in range(heads):
+        base = bias_ref[h]
+        bias = jnp.concatenate(
+            [base if n == 0 else pltpu.roll(base, 2 * GRID * n, 1) for n in range(GRID)], axis=0
         )
-        weights = []
-        for j in range(per):
-            base = bias_ref[p * per + j]
-            bias = jnp.concatenate(
-                [base if n == 0 else pltpu.roll(base, 16 * n, 1) for n in range(GRID)], axis=0
-            )
-            s = scores[:, tokens * j : tokens * (j + 1)] * scale + bias
-            weights.append(jnp.exp2(s - jnp.max(s, axis=0, keepdims=True)).astype(BF16))
-        summed = jnp.dot(v_t, jnp.concatenate(weights, axis=1), preferred_element_type=F32)
-        parts = []
+        span = slice(tokens * h, tokens * (h + 1))
+        s = s_buf[:, span] * scale + bias
+        p_buf[:, span] = jnp.exp2(s - jnp.max(s, axis=0, keepdims=True)).astype(BF16)
+    for p in range(packs):
+        values = jnp.concatenate([jnp.transpose(v_buf[:, 128 * p : 128 * (p + 1)]), ones], axis=0)
+        span = slice(per * tokens * p, per * tokens * (p + 1))
+        summed = jnp.dot(values, p_buf[:, span], preferred_element_type=F32)
         for j in range(per):
             block = summed[:, tokens * j : tokens * (j + 1)]
-            parts.append(block[head_dim * j : head_dim * (j + 1)] * (1.0 / block[128:129]))
-        o_buf[:, lanes] = jnp.transpose(jnp.concatenate(parts, axis=0))
+            at = 128 * p + head_dim * j
+            t_buf[at : at + head_dim, :] = block[head_dim * j : head_dim * (j + 1)] * (
+                1.0 / block[128:129]
+            )
+    for p in range(packs):
+        x_buf[:, 128 * p : 128 * (p + 1)] = jnp.transpose(t_buf[128 * p : 128 * (p + 1), :])
     for k in range(tokens // 4):
-        out_ref[k] = o_buf[4 * k : 4 * k + 4, :].astype(BF16)
+        out_ref[k] = x_buf[4 * k : 4 * k + 4, :].astype(BF16)
 
 
 def out_kernel(a_ref, w_ref, mixed_ref, out_ref, a_buf, *, rows, cols):
-    tokens = rows * cols
-    for k in range(tokens // 4):
-        a_buf[4 * k : 4 * k + 4, :] = a_ref[k].astype(F32)
-    attended = jnp.dot(
-        send_matrix(rows, cols, True), a_buf[...].astype(BF16), preferred_element_type=F32
-    ).astype(BF16)
+    strips, pairs = rows // 2, cols // 2
+    for k in range(a_ref.shape[0]):
+        got = a_ref[k].astype(F32)
+        for m in range(2):
+            at = (m * strips + k // pairs) * cols + 2 * (k % pairs)
+            a_buf[at : at + 2, :] = got[2 * m : 2 * m + 2]
     result = mixed_ref[...].astype(F32) + jnp.dot(
-        attended, w_ref[...], preferred_element_type=F32
+        a_buf[...].astype(BF16), w_ref[...], preferred_element_type=F32
     )
     out_ref[...] = result.astype(BF16)
 
@@ -359,7 +348,7 @@
     lons, lats = lax.axis_size(lon), lax.axis_size(lat)
     everyone = lon + (lat,)
     swap_core = [(i, i ^ 1) for i in range(lats)]
-    swap_next = [(i, j) for k in range(1, lats - 1, 2) for i, j in ((k, k + 1), (k + 1, k))]
+    swap_next = [(i, (i + 1) % lats if i % 2 else (i - 1) % lats) for i in range(lats)]
 
     def call(kernel, name, ins, in_specs, outs, scratch, limit, **more):
         return pl.pallas_call(
@@ -401,14 +390,17 @@
         (*fixed, far_a), [VM] * 4 + [HBM] * 3 + [VM],
         inner_outs + [end_shape], inner_scratch, 8, input_output_aliases={7: 5},
     )
-    col_a, col_b = call(
-        functools.partial(pack_kernel, lat=lat, lon=lon), "pack", (col_a, col_b, far_a, far_b),
-        [VM] * 4, [((rows, width_exp + 2 * width_exp // rows), BF16)] * 2, [], 4,
-    )
+    packed = []
+    for second, column in enumerate((col_a, col_b)):
+        packed += call(
+            functools.partial(pack_kernel, lat=lat, lon=lon, second=bool(second)), "pack",
+            (column, far_a, far_b, taps, *packed), [VM] * (4 + second), [col_shape], [], 4,
+        )
+    col_a, col_b = packed
+    seen_a = lax.ppermute(col_a, lon, [(i, i ^ 1) for i in range(lons)])
     seen_b = lax.ppermute(
         col_b, lon, [(i, (i + 1) % lons if i % 2 else (i - 1) % lons) for i in range(lons)]
     )
-    seen_a = lax.ppermute(col_a, lon, [(i, i ^ 1) for i in range(lons)])
     act, edge, land_lanes, w_proj, bias, *_ = call(
         functools.partial(inner_kernel, aliased=6, early=False, chunk=chunk), "inner_late",
         (*fixed, *inner, col_a), [VM] * 4 + [HBM] * 3 + [VM] * 6, inner_outs, inner_scratch, 8,
@@ -431,10 +423,9 @@
         cost_estimate=pl.CostEstimate(flops=10**9, bytes_accessed=10**6, transcendentals=0),
     )
     mixed, sent = call(
-        functools.partial(edge_kernel, lon=lon, chunk=chunk), "edge",
-        (edge, seen_a, seen_b, taps, w_proj, stream, sent, mixed), [VM] * 8,
-        [token_shape, sent_shape],
-        [pltpu.VMEM((2 * rows, width_exp), BF16), pltpu.VMEM((4, width_exp), F32)], 8,
+        functools.partial(edge_kernel, lon=lon, chunk=width), "edge",
+        (edge, seen_a, seen_b, w_proj, stream, sent, mixed), [VM] * 7,
+        [token_shape, sent_shape], [], 8, input_output_aliases={5: 1, 6: 0},
     )
 
     group = ("nhi", lat)
@@ -447,7 +438,8 @@
         out_specs=VM,
         scratch_shapes=[
             pltpu.VMEM((tokens, width), F32), pltpu.VMEM((tokens, 2 * width), BF16),
-            pltpu.VMEM((tokens, width), F32), pltpu.VMEM((tokens, width), F32),
+            pltpu.VMEM((tokens, width), BF16), pltpu.VMEM((tokens, tokens * heads), F32),
+            pltpu.VMEM((tokens, tokens * heads), BF16), pltpu.VMEM((width, tokens), F32),
         ],
         compiler_params=pltpu.CompilerParams(vmem_limit_bytes=8 << 20),
     )(mine, w_qkv, bias)

time: 51.3 us -> 47.6 us (0.928)
  starting transfers between devices: 15.3 us -> 13.6 us
  Pallas kernels: 10.7 us -> 9.99 us
  waiting for transfers between devices: 0.66 us -> 0.02 us
    ppermute x1, starting transfers between devices: 3.64 us -> 1.65 us  [local(): got_b = lax.ppermute(row_b, lat, swap_next)]
    ppermute x1, starting transfers between devices: 6.36 us -> 8.31 us  [local(): lax.ppermute(col_b, lon, [(i, (i + 1) % lons if i % 2 else (i - 1) % lons...]
    ppermute x1, starting transfers between devices: 1.91 us -> 0.01 us  [local(): far_b = lax.ppermute(end_b, lat, swap_next)]
    pallas_call x1, Pallas kernels: 2.15 us -> 1.53 us  [local(): pl.pallas_call(functools.partial(attend_kernel, heads=heads), name='atten...]
    ppermute x1, waiting for transfers between devices: 0.55 us -> 0.01 us  [local(): seen_a = lax.ppermute(col_a, lon, [(i, i ^ 1) for i in range(lons)])]
    pallas_call x6 -> x7, Pallas kernels: 7.34 us -> 7.4 us  [call(): pl.pallas_call(kernel, name=name, out_shape=tuple((pltpu.VMEM(shape, dtyp...]
  transfers between devices with their start and end apart: 6 -> 6, of which waited for: 2 -> 0; matrix products, arithmetic and copies ran while one was open for 0% -> 0% of each run, Pallas kernels for 10% -> 11%
where the time goes in v3:
time: 47.6 us; the launch traced here: 47.3 us
  blocking collectives  23.6 us (50%)
  starting transfers between devices  13.6 us (29%)
  Pallas kernels  9.99 us (21%)
    all_to_all x1, blocking collectives, local(): back = lax.all_to_all(attended, group, 0, 0, tiled=True)  12.2 us
    all_to_all x1, blocking collectives, local(): mine = lax.all_to_all(sent, group, 0, 0, tiled=True)  11.5 us
    ppermute x1, starting transfers between devices, local(): lax.ppermute(col_b, lon, [(i, (i + 1) % lons if i % 2 else (i - 1) % lons...  8.31 us
    pallas_call x7, Pallas kernels, call(): pl.pallas_call(kernel, name=name, out_shape=tuple((pltpu.VMEM(shape, dtyp...  7.4 us
    ppermute x1, starting transfers between devices, local(): far_a = lax.ppermute(end_a, lat, swap_core)  3.33 us
    ppermute x1, starting transfers between devices, local(): got_b = lax.ppermute(row_b, lat, swap_next)  1.65 us
    pallas_call x1, Pallas kernels, local(): pl.pallas_call(functools.partial(attend_kernel, heads=heads), name='atten...  1.53 us
    pallas_call x1, Pallas kernels, local(): pl.pallas_call(functools.partial(out_kernel, rows=rows, cols=cols), name=...  1.06 us
  transfers between devices with their start and end apart: 6, of which 0 were waited for; matrix products, arithmetic and copies ran while one was open for 0% of the time, Pallas kernels for 11%

profile of v3, /device:TPU:1, one launch (start us, length us, event | category | flops | bytes accessed | tf_op | source)
XLA Modules:
  0.0 47.3 jit_solution(849448468562094710)
XLA Ops:
  0.0 1.4 %pick.1 = (bf16[8,16,3072]{2,1,0:T(8,128)(2,1)S(1)}, f32[3,3,3072]{2,1,0:T(4,128)S(1)}, f32[1,3072]{1,0:T(1,128)S(1)}, s32[8,16]{1,0:T(8,128)S(1)}, bf16[8,16,76...) custom-call(bf16[8,16,3072]{2,1,0:T(8,128)(2,1)} %refs_0_.1, ...), custom_call_target="tpu_custom_call" | custom-call | tf_op jit(solution)/shard_map/pick/pallas_call | solution.py:354
  1.4 3.3 %collective-permute-start.2 = (bf16[2,3072]{1,0:T(2,128)(2,1)S(1)}, bf16[2,3072]{1,0:T(2,128)(2,1)S(1)}, u32[]{:S(2)}, u32[]{:S(2)}) collective-permute-start(bf16[2,3072]{1,0:T(2,128)(2,1)S(1)} %get-tuple-element.40), channel_id=1, source_target_pairs={{0,1},{1,0},{2,3},{3,2},{4,5},{5,4},{6,7},{7,6},{8,9},{9,8},{10,11... | collective-permute-start | bytes 36872 | tf_op jit(solution)/shard_map/ppermute | solution.py:384
  4.8 0.0 collective-permute-start.3
  4.8 0.2 collective-permute-start
  5.0 1.6 %collective-permute-start.1 = (bf16[16,3072]{1,0:T(8,128)(2,1)S(1)}, bf16[16,3072]{1,0:T(8,128)(2,1)S(1)}, u32[]{:S(2)}, u32[]{:S(2)}) collective-permute-start(bf16[16,3072]{1,0:T(8,128)(2,1)S(1)} %get-tuple-element.36), channel_id=1, source_target_pairs={{0,3},{1,2},{2,1},{3,0},{4,7},{5,6},{6,5},{7,4},{8,11},{9,10},{10,... | collective-permute-start | bytes 294920 | tf_op jit(solution)/shard_map/ppermute | solution.py:387
  6.6 0.0 collective-permute-done.2.refs_7_
  6.6 2.4 %inner_early.1 = (bf16[128,3072]{1,0:T(8,128)(2,1)S(1)}, f32[16,3072]{1,0:T(8,128)S(1)}, f32[128,128]{1,0:T(8,128)S(1)}, bf16[3072,768]{1,0:T(8,128)(2,1)S(1)}, ...) custom-call(bf16[8,16,3072]{2,1,0:T(8,128)(2,1)S(1)} %get-tuple-element.34.refs_0_.e_ref, ...), custom_call_target="tpu_custom_call", output_to_operand_aliasing={{5}: (7, {})} | custom-call | tf_op jit(solution)/shard_map/inner_early/pallas_call | solution.py:354
  9.1 0.0 collective-permute-done.3.xb_ref
  9.1 0.1 pack.2.refs_12_.refs_0_
  9.2 0.1 collective-permute-start.4
  9.3 0.1 pack.3
  9.3 8.3 %collective-permute-start.5 = (bf16[8,3072]{1,0:T(8,128)(2,1)S(1)}, bf16[8,3072]{1,0:T(8,128)(2,1)S(1)}, u32[]{:S(2)}, u32[]{:S(2)}) collective-permute-start(bf16[8,3072]{1,0:T(8,128)(2,1)S(1)} %pack.3), channel_id=1, source_target_pairs={{0,252},{4,8},{8,4},{12,16},{16,12},{20,24},{24,20},{28,32},{32,28... | collective-permute-start | bytes 147464 | tf_op jit(solution)/shard_map/ppermute | solution.py:401
  17.7 0.0 collective-permute-done.ra_ref
  17.7 0.0 collective-permute-done.1.rb_ref
  17.7 2.4 %mix.1 = (bf16[128,768]{1,0:T(8,128)(2,1)S(1)}, bf16[32,4,768]{2,1,0:T(4,128)(2,1)S(1)}, bf16[128,3072]{1,0:T(8,128)(2,1)S(1)}, f32[16,3072]{1,0:T(8,128)S(1)}, ...) custom-call(bf16[8,16,3072]{2,1,0:T(8,128)(2,1)S(1)} %get-tuple-elemen, ...), custom_call_target="tpu_custom_call", output_to_operand_aliasing={{2}: (10, {}), {3}: (11, {})} | custom-call | flops 1000000000 | bytes 1000000 | tf_op jit(solution)/shard_map/mix/pallas_call | solution.py:354
  20.1 0.0 collective-permute-done.5.cb_ref
  20.1 0.0 collective-permute-done.4.ca_ref
  20.1 1.0 %edge.1 = (bf16[128,768]{1,0:T(8,128)(2,1)S(1)}, bf16[32,4,768]{2,1,0:T(4,128)(2,1)S(1)}) custom-call(f32[16,3072]{1,0:T(8,128)S(1)} %get-tuple-element.54.edge_ref, bf16[8,3072]{1,0:T(8,128)(2,1)S(1)} %collective-permute-done.4.ca_ref, bf16[8,3072]{1,0:T(8,128)(2,1)S(1)} %collective-permute-done.5.cb_ref, ...), custom_call_target="tpu_custom_call", output_to_operand_aliasing={{1}: (5, {}), {0}: (6, {})} | custom-call | tf_op jit(solution)/shard_map/edge/pallas_call | solution.py:354
  21.1 11.5 %all_to_all.10.x_ref = bf16[32,4,768]{2,1,0:T(4,128)(2,1)S(1)} all-to-all(bf16[32,4,768]{2,1,0:T(4,128)(2,1)S(1)} %get-tuple-element.58), channel_id=1, replica_groups=mesh['nhi'=8,'nlo'=8,'lat'=4] {'nhi','lat'}, dimensions={0} | all-to-all | bytes 393216 | tf_op jit(solution)/shard_map/all_to_all | solution.py:432
  32.6 1.5 %attend.1 = bf16[32,4,768]{2,1,0:T(4,128)(2,1)S(1)} custom-call(bf16[32,4,768]{2,1,0:T(4,128)(2,1)S(1)} %all_to_all.10.x_ref, bf16[768,2304]{1,0:T(8,128)(2,1)S(1)} %get-tuple-element.59.w_ref, f32[24,16,128]{2,1,0:T(8,128)S(1)} %get-tuple-element.60.bias_ref), custom_call_target="tpu_custom_call" | custom-call | tf_op jit(solution)/shard_map/attend/pallas_call | solution.py:433
  34.1 12.2 %all_to_all.11.a_ref = bf16[32,4,768]{2,1,0:T(4,128)(2,1)S(1)} all-to-all(bf16[32,4,768]{2,1,0:T(4,128)(2,1)S(1)} %attend.1), channel_id=1, replica_groups=mesh['nhi'=8,'nlo'=8,'lat'=4] {'nhi','lat'}, dimensions={0} | all-to-all | bytes 393216 | tf_op jit(solution)/shard_map/all_to_all | solution.py:446
  46.3 1.1 %out.1 = bf16[128,768]{1,0:T(8,128)(2,1)} custom-call(bf16[32,4,768]{2,1,0:T(4,128)(2,1)S(1)} %all_to_all.11.a_ref, bf16[768,768]{1,0:T(8,128)(2,1)S(1)} %get-tuple-element.61.w_ref, bf16[128,768]{1,0:T(8,128)(2,1)S(1)} %get-tuple-element.62.mixed_ref), custom_call_target="tpu_custom_call" | custom-call | tf_op jit(solution)/shard_map/out/pallas_call | solution.py:447
  (1 shorter events, 0.0 us)
Async XLA Ops:
  1.4 5.2 %collective-permute-start.2 = (bf16[2,3072]{1,0:T(2,128)(2,1)S(1)}, bf16[2,3072]{1,0:T(2,128)(2,1)S(1)}, u32[]{:S(2)}, u32[]{:S(2)}) collective-permute-start(bf16[2,3072]{1,0:T(2,128)(2,1)S(1)} %get-tuple-element.40), channel_id=1, source_target_pairs={{0,1},{1,0},{2,3},{3,2},{4,5},{5,4},{6,7},{7,6},{8,9},{9,8},{10,11... | collective-permute-start | bytes 36872 | tf_op jit(solution)/shard_map/ppermute | solution.py:384
  4.8 4.3 %collective-permute-start.3 = (bf16[2,3072]{1,0:T(2,128)(2,1)S(1)}, bf16[2,3072]{1,0:T(2,128)(2,1)S(1)}, u32[]{:S(2)}, u32[]{:S(2)}) collective-permute-start(bf16[2,3072]{1,0:T(2,128)(2,1)S(1)} %get-tuple-element.48), channel_id=1, source_target_pairs={{0,3},{1,2},{2,1},{3,0},{4,7},{5,6},{6,5},{7,4},{8,11},{9,10},{10,... | collective-permute-start | bytes 36872 | tf_op jit(solution)/shard_map/ppermute | solution.py:385
  4.8 12.9 %collective-permute-start = (bf16[16,3072]{1,0:T(8,128)(2,1)S(1)}, bf16[16,3072]{1,0:T(8,128)(2,1)S(1)}, u32[]{:S(2)}, u32[]{:S(2)}) collective-permute-start(bf16[16,3072]{1,0:T(8,128)(2,1)S(1)} %get-tuple-element.35), channel_id=1, source_target_pairs={{0,1},{1,0},{2,3},{3,2},{4,5},{5,4},{6,7},{7,6},{8,9},{9,8},{10,11... | collective-permute-start | bytes 294920 | tf_op jit(solution)/shard_map/ppermute | solution.py:386
  5.0 12.7 %collective-permute-start.1 = (bf16[16,3072]{1,0:T(8,128)(2,1)S(1)}, bf16[16,3072]{1,0:T(8,128)(2,1)S(1)}, u32[]{:S(2)}, u32[]{:S(2)}) collective-permute-start(bf16[16,3072]{1,0:T(8,128)(2,1)S(1)} %get-tuple-element.36), channel_id=1, source_target_pairs={{0,3},{1,2},{2,1},{3,0},{4,7},{5,6},{6,5},{7,4},{8,11},{9,10},{10,... | collective-permute-start | bytes 294920 | tf_op jit(solution)/shard_map/ppermute | solution.py:387
  9.2 10.9 %collective-permute-start.4 = (bf16[8,3072]{1,0:T(8,128)(2,1)S(1)}, bf16[8,3072]{1,0:T(8,128)(2,1)S(1)}, u32[]{:S(2)}, u32[]{:S(2)}) collective-permute-start(bf16[8,3072]{1,0:T(8,128)(2,1)S(1)} %pack.2.refs_12_.refs_0_), channel_id=1, source_target_pairs={{0,4},{4,0},{8,12},{12,8},{16,20},{20,16},{24,28},{28,24},{32,36},... | collective-permute-start | bytes 147464 | tf_op jit(solution)/shard_map/ppermute | solution.py:400
  9.3 10.7 %collective-permute-start.5 = (bf16[8,3072]{1,0:T(8,128)(2,1)S(1)}, bf16[8,3072]{1,0:T(8,128)(2,1)S(1)}, u32[]{:S(2)}, u32[]{:S(2)}) collective-permute-start(bf16[8,3072]{1,0:T(8,128)(2,1)S(1)} %pack.3), channel_id=1, source_target_pairs={{0,252},{4,8},{8,4},{12,16},{16,12},{20,24},{24,20},{28,32},{32,28... | collective-permute-start | bytes 147464 | tf_op jit(solution)/shard_map/ppermute | solution.py:401

commit v4 on v3

--- a/solution.py
+++ b/solution.py
@@ -44,52 +44,46 @@
     return lax.rem(lax.axis_index(axes), 2) == 0
 
 
-def pick_kernel(*refs, lat, lon):
-    ins, outs, refs = refs[:5], refs[5:10], refs[10:]
-    xa_ref, xb_ref, ra_ref, rb_ref, ca_ref, cb_ref, first, last, sem = refs
-    e_hbm, e_ref = ins[0], outs[0]
+def pick_kernel(*refs, lat):
+    ins, outs, (xa_ref, xb_ref, ra_ref, rb_ref, first, last, sem) = refs[:4], refs[4:8], refs[8:]
+    e_ref = outs[0]
     rows, cols, _ = e_ref.shape
-    lines = [pltpu.make_async_copy(e_hbm.at[r], e_ref.at[r], sem.at[r]) for r in range(rows)]
-    rest = [
-        pltpu.make_async_copy(src, dst, sem.at[rows + i])
-        for i, (src, dst) in enumerate(zip(ins[1:], outs[1:]))
+    copies = [
+        pltpu.make_async_copy(src, dst, sem.at[i]) for i, (src, dst) in enumerate(zip(ins, outs))
     ]
-    for copy in lines + rest:
+    for copy in copies:
         copy.start()
-    for r in range(rows):
-        lines[r].wait()
-        line = e_ref[r].astype(F32)
-        first[r : r + 1, :] = line[0:1]
-        last[r : r + 1, :] = line[cols - 1 : cols]
-    lat_even, lon_even = even(lat), even(lon)
-    top = e_ref[0].astype(F32)
-    bottom = e_ref[rows - 1].astype(F32)
-    ra_ref[...] = jnp.where(lat_even, bottom, top).astype(BF16)
-    rb_ref[...] = jnp.where(lat_even, top, bottom).astype(BF16)
-    a, b = first[...], last[...]
-    ca_ref[...] = jnp.where(lon_even, b, a).astype(BF16)
-    cb_ref[...] = jnp.where(lon_even, a, b).astype(BF16)
+    lat_even = even(lat)
+    copies[0].wait()
+    ra_ref[...] = jnp.where(lat_even, e_ref[rows - 1], e_ref[0])
+    rb_ref[...] = jnp.where(lat_even, e_ref[0], e_ref[rows - 1])
+    lines = [e_ref[r].astype(F32) for r in range(rows)]
+    a = jnp.concatenate([line[0:1] for line in lines], axis=0)
+    b = jnp.concatenate([line[cols - 1 : cols] for line in lines], axis=0)
+    first[...] = a.astype(BF16)
+    last[...] = b.astype(BF16)
     above = jnp.concatenate([a[0:1], b[0:1]], axis=0)
     below = jnp.concatenate([a[rows - 1 : rows], b[rows - 1 : rows]], axis=0)
     xa_ref[...] = jnp.where(lat_even, below, above).astype(BF16)
     xb_ref[...] = jnp.where(lat_even, above, below).astype(BF16)
-    for copy in rest:
+    for copy in copies[1:]:
         copy.wait()
 
 
-def pack_kernel(c_ref, xa_ref, xb_ref, taps_ref, *refs, lat, lon, second):
+def pack_kernel(c_ref, xa_ref, xb_ref, taps_ref, *refs, lat, is_last):
     o_ref = refs[-1]
-    lat_even, is_last = even(lat), even(lon) ^ second
+    lat_even = even(lat)
     rows = c_ref.shape[0]
-    xa, xb = xa_ref[...].astype(F32), jnp.where(at_pole(lat), 0.0, xb_ref[...].astype(F32))
+    end, tap = (1, 0) if is_last else (0, 2)
+    xa, xb = (ref[end : end + 1].astype(F32) for ref in (xa_ref, xb_ref))
+    xb = jnp.where(at_pole(lat), 0.0, xb)
     above, below = jnp.where(lat_even, xb, xa), jnp.where(lat_even, xa, xb)
     sub = lax.broadcasted_iota(jnp.int32, c_ref.shape, 0)
     here = c_ref[...].astype(F32)
-    up, down = (jnp.where(is_last, end[1:2], end[0:1]) for end in (above, below))
-    up = jnp.where(sub == 0, up, pltpu.roll(here, 1, 0))
-    down = jnp.where(sub == rows - 1, down, pltpu.roll(here, rows - 1, 0))
-    tap = [jnp.where(is_last, taps_ref[i, 0:1], taps_ref[i, 2:3]) for i in range(3)]
-    o_ref[...] = (tap[0] * up + tap[1] * here + tap[2] * down).astype(BF16)
+    above = jnp.where(sub == 0, above, pltpu.roll(here, 1, 0))
+    below = jnp.where(sub == rows - 1, below, pltpu.roll(here, rows - 1, 0))
+    tap = [taps_ref[i, tap : tap + 1] for i in range(3)]
+    o_ref[...] = (tap[0] * above + tap[1] * here + tap[2] * below).astype(BF16)
 
 
 def gelu(x):
@@ -154,10 +148,10 @@
 
 
 def inner_kernel(*refs, aliased, early, chunk):
-    ins, refs = refs[:7], refs[7 + aliased :]
+    ins, refs = refs[:8], refs[8 + aliased :]
     outs, (rel_ref, polar_ref, sem) = refs[:-3], refs[-3:]
-    e_ref, taps_ref, shift_ref, land_raw, w_hbm, rel_hbm, polar_hbm = ins
-    act_ref, edge_ref, land_ref, w_ref, bias_ref = outs[:5]
+    e_ref, taps_ref, shift_ref, land_raw, w_hbm, rel_hbm, polar_hbm, stream_hbm = ins
+    act_ref, edge_ref, land_ref, w_ref, bias_ref, stream_ref = outs[:6]
     rows, cols, width_exp = e_ref.shape
     here = lax.axis_index("nlo") == 0
 
@@ -168,6 +162,7 @@
             for i, (src, dst) in enumerate(
                 (
                     (rel_hbm, rel_ref), (polar_hbm, polar_ref), (w_hbm, w_ref),
+                    (stream_hbm, stream_ref),
                 )
             )
         ]
@@ -240,17 +235,15 @@
 
 
 def edge_kernel(
-    edge_ref, ca_ref, cb_ref, w_ref, stream_ref, sent_ref, inner_ref, mixed_ref, out_ref,
-    *, lon, chunk,
+    edge_ref, left_ref, right_ref, w_ref, stream_ref, sent_ref, inner_ref, mixed_ref, out_ref,
+    *, chunk,
 ):
     double, width_exp = edge_ref.shape
     rows = double // 2
-    lon_even = even(lon)
     projected = 0.0
     for at in range(0, width_exp, chunk):
         lanes = slice(at, at + chunk)
-        ca, cb = ca_ref[:, lanes].astype(F32), cb_ref[:, lanes].astype(F32)
-        beyond = jnp.where(lon_even, cb, ca), jnp.where(lon_even, ca, cb)
+        beyond = [ref[:, lanes].astype(F32) for ref in (left_ref, right_ref)]
         act = gelu(edge_ref[:, lanes] + jnp.concatenate(beyond, axis=0)).astype(BF16)
         projected += jnp.dot(act, w_ref[lanes, :], preferred_element_type=F32)
     cols = stream_ref.shape[1]
@@ -288,40 +281,65 @@
     x = x_buf[...].astype(BF16)
     scale = np.float32(head_dim**-0.5) * LOG2E
     per = 128 // head_dim
-    packs = heads // per
+    wide = 256
     row_head = lax.broadcasted_iota(jnp.int32, (128, tokens), 0) // head_dim
     ones = jnp.ones((16, tokens), BF16)
-    both = 2 * width
-    qk_buf[...] = jnp.dot(x, w_ref[:, :both], preferred_element_type=F32).astype(BF16)
-    v_buf[...] = jnp.dot(x, w_ref[:, both:], preferred_element_type=F32).astype(BF16)
-    for p in range(packs):
-        q = jnp.transpose(qk_buf[:, 128 * p : 128 * (p + 1)])
-        queries = jnp.concatenate(
-            [jnp.where(row_head == j, q, jnp.zeros_like(q)) for j in range(per)], axis=1
-        )
-        keys = qk_buf[:, width + 128 * p : width + 128 * (p + 1)]
-        span = slice(per * tokens * p, per * tokens * (p + 1))
-        s_buf[:, span] = jnp.dot(keys, queries, preferred_element_type=F32)
-    for h in range(heads):
-        base = bias_ref[h]
-        bias = jnp.concatenate(
-            [base if n == 0 else pltpu.roll(base, 2 * GRID * n, 1) for n in range(GRID)], axis=0
-        )
-        span = slice(tokens * h, tokens * (h + 1))
-        s = s_buf[:, span] * scale + bias
-        p_buf[:, span] = jnp.exp2(s - jnp.max(s, axis=0, keepdims=True)).astype(BF16)
-    for p in range(packs):
-        values = jnp.concatenate([jnp.transpose(v_buf[:, 128 * p : 128 * (p + 1)]), ones], axis=0)
-        span = slice(per * tokens * p, per * tokens * (p + 1))
-        summed = jnp.dot(values, p_buf[:, span], preferred_element_type=F32)
-        for j in range(per):
-            block = summed[:, tokens * j : tokens * (j + 1)]
-            at = 128 * p + head_dim * j
-            t_buf[at : at + head_dim, :] = block[head_dim * j : head_dim * (j + 1)] * (
-                1.0 / block[128:129]
+
+    def packs(g):
+        return range(g * wide // 128, (g + 1) * wide // 128)
+
+    def span(p):
+        return slice(per * tokens * p, per * tokens * (p + 1))
+
+    def project(g):
+        for i, ref, at in ((0, qk_buf, 0), (1, qk_buf, width), (2, v_buf, 0)):
+            lanes = slice(wide * g, wide * (g + 1))
+            w = w_ref[:, i * width + lanes.start : i * width + lanes.stop]
+            ref[:, at + lanes.start : at + lanes.stop] = jnp.dot(
+                x, w, preferred_element_type=F32
+            ).astype(BF16)
+
+    def score(g):
+        for p in packs(g):
+            q = jnp.transpose(qk_buf[:, 128 * p : 128 * (p + 1)])
+            queries = jnp.concatenate(
+                [jnp.where(row_head == j, q, jnp.zeros_like(q)) for j in range(per)], axis=1
             )
-    for p in range(packs):
-        x_buf[:, 128 * p : 128 * (p + 1)] = jnp.transpose(t_buf[128 * p : 128 * (p + 1), :])
+            keys = qk_buf[:, width + 128 * p : width + 128 * (p + 1)]
+            s_buf[:, span(p)] = jnp.dot(keys, queries, preferred_element_type=F32)
+
+    def weigh(g):
+        for h in range(g * wide // head_dim, (g + 1) * wide // head_dim):
+            base = bias_ref[h]
+            bias = jnp.concatenate(
+                [base if n == 0 else pltpu.roll(base, 2 * GRID * n, 1) for n in range(GRID)], axis=0
+            )
+            lanes = slice(tokens * h, tokens * (h + 1))
+            s = s_buf[:, lanes] * scale + bias
+            p_buf[:, lanes] = jnp.exp2(s - jnp.max(s, axis=0, keepdims=True)).astype(BF16)
+
+    def gather(g):
+        for p in packs(g):
+            values = jnp.concatenate(
+                [jnp.transpose(v_buf[:, 128 * p : 128 * (p + 1)]), ones], axis=0
+            )
+            summed = jnp.dot(values, p_buf[:, span(p)], preferred_element_type=F32)
+            for j in range(per):
+                block = summed[:, tokens * j : tokens * (j + 1)]
+                at = 128 * p + head_dim * j
+                t_buf[at : at + head_dim, :] = block[head_dim * j : head_dim * (j + 1)] * (
+                    1.0 / block[128:129]
+                )
+
+    def turn(g):
+        for p in packs(g):
+            x_buf[:, 128 * p : 128 * (p + 1)] = jnp.transpose(t_buf[128 * p : 128 * (p + 1), :])
+
+    for stage, g in (
+        (project, 0), (project, 1), (score, 0), (project, 2), (score, 1), (weigh, 0), (score, 2),
+        (weigh, 1), (gather, 0), (weigh, 2), (gather, 1), (turn, 0), (gather, 2), (turn, 1), (turn, 2),
+    ):
+        stage(g)
     for k in range(tokens // 4):
         out_ref[k] = x_buf[4 * k : 4 * k + 4, :].astype(BF16)
 
@@ -364,47 +382,44 @@
 
     row_shape, col_shape = ((cols, width_exp), BF16), ((rows, width_exp), BF16)
     end_shape = ((2, width_exp), BF16)
-    small = (expanded, dw_kernel, land_shift[None], land, stream)
-    e_here, taps, shift, land, stream, *picked = call(
-        functools.partial(pick_kernel, lat=lat, lon=lon), "pick", map(in_hbm, small), [HBM] * 5,
+    small = (expanded, dw_kernel, land_shift[None], land)
+    e_here, taps, shift, land, *picked = call(
+        functools.partial(pick_kernel, lat=lat), "pick", map(in_hbm, small), [HBM] * 4,
         [(x.shape, x.dtype) for x in small] + [end_shape] * 2 + [row_shape] * 2 + [col_shape] * 2,
-        [pltpu.VMEM((rows, width_exp), F32)] * 2 + [pltpu.SemaphoreType.DMA((rows + 4,))], 8,
+        [pltpu.SemaphoreType.DMA((4,))], 8,
     )
     rel = jnp.transpose(rel_bias, (1, 2, 0)).reshape(-1, heads)
     chunk = 256
-    fixed = (e_here, taps, shift, land, *map(in_hbm, (w_proj, rel, polar)))
+    fixed = (e_here, taps, shift, land, *map(in_hbm, (w_proj, rel, polar, stream)))
     inner_outs = [
         ((tokens, width_exp), BF16), ((2 * rows, width_exp), F32), ((tokens, 128), F32),
-        (w_proj.shape, BF16), ((heads, 2 * GRID, 128), F32),
+        (w_proj.shape, BF16), ((heads, 2 * GRID, 128), F32), (stream.shape, BF16),
     ]
     inner_scratch = [
-        pltpu.VMEM(rel.shape, F32), pltpu.SMEM(polar.shape, jnp.int32), pltpu.SemaphoreType.DMA((3,)),
+        pltpu.VMEM(rel.shape, F32), pltpu.SMEM(polar.shape, jnp.int32), pltpu.SemaphoreType.DMA((4,)),
     ]
-    end_a, end_b, row_a, row_b, col_a, col_b = picked
+    end_a, end_b, row_a, row_b, first, last = picked
     far_a = lax.ppermute(end_a, lat, swap_core)
     far_b = lax.ppermute(end_b, lat, swap_next)
     got_a = lax.ppermute(row_a, lat, swap_core)
     got_b = lax.ppermute(row_b, lat, swap_next)
     *inner, far_a = call(
         functools.partial(inner_kernel, aliased=1, early=True, chunk=chunk), "inner_early",
-        (*fixed, far_a), [VM] * 4 + [HBM] * 3 + [VM],
-        inner_outs + [end_shape], inner_scratch, 8, input_output_aliases={7: 5},
+        (*fixed, far_a), [VM] * 4 + [HBM] * 4 + [VM],
+        inner_outs + [end_shape], inner_scratch, 8, input_output_aliases={8: 6},
     )
     packed = []
-    for second, column in enumerate((col_a, col_b)):
+    for column, is_last in ((last, True), (first, False)):
         packed += call(
-            functools.partial(pack_kernel, lat=lat, lon=lon, second=bool(second)), "pack",
-            (column, far_a, far_b, taps, *packed), [VM] * (4 + second), [col_shape], [], 4,
+            functools.partial(pack_kernel, lat=lat, is_last=is_last), "pack",
+            (column, far_a, far_b, taps, *packed), [VM] * (4 + len(packed)), [col_shape], [], 4,
         )
-    col_a, col_b = packed
-    seen_a = lax.ppermute(col_a, lon, [(i, i ^ 1) for i in range(lons)])
-    seen_b = lax.ppermute(
-        col_b, lon, [(i, (i + 1) % lons if i % 2 else (i - 1) % lons) for i in range(lons)]
-    )
-    act, edge, land_lanes, w_proj, bias, *_ = call(
-        functools.partial(inner_kernel, aliased=6, early=False, chunk=chunk), "inner_late",
-        (*fixed, *inner, col_a), [VM] * 4 + [HBM] * 3 + [VM] * 6, inner_outs, inner_scratch, 8,
-        input_output_aliases={7 + i: i for i in range(5)},
+    from_left = lax.ppermute(packed[0], lon, [(i, (i + 1) % lons) for i in range(lons)])
+    from_right = lax.ppermute(packed[1], lon, [(i, (i - 1) % lons) for i in range(lons)])
+    act, edge, land_lanes, w_proj, bias, stream = call(
+        functools.partial(inner_kernel, aliased=7, early=False, chunk=chunk), "inner_late",
+        (*fixed, *inner, packed[0]), [VM] * 4 + [HBM] * 4 + [VM] * 7, inner_outs, inner_scratch, 8,
+        input_output_aliases={8 + i: i for i in range(6)},
         cost_estimate=pl.CostEstimate(flops=10**9, bytes_accessed=10**6, transcendentals=0),
     )
     token_shape, sent_shape = ((tokens, width), BF16), ((tokens // 4, 4, width), BF16)
@@ -423,8 +438,8 @@
         cost_estimate=pl.CostEstimate(flops=10**9, bytes_accessed=10**6, transcendentals=0),
     )
     mixed, sent = call(
-        functools.partial(edge_kernel, lon=lon, chunk=width), "edge",
-        (edge, seen_a, seen_b, w_proj, stream, sent, mixed), [VM] * 7,
+        functools.partial(edge_kernel, chunk=width), "edge",
+        (edge, from_left, from_right, w_proj, stream, sent, mixed), [VM] * 7,
         [token_shape, sent_shape], [], 8, input_output_aliases={5: 1, 6: 0},
     )
 

time: 47.6 us -> 46.6 us (0.979)
  starting transfers between devices: 13.6 us -> 12.8 us
    ppermute x2, starting transfers between devices: 8.41 us -> 7.66 us  [the longest x1 7.57 us: local(): lax.ppermute(packed[1], lon, [(i, (i - 1) % lons) for i in range(lons)])]
where the time goes in v4:
time: 46.6 us; the launch traced here: 46.4 us
  blocking collectives  23.7 us (51%)
  starting transfers between devices  12.8 us (27%)
  Pallas kernels  9.78 us (21%)
    all_to_all x1, blocking collectives, local(): back = lax.all_to_all(attended, group, 0, 0, tiled=True)  12.2 us
    all_to_all x1, blocking collectives, local(): mine = lax.all_to_all(sent, group, 0, 0, tiled=True)  11.5 us
    ppermute x1, starting transfers between devices, local(): lax.ppermute(packed[1], lon, [(i, (i - 1) % lons) for i in range(lons)])  7.57 us
    pallas_call x7, Pallas kernels, call(): pl.pallas_call(kernel, name=name, out_shape=tuple((pltpu.VMEM(shape, dtyp...  7.29 us
    ppermute x1, starting transfers between devices, local(): far_a = lax.ppermute(end_a, lat, swap_core)  3.33 us
    ppermute x1, starting transfers between devices, local(): got_b = lax.ppermute(row_b, lat, swap_next)  1.65 us
    pallas_call x1, Pallas kernels, local(): pl.pallas_call(functools.partial(attend_kernel, heads=heads), name='atten...  1.43 us
    pallas_call x1, Pallas kernels, local(): pl.pallas_call(functools.partial(out_kernel, rows=rows, cols=cols), name=...  1.06 us
  transfers between devices with their start and end apart: 6, of which 0 were waited for; matrix products, arithmetic and copies ran while one was open for 0% of the time, Pallas kernels for 11%

profile of v4, /device:TPU:1, one launch (start us, length us, event | category | flops | bytes accessed | tf_op | source)
XLA Modules:
  0.0 46.4 jit_solution(824289546930118198)
XLA Ops:
  0.0 1.4 %pick.1 = (bf16[8,16,3072]{2,1,0:T(8,128)(2,1)S(1)}, f32[3,3,3072]{2,1,0:T(4,128)S(1)}, f32[1,3072]{1,0:T(1,128)S(1)}, s32[8,16]{1,0:T(8,128)S(1)}, bf16[2,3072]...) custom-call(bf16[8,16,3072]{2,1,0:T(8,128)(2,1)} %refs_0_.1, ...), custom_call_target="tpu_custom_call" | custom-call | tf_op jit(solution)/shard_map/pick/pallas_call | solution.py:372
  1.4 3.3 %collective-permute-start.2 = (bf16[2,3072]{1,0:T(2,128)(2,1)S(1)}, bf16[2,3072]{1,0:T(2,128)(2,1)S(1)}, u32[]{:S(2)}, u32[]{:S(2)}) collective-permute-start(bf16[2,3072]{1,0:T(2,128)(2,1)S(1)} %get-tuple-element.41), channel_id=1, source_target_pairs={{0,1},{1,0},{2,3},{3,2},{4,5},{5,4},{6,7},{7,6},{8,9},{9,8},{10,11... | collective-permute-start | bytes 36872 | tf_op jit(solution)/shard_map/ppermute | solution.py:402
  4.7 0.0 collective-permute-start.3
  4.7 0.2 collective-permute-start
  4.9 1.6 %collective-permute-start.1 = (bf16[16,3072]{1,0:T(8,128)(2,1)S(1)}, bf16[16,3072]{1,0:T(8,128)(2,1)S(1)}, u32[]{:S(2)}, u32[]{:S(2)}) collective-permute-start(bf16[16,3072]{1,0:T(8,128)(2,1)S(1)} %get-tuple-element.37), channel_id=1, source_target_pairs={{0,3},{1,2},{2,1},{3,0},{4,7},{5,6},{6,5},{7,4},{8,11},{9,10},{10,... | collective-permute-start | bytes 294920 | tf_op jit(solution)/shard_map/ppermute | solution.py:405
  6.5 0.0 collective-permute-done.2.refs_8_
  6.5 2.4 %inner_early.1 = (bf16[128,3072]{1,0:T(8,128)(2,1)S(1)}, f32[16,3072]{1,0:T(8,128)S(1)}, f32[128,128]{1,0:T(8,128)S(1)}, bf16[3072,768]{1,0:T(8,128)(2,1)S(1)}, ...) custom-call(bf16[8,16,3072]{2,1,0:T(8,128)(2,1)S(1)} %get-tuple-elem, ...), custom_call_target="tpu_custom_call", output_to_operand_aliasing={{6}: (8, {})} | custom-call | tf_op jit(solution)/shard_map/inner_early/pallas_call | solution.py:372
  9.0 0.0 collective-permute-done.3.xb_ref
  9.0 0.1 pack.2.refs_14_.refs_0_
  9.1 0.1 collective-permute-start.4
  9.2 0.1 pack.3
  9.2 7.6 %collective-permute-start.5 = (bf16[8,3072]{1,0:T(8,128)(2,1)S(1)}, bf16[8,3072]{1,0:T(8,128)(2,1)S(1)}, u32[]{:S(2)}, u32[]{:S(2)}) collective-permute-start(bf16[8,3072]{1,0:T(8,128)(2,1)S(1)} %pack.3), channel_id=1, source_target_pairs={{0,252},{4,0},{8,4},{12,8},{16,12},{20,16},{24,20},{28,24},{32,28}... | collective-permute-start | bytes 147464 | tf_op jit(solution)/shard_map/ppermute | solution.py:418
  16.8 0.0 collective-permute-done.ra_ref
  16.9 0.0 collective-permute-done.1.rb_ref
  16.9 2.4 %mix.1 = (bf16[128,768]{1,0:T(8,128)(2,1)S(1)}, bf16[32,4,768]{2,1,0:T(4,128)(2,1)S(1)}, bf16[128,3072]{1,0:T(8,128)(2,1)S(1)}, f32[16,3072]{1,0:T(8,128)S(1)}, ...) custom-call(bf16[8,16,3072]{2,1,0:T(8,128)(2,1)S(1)} %get-tuple-elemen, ...), custom_call_target="tpu_custom_call", output_to_operand_aliasing={{2}: (10, {}), {3}: (11, {})} | custom-call | flops 1000000000 | bytes 1000000 | tf_op jit(solution)/shard_map/mix/pallas_call | solution.py:372
  19.2 0.0 collective-permute-done.5.right_ref
  19.2 0.0 collective-permute-done.4.left_ref
  19.3 1.0 %edge.1 = (bf16[128,768]{1,0:T(8,128)(2,1)S(1)}, bf16[32,4,768]{2,1,0:T(4,128)(2,1)S(1)}) custom-call(f32[16,3072]{1,0:T(8,128)S(1)} %get-tuple-element.56.edge_ref, bf16[8,3072]{1,0:T(8,128)(2,1)S(1)} %collective-permute-done.4.left_ref, bf16[8,3072]{1,0:T(8,128)(2,1)S(1)} %collective-permute-done.5.right_ref, ...), custom_call_target="tpu_custom_call", output_to_operand_aliasing={{1}: (5, {}), {0}: (6, {})} | custom-call | tf_op jit(solution)/shard_map/edge/pallas_call | solution.py:372
  20.2 11.5 %all_to_all.10.x_ref = bf16[32,4,768]{2,1,0:T(4,128)(2,1)S(1)} all-to-all(bf16[32,4,768]{2,1,0:T(4,128)(2,1)S(1)} %get-tuple-element.60), channel_id=1, replica_groups=mesh['nhi'=8,'nlo'=8,'lat'=4] {'nhi','lat'}, dimensions={0} | all-to-all | bytes 393216 | tf_op jit(solution)/shard_map/all_to_all | solution.py:447
  31.8 1.4 %attend.1 = bf16[32,4,768]{2,1,0:T(4,128)(2,1)S(1)} custom-call(bf16[32,4,768]{2,1,0:T(4,128)(2,1)S(1)} %all_to_all.10.x_ref, bf16[768,2304]{1,0:T(8,128)(2,1)S(1)} %get-tuple-element.61.w_ref, f32[24,16,128]{2,1,0:T(8,128)S(1)} %get-tuple-element.62.bias_ref), custom_call_target="tpu_custom_call" | custom-call | tf_op jit(solution)/shard_map/attend/pallas_call | solution.py:448
  33.2 12.2 %all_to_all.11.a_ref = bf16[32,4,768]{2,1,0:T(4,128)(2,1)S(1)} all-to-all(bf16[32,4,768]{2,1,0:T(4,128)(2,1)S(1)} %attend.1), channel_id=1, replica_groups=mesh['nhi'=8,'nlo'=8,'lat'=4] {'nhi','lat'}, dimensions={0} | all-to-all | bytes 393216 | tf_op jit(solution)/shard_map/all_to_all | solution.py:461
  45.4 1.1 %out.1 = bf16[128,768]{1,0:T(8,128)(2,1)} custom-call(bf16[32,4,768]{2,1,0:T(4,128)(2,1)S(1)} %all_to_all.11.a_ref, bf16[768,768]{1,0:T(8,128)(2,1)S(1)} %get-tuple-element.63.w_ref, bf16[128,768]{1,0:T(8,128)(2,1)S(1)} %get-tuple-element.64.mixed_ref), custom_call_target="tpu_custom_call" | custom-call | tf_op jit(solution)/shard_map/out/pallas_call | solution.py:462
  (1 shorter events, 0.0 us)
Async XLA Ops:
  1.4 5.2 %collective-permute-start.2 = (bf16[2,3072]{1,0:T(2,128)(2,1)S(1)}, bf16[2,3072]{1,0:T(2,128)(2,1)S(1)}, u32[]{:S(2)}, u32[]{:S(2)}) collective-permute-start(bf16[2,3072]{1,0:T(2,128)(2,1)S(1)} %get-tuple-element.41), channel_id=1, source_target_pairs={{0,1},{1,0},{2,3},{3,2},{4,5},{5,4},{6,7},{7,6},{8,9},{9,8},{10,11... | collective-permute-start | bytes 36872 | tf_op jit(solution)/shard_map/ppermute | solution.py:402
  4.7 4.3 %collective-permute-start.3 = (bf16[2,3072]{1,0:T(2,128)(2,1)S(1)}, bf16[2,3072]{1,0:T(2,128)(2,1)S(1)}, u32[]{:S(2)}, u32[]{:S(2)}) collective-permute-start(bf16[2,3072]{1,0:T(2,128)(2,1)S(1)} %get-tuple-element.50), channel_id=1, source_target_pairs={{0,3},{1,2},{2,1},{3,0},{4,7},{5,6},{6,5},{7,4},{8,11},{9,10},{10,... | collective-permute-start | bytes 36872 | tf_op jit(solution)/shard_map/ppermute | solution.py:403
  4.7 12.1 %collective-permute-start = (bf16[16,3072]{1,0:T(8,128)(2,1)S(1)}, bf16[16,3072]{1,0:T(8,128)(2,1)S(1)}, u32[]{:S(2)}, u32[]{:S(2)}) collective-permute-start(bf16[16,3072]{1,0:T(8,128)(2,1)S(1)} %get-tuple-element.36), channel_id=1, source_target_pairs={{0,1},{1,0},{2,3},{3,2},{4,5},{5,4},{6,7},{7,6},{8,9},{9,8},{10,11... | collective-permute-start | bytes 294920 | tf_op jit(solution)/shard_map/ppermute | solution.py:404
  4.9 12.0 %collective-permute-start.1 = (bf16[16,3072]{1,0:T(8,128)(2,1)S(1)}, bf16[16,3072]{1,0:T(8,128)(2,1)S(1)}, u32[]{:S(2)}, u32[]{:S(2)}) collective-permute-start(bf16[16,3072]{1,0:T(8,128)(2,1)S(1)} %get-tuple-element.37), channel_id=1, source_target_pairs={{0,3},{1,2},{2,1},{3,0},{4,7},{5,6},{6,5},{7,4},{8,11},{9,10},{10,... | collective-permute-start | bytes 294920 | tf_op jit(solution)/shard_map/ppermute | solution.py:405
  9.1 10.2 %collective-permute-start.4 = (bf16[8,3072]{1,0:T(8,128)(2,1)S(1)}, bf16[8,3072]{1,0:T(8,128)(2,1)S(1)}, u32[]{:S(2)}, u32[]{:S(2)}) collective-permute-start(bf16[8,3072]{1,0:T(8,128)(2,1)S(1)} %pack.2.refs_14_.refs_0_), channel_id=1, source_target_pairs={{0,4},{4,8},{8,12},{12,16},{16,20},{20,24},{24,28},{28,32},{32,36}... | collective-permute-start | bytes 147464 | tf_op jit(solution)/shard_map/ppermute | solution.py:417
  9.2 10.0 %collective-permute-start.5 = (bf16[8,3072]{1,0:T(8,128)(2,1)S(1)}, bf16[8,3072]{1,0:T(8,128)(2,1)S(1)}, u32[]{:S(2)}, u32[]{:S(2)}) collective-permute-start(bf16[8,3072]{1,0:T(8,128)(2,1)S(1)} %pack.3), channel_id=1, source_target_pairs={{0,252},{4,0},{8,4},{12,8},{16,12},{20,16},{24,20},{28,24},{32,28}... | collective-permute-start | bytes 147464 | tf_op jit(solution)/shard_map/ppermute | solution.py:418

commit v5 on v4

--- a/solution.py
+++ b/solution.py
@@ -70,8 +70,7 @@
         copy.wait()
 
 
-def pack_kernel(c_ref, xa_ref, xb_ref, taps_ref, *refs, lat, is_last):
-    o_ref = refs[-1]
+def pack_kernel(c_ref, xa_ref, xb_ref, taps_ref, o_ref, *, lat, is_last):
     lat_even = even(lat)
     rows = c_ref.shape[0]
     end, tap = (1, 0) if is_last else (0, 2)
@@ -403,22 +402,25 @@
     far_b = lax.ppermute(end_b, lat, swap_next)
     got_a = lax.ppermute(row_a, lat, swap_core)
     got_b = lax.ppermute(row_b, lat, swap_next)
-    *inner, far_a = call(
-        functools.partial(inner_kernel, aliased=1, early=True, chunk=chunk), "inner_early",
-        (*fixed, far_a), [VM] * 4 + [HBM] * 4 + [VM],
-        inner_outs + [end_shape], inner_scratch, 8, input_output_aliases={8: 6},
-    )
-    packed = []
-    for column, is_last in ((last, True), (first, False)):
-        packed += call(
+
+    def pack(column, is_last):
+        return call(
             functools.partial(pack_kernel, lat=lat, is_last=is_last), "pack",
-            (column, far_a, far_b, taps, *packed), [VM] * (4 + len(packed)), [col_shape], [], 4,
-        )
-    from_left = lax.ppermute(packed[0], lon, [(i, (i + 1) % lons) for i in range(lons)])
-    from_right = lax.ppermute(packed[1], lon, [(i, (i - 1) % lons) for i in range(lons)])
+            (column, far_a, far_b, taps), [VM] * 4, [col_shape], [], 4,
+        )[0]
+
+    rightward = pack(last, True)
+    from_left = lax.ppermute(rightward, lon, [(i, (i + 1) % lons) for i in range(lons)])
+    *inner, first = call(
+        functools.partial(inner_kernel, aliased=2, early=True, chunk=chunk), "inner_early",
+        (*fixed, first, rightward), [VM] * 4 + [HBM] * 4 + [VM] * 2,
+        inner_outs + [col_shape], inner_scratch, 8, input_output_aliases={8: 6},
+    )
+    leftward = pack(first, False)
+    from_right = lax.ppermute(leftward, lon, [(i, (i - 1) % lons) for i in range(lons)])
     act, edge, land_lanes, w_proj, bias, stream = call(
         functools.partial(inner_kernel, aliased=7, early=False, chunk=chunk), "inner_late",
-        (*fixed, *inner, packed[0]), [VM] * 4 + [HBM] * 4 + [VM] * 7, inner_outs, inner_scratch, 8,
+        (*fixed, *inner, leftward), [VM] * 4 + [HBM] * 4 + [VM] * 7, inner_outs, inner_scratch, 8,
         input_output_aliases={8 + i: i for i in range(6)},
         cost_estimate=pl.CostEstimate(flops=10**9, bytes_accessed=10**6, transcendentals=0),
     )

time: 46.6 us -> 46.4 us (level)
  waiting for transfers between devices: 0.02 us -> 1.73 us
  starting transfers between devices: 12.8 us -> 11.2 us
    ppermute x1, waiting for transfers between devices: 0.01 us -> 1.71 us  [local(): far_b = lax.ppermute(end_b, lat, swap_next)]
    ppermute x2, starting transfers between devices: 7.66 us -> 6.02 us  [the longest x1 5.94 us: local(): lax.ppermute(leftward, lon, [(i, (i - 1) % lons) for i in range(lons)])]
  transfers between devices with their start and end apart: 6 -> 6, of which waited for: 0 -> 1; matrix products, arithmetic and copies ran while one was open for 0% -> 0% of each run, Pallas kernels for 11% -> 11%
where the time goes in v5:
time: 46.4 us; the launch traced here: 46.2 us
  blocking collectives  23.4 us (50%)
  starting transfers between devices  11.2 us (24%)
  Pallas kernels  9.77 us (21%)
  waiting for transfers between devices  1.73 us (4%)
    all_to_all x1, blocking collectives, local(): back = lax.all_to_all(attended, group, 0, 0, tiled=True)  12.2 us
    all_to_all x1, blocking collectives, local(): mine = lax.all_to_all(sent, group, 0, 0, tiled=True)  11.2 us
    pallas_call x7, Pallas kernels, call(): pl.pallas_call(kernel, name=name, out_shape=tuple((pltpu.VMEM(shape, dtyp...  7.31 us
    ppermute x1, starting transfers between devices, local(): lax.ppermute(leftward, lon, [(i, (i - 1) % lons) for i in range(lons)])  5.94 us
    ppermute x1, starting transfers between devices, local(): far_a = lax.ppermute(end_a, lat, swap_core)  3.33 us
    ppermute x1, waiting for transfers between devices, local(): far_b = lax.ppermute(end_b, lat, swap_next)  1.71 us
    ppermute x1, starting transfers between devices, local(): got_b = lax.ppermute(row_b, lat, swap_next)  1.65 us
    pallas_call x1, Pallas kernels, local(): pl.pallas_call(functools.partial(attend_kernel, heads=heads), name='atten...  1.41 us
  transfers between devices with their start and end apart: 6, of which 1 were waited for; matrix products, arithmetic and copies ran while one was open for 0% of the time, Pallas kernels for 11%

profile of v5, /device:TPU:1, one launch (start us, length us, event | category | flops | bytes accessed | tf_op | source)
XLA Modules:
  0.0 46.2 jit_solution(5241858510854180808)
XLA Ops:
  0.0 1.4 %pick.1 = (bf16[8,16,3072]{2,1,0:T(8,128)(2,1)S(1)}, f32[3,3,3072]{2,1,0:T(4,128)S(1)}, f32[1,3072]{1,0:T(1,128)S(1)}, s32[8,16]{1,0:T(8,128)S(1)}, bf16[2,3072]...) custom-call(bf16[8,16,3072]{2,1,0:T(8,128)(2,1)} %refs_0_.1, ...), custom_call_target="tpu_custom_call" | custom-call | tf_op jit(solution)/shard_map/pick/pallas_call | solution.py:371
  1.4 3.3 %collective-permute-start.2 = (bf16[2,3072]{1,0:T(2,128)(2,1)S(1)}, bf16[2,3072]{1,0:T(2,128)(2,1)S(1)}, u32[]{:S(2)}, u32[]{:S(2)}) collective-permute-start(bf16[2,3072]{1,0:T(2,128)(2,1)S(1)} %get-tuple-element.43), channel_id=1, source_target_pairs={{0,1},{1,0},{2,3},{3,2},{4,5},{5,4},{6,7},{7,6},{8,9},{9,8},{10,11... | collective-permute-start | bytes 36872 | tf_op jit(solution)/shard_map/ppermute | solution.py:401
  4.7 0.0 collective-permute-start.3
  4.7 0.2 collective-permute-start
  4.9 1.6 %collective-permute-start.1 = (bf16[16,3072]{1,0:T(8,128)(2,1)S(1)}, bf16[16,3072]{1,0:T(8,128)(2,1)S(1)}, u32[]{:S(2)}, u32[]{:S(2)}) collective-permute-start(bf16[16,3072]{1,0:T(8,128)(2,1)S(1)} %get-tuple-element.37), channel_id=1, source_target_pairs={{0,3},{1,2},{2,1},{3,0},{4,7},{5,6},{6,5},{7,4},{8,11},{9,10},{10,... | collective-permute-start | bytes 294920 | tf_op jit(solution)/shard_map/ppermute | solution.py:404
  6.5 0.0 collective-permute-done.2.xa_ref
  6.5 1.7 %collective-permute-done.3.xb_ref = bf16[2,3072]{1,0:T(2,128)(2,1)S(1)} collective-permute-done((bf16[2,3072]{1,0:T(2,128)(2,1)S(1)}, bf16[2,3072]{1,0:T(2,128)(2,1)S(1)}, u32[]{:S(2)}, u32[]{:S(2)}) %collective-permute-start.3) | collective-permute-done | bytes 12320 | tf_op jit(solution)/shard_map/ppermute | solution.py:402
  8.3 0.1 pack.2.refs_9_
  8.3 0.1 collective-permute-start.4
  8.4 2.4 %inner_early.1 = (bf16[128,3072]{1,0:T(8,128)(2,1)S(1)}, f32[16,3072]{1,0:T(8,128)S(1)}, f32[128,128]{1,0:T(8,128)S(1)}, bf16[3072,768]{1,0:T(8,128)(2,1)S(1)}, ...) custom-call(bf16[8,16,3072]{2,1,0:T(8,128)(2,1)S(1)} %get-tuple-elem, ...), custom_call_target="tpu_custom_call", output_to_operand_aliasing={{6}: (8, {})} | custom-call | tf_op jit(solution)/shard_map/inner_early/pallas_call | solution.py:371
  10.9 0.1 pack.3.refs_14_
  10.9 5.9 %collective-permute-start.5 = (bf16[8,3072]{1,0:T(8,128)(2,1)S(1)}, bf16[8,3072]{1,0:T(8,128)(2,1)S(1)}, u32[]{:S(2)}, u32[]{:S(2)}) collective-permute-start(bf16[8,3072]{1,0:T(8,128)(2,1)S(1)} %pack.3.refs_14_), channel_id=1, source_target_pairs={{0,252},{4,0},{8,4},{12,8},{16,12},{20,16},{24,20},{28,24},{32,28}... | collective-permute-start | bytes 147464 | tf_op jit(solution)/shard_map/ppermute | solution.py:420
  16.9 0.0 collective-permute-done.ra_ref
  16.9 0.0 collective-permute-done.1.rb_ref
  16.9 2.4 %mix.1 = (bf16[128,768]{1,0:T(8,128)(2,1)S(1)}, bf16[32,4,768]{2,1,0:T(4,128)(2,1)S(1)}, bf16[128,3072]{1,0:T(8,128)(2,1)S(1)}, f32[16,3072]{1,0:T(8,128)S(1)}, ...) custom-call(bf16[8,16,3072]{2,1,0:T(8,128)(2,1)S(1)} %get-tuple-elemen, ...), custom_call_target="tpu_custom_call", output_to_operand_aliasing={{2}: (10, {}), {3}: (11, {})} | custom-call | flops 1000000000 | bytes 1000000 | tf_op jit(solution)/shard_map/mix/pallas_call | solution.py:371
  19.3 0.0 collective-permute-done.4.left_ref
  19.3 0.0 collective-permute-done.5.right_ref
  19.3 1.0 %edge.1 = (bf16[128,768]{1,0:T(8,128)(2,1)S(1)}, bf16[32,4,768]{2,1,0:T(4,128)(2,1)S(1)}) custom-call(f32[16,3072]{1,0:T(8,128)S(1)} %get-tuple-element.57.edge_ref, bf16[8,3072]{1,0:T(8,128)(2,1)S(1)} %collective-permute-done.4.left_ref, bf16[8,3072]{1,0:T(8,128)(2,1)S(1)} %collective-permute-done.5.right_ref, ...), custom_call_target="tpu_custom_call", output_to_operand_aliasing={{1}: (5, {}), {0}: (6, {})} | custom-call | tf_op jit(solution)/shard_map/edge/pallas_call | solution.py:371
  20.3 11.2 %all_to_all.10.x_ref = bf16[32,4,768]{2,1,0:T(4,128)(2,1)S(1)} all-to-all(bf16[32,4,768]{2,1,0:T(4,128)(2,1)S(1)} %get-tuple-element.60), channel_id=1, replica_groups=mesh['nhi'=8,'nlo'=8,'lat'=4] {'nhi','lat'}, dimensions={0} | all-to-all | bytes 393216 | tf_op jit(solution)/shard_map/all_to_all | solution.py:449
  31.5 1.4 %attend.1 = bf16[32,4,768]{2,1,0:T(4,128)(2,1)S(1)} custom-call(bf16[32,4,768]{2,1,0:T(4,128)(2,1)S(1)} %all_to_all.10.x_ref, bf16[768,2304]{1,0:T(8,128)(2,1)S(1)} %get-tuple-element.61.w_ref, f32[24,16,128]{2,1,0:T(8,128)S(1)} %get-tuple-element.62.bias_ref), custom_call_target="tpu_custom_call" | custom-call | tf_op jit(solution)/shard_map/attend/pallas_call | solution.py:450
  32.9 12.2 %all_to_all.11.a_ref = bf16[32,4,768]{2,1,0:T(4,128)(2,1)S(1)} all-to-all(bf16[32,4,768]{2,1,0:T(4,128)(2,1)S(1)} %attend.1), channel_id=1, replica_groups=mesh['nhi'=8,'nlo'=8,'lat'=4] {'nhi','lat'}, dimensions={0} | all-to-all | bytes 393216 | tf_op jit(solution)/shard_map/all_to_all | solution.py:463
  45.1 1.1 %out.1 = bf16[128,768]{1,0:T(8,128)(2,1)} custom-call(bf16[32,4,768]{2,1,0:T(4,128)(2,1)S(1)} %all_to_all.11.a_ref, bf16[768,768]{1,0:T(8,128)(2,1)S(1)} %get-tuple-element.63.w_ref, bf16[128,768]{1,0:T(8,128)(2,1)S(1)} %get-tuple-element.64.mixed_ref), custom_call_target="tpu_custom_call" | custom-call | tf_op jit(solution)/shard_map/out/pallas_call | solution.py:464
  (1 shorter events, 0.0 us)
Async XLA Ops:
  1.4 5.2 %collective-permute-start.2 = (bf16[2,3072]{1,0:T(2,128)(2,1)S(1)}, bf16[2,3072]{1,0:T(2,128)(2,1)S(1)}, u32[]{:S(2)}, u32[]{:S(2)}) collective-permute-start(bf16[2,3072]{1,0:T(2,128)(2,1)S(1)} %get-tuple-element.43), channel_id=1, source_target_pairs={{0,1},{1,0},{2,3},{3,2},{4,5},{5,4},{6,7},{7,6},{8,9},{9,8},{10,11... | collective-permute-start | bytes 36872 | tf_op jit(solution)/shard_map/ppermute | solution.py:401
  4.7 3.6 %collective-permute-start.3 = (bf16[2,3072]{1,0:T(2,128)(2,1)S(1)}, bf16[2,3072]{1,0:T(2,128)(2,1)S(1)}, u32[]{:S(2)}, u32[]{:S(2)}) collective-permute-start(bf16[2,3072]{1,0:T(2,128)(2,1)S(1)} %get-tuple-element.44), channel_id=1, source_target_pairs={{0,3},{1,2},{2,1},{3,0},{4,7},{5,6},{6,5},{7,4},{8,11},{9,10},{10,... | collective-permute-start | bytes 36872 | tf_op jit(solution)/shard_map/ppermute | solution.py:402
  4.7 12.2 %collective-permute-start = (bf16[16,3072]{1,0:T(8,128)(2,1)S(1)}, bf16[16,3072]{1,0:T(8,128)(2,1)S(1)}, u32[]{:S(2)}, u32[]{:S(2)}) collective-permute-start(bf16[16,3072]{1,0:T(8,128)(2,1)S(1)} %get-tuple-element.36), channel_id=1, source_target_pairs={{0,1},{1,0},{2,3},{3,2},{4,5},{5,4},{6,7},{7,6},{8,9},{9,8},{10,11... | collective-permute-start | bytes 294920 | tf_op jit(solution)/shard_map/ppermute | solution.py:403
  4.9 12.0 %collective-permute-start.1 = (bf16[16,3072]{1,0:T(8,128)(2,1)S(1)}, bf16[16,3072]{1,0:T(8,128)(2,1)S(1)}, u32[]{:S(2)}, u32[]{:S(2)}) collective-permute-start(bf16[16,3072]{1,0:T(8,128)(2,1)S(1)} %get-tuple-element.37), channel_id=1, source_target_pairs={{0,3},{1,2},{2,1},{3,0},{4,7},{5,6},{6,5},{7,4},{8,11},{9,10},{10,... | collective-permute-start | bytes 294920 | tf_op jit(solution)/shard_map/ppermute | solution.py:404
  8.3 11.0 %collective-permute-start.4 = (bf16[8,3072]{1,0:T(8,128)(2,1)S(1)}, bf16[8,3072]{1,0:T(8,128)(2,1)S(1)}, u32[]{:S(2)}, u32[]{:S(2)}) collective-permute-start(bf16[8,3072]{1,0:T(8,128)(2,1)S(1)} %pack.2.refs_9_), channel_id=1, source_target_pairs={{0,4},{4,8},{8,12},{12,16},{16,20},{20,24},{24,28},{28,32},{32,36}... | collective-permute-start | bytes 147464 | tf_op jit(solution)/shard_map/ppermute | solution.py:413
  10.9 8.4 %collective-permute-start.5 = (bf16[8,3072]{1,0:T(8,128)(2,1)S(1)}, bf16[8,3072]{1,0:T(8,128)(2,1)S(1)}, u32[]{:S(2)}, u32[]{:S(2)}) collective-permute-start(bf16[8,3072]{1,0:T(8,128)(2,1)S(1)} %pack.3.refs_14_), channel_id=1, source_target_pairs={{0,252},{4,0},{8,4},{12,8},{16,12},{20,16},{24,20},{28,24},{32,28}... | collective-permute-start | bytes 147464 | tf_op jit(solution)/shard_map/ppermute | solution.py:420

commit v6 on v5

--- a/solution.py
+++ b/solution.py
@@ -179,7 +179,7 @@
                 )
             return carry
 
-        lax.fori_loop(0, width_exp // 128, step, 0)
+        lax.fori_loop(0, width_exp // 128, step, 0, unroll=2)
         for copy in copies[:2]:
             copy.wait()
         fill_bias(polar_ref, rel_ref[...], bias_ref, rows // 2, "nhi")
@@ -388,7 +388,7 @@
         [pltpu.SemaphoreType.DMA((4,))], 8,
     )
     rel = jnp.transpose(rel_bias, (1, 2, 0)).reshape(-1, heads)
-    chunk = 256
+    chunk = 768
     fixed = (e_here, taps, shift, land, *map(in_hbm, (w_proj, rel, polar, stream)))
     inner_outs = [
         ((tokens, width_exp), BF16), ((2 * rows, width_exp), F32), ((tokens, 128), F32),

time: 46.4 us -> 46.4 us (level)
  no operation moved by 1% of the time
where the time goes in v6:
time: 46.4 us; the launch traced here: 46.2 us
  blocking collectives  23.4 us (50%)
  starting transfers between devices  11.2 us (24%)
  Pallas kernels  9.76 us (21%)
  waiting for transfers between devices  1.73 us (4%)
    all_to_all x1, blocking collectives, local(): back = lax.all_to_all(attended, group, 0, 0, tiled=True)  12.2 us
    all_to_all x1, blocking collectives, local(): mine = lax.all_to_all(sent, group, 0, 0, tiled=True)  11.2 us
    pallas_call x7, Pallas kernels, call(): pl.pallas_call(kernel, name=name, out_shape=tuple((pltpu.VMEM(shape, dtyp...  7.3 us
    ppermute x1, starting transfers between devices, local(): lax.ppermute(leftward, lon, [(i, (i - 1) % lons) for i in range(lons)])  5.95 us
    ppermute x1, starting transfers between devices, local(): far_a = lax.ppermute(end_a, lat, swap_core)  3.33 us
    ppermute x1, waiting for transfers between devices, local(): far_b = lax.ppermute(end_b, lat, swap_next)  1.71 us
    ppermute x1, starting transfers between devices, local(): got_b = lax.ppermute(row_b, lat, swap_next)  1.65 us
    pallas_call x1, Pallas kernels, local(): pl.pallas_call(functools.partial(attend_kernel, heads=heads), name='atten...  1.41 us
  transfers between devices with their start and end apart: 6, of which 1 were waited for; matrix products, arithmetic and copies ran while one was open for 0% of the time, Pallas kernels for 11%

profile of v6, /device:TPU:1, one launch (start us, length us, event | category | flops | bytes accessed | tf_op | source)
XLA Modules:
  0.0 46.2 jit_solution(12746965375001662629)
XLA Ops:
  0.0 1.4 %pick.1 = (bf16[8,16,3072]{2,1,0:T(8,128)(2,1)S(1)}, f32[3,3,3072]{2,1,0:T(4,128)S(1)}, f32[1,3072]{1,0:T(1,128)S(1)}, s32[8,16]{1,0:T(8,128)S(1)}, bf16[2,3072]...) custom-call(bf16[8,16,3072]{2,1,0:T(8,128)(2,1)} %refs_0_.1, ...), custom_call_target="tpu_custom_call" | custom-call | tf_op jit(solution)/shard_map/pick/pallas_call | solution.py:371
  1.4 3.3 %collective-permute-start.2 = (bf16[2,3072]{1,0:T(2,128)(2,1)S(1)}, bf16[2,3072]{1,0:T(2,128)(2,1)S(1)}, u32[]{:S(2)}, u32[]{:S(2)}) collective-permute-start(bf16[2,3072]{1,0:T(2,128)(2,1)S(1)} %get-tuple-element.43), channel_id=1, source_target_pairs={{0,1},{1,0},{2,3},{3,2},{4,5},{5,4},{6,7},{7,6},{8,9},{9,8},{10,11... | collective-permute-start | bytes 36872 | tf_op jit(solution)/shard_map/ppermute | solution.py:401
  4.7 0.0 collective-permute-start.3
  4.7 0.2 collective-permute-start
  4.9 1.6 %collective-permute-start.1 = (bf16[16,3072]{1,0:T(8,128)(2,1)S(1)}, bf16[16,3072]{1,0:T(8,128)(2,1)S(1)}, u32[]{:S(2)}, u32[]{:S(2)}) collective-permute-start(bf16[16,3072]{1,0:T(8,128)(2,1)S(1)} %get-tuple-element.37), channel_id=1, source_target_pairs={{0,3},{1,2},{2,1},{3,0},{4,7},{5,6},{6,5},{7,4},{8,11},{9,10},{10,... | collective-permute-start | bytes 294920 | tf_op jit(solution)/shard_map/ppermute | solution.py:404
  6.5 0.0 collective-permute-done.2.xa_ref
  6.5 1.7 %collective-permute-done.3.xb_ref = bf16[2,3072]{1,0:T(2,128)(2,1)S(1)} collective-permute-done((bf16[2,3072]{1,0:T(2,128)(2,1)S(1)}, bf16[2,3072]{1,0:T(2,128)(2,1)S(1)}, u32[]{:S(2)}, u32[]{:S(2)}) %collective-permute-start.3) | collective-permute-done | bytes 12320 | tf_op jit(solution)/shard_map/ppermute | solution.py:402
  8.3 0.1 pack.2.refs_9_
  8.3 0.1 collective-permute-start.4
  8.4 2.4 %inner_early.1 = (bf16[128,3072]{1,0:T(8,128)(2,1)S(1)}, f32[16,3072]{1,0:T(8,128)S(1)}, f32[128,128]{1,0:T(8,128)S(1)}, bf16[3072,768]{1,0:T(8,128)(2,1)S(1)}, ...) custom-call(bf16[8,16,3072]{2,1,0:T(8,128)(2,1)S(1)} %get-tuple-elem, ...), custom_call_target="tpu_custom_call", output_to_operand_aliasing={{6}: (8, {})} | custom-call | tf_op jit(solution)/shard_map/inner_early/pallas_call | solution.py:371
  10.9 0.1 pack.3.refs_14_
  10.9 6.0 %collective-permute-start.5 = (bf16[8,3072]{1,0:T(8,128)(2,1)S(1)}, bf16[8,3072]{1,0:T(8,128)(2,1)S(1)}, u32[]{:S(2)}, u32[]{:S(2)}) collective-permute-start(bf16[8,3072]{1,0:T(8,128)(2,1)S(1)} %pack.3.refs_14_), channel_id=1, source_target_pairs={{0,252},{4,0},{8,4},{12,8},{16,12},{20,16},{24,20},{28,24},{32,28}... | collective-permute-start | bytes 147464 | tf_op jit(solution)/shard_map/ppermute | solution.py:420
  16.9 0.0 collective-permute-done.ra_ref
  16.9 0.0 collective-permute-done.1.rb_ref
  16.9 2.4 %mix.1 = (bf16[128,768]{1,0:T(8,128)(2,1)S(1)}, bf16[32,4,768]{2,1,0:T(4,128)(2,1)S(1)}, bf16[128,3072]{1,0:T(8,128)(2,1)S(1)}, f32[16,3072]{1,0:T(8,128)S(1)}, ...) custom-call(bf16[8,16,3072]{2,1,0:T(8,128)(2,1)S(1)} %get-tuple-elemen, ...), custom_call_target="tpu_custom_call", output_to_operand_aliasing={{2}: (10, {}), {3}: (11, {})} | custom-call | flops 1000000000 | bytes 1000000 | tf_op jit(solution)/shard_map/mix/pallas_call | solution.py:371
  19.3 0.0 collective-permute-done.4.left_ref
  19.3 0.0 collective-permute-done.5.right_ref
  19.3 1.0 %edge.1 = (bf16[128,768]{1,0:T(8,128)(2,1)S(1)}, bf16[32,4,768]{2,1,0:T(4,128)(2,1)S(1)}) custom-call(f32[16,3072]{1,0:T(8,128)S(1)} %get-tuple-element.57.edge_ref, bf16[8,3072]{1,0:T(8,128)(2,1)S(1)} %collective-permute-done.4.left_ref, bf16[8,3072]{1,0:T(8,128)(2,1)S(1)} %collective-permute-done.5.right_ref, ...), custom_call_target="tpu_custom_call", output_to_operand_aliasing={{1}: (5, {}), {0}: (6, {})} | custom-call | tf_op jit(solution)/shard_map/edge/pallas_call | solution.py:371
  20.3 11.2 %all_to_all.10.x_ref = bf16[32,4,768]{2,1,0:T(4,128)(2,1)S(1)} all-to-all(bf16[32,4,768]{2,1,0:T(4,128)(2,1)S(1)} %get-tuple-element.60), channel_id=1, replica_groups=mesh['nhi'=8,'nlo'=8,'lat'=4] {'nhi','lat'}, dimensions={0} | all-to-all | bytes 393216 | tf_op jit(solution)/shard_map/all_to_all | solution.py:449
  31.5 1.4 %attend.1 = bf16[32,4,768]{2,1,0:T(4,128)(2,1)S(1)} custom-call(bf16[32,4,768]{2,1,0:T(4,128)(2,1)S(1)} %all_to_all.10.x_ref, bf16[768,2304]{1,0:T(8,128)(2,1)S(1)} %get-tuple-element.61.w_ref, f32[24,16,128]{2,1,0:T(8,128)S(1)} %get-tuple-element.62.bias_ref), custom_call_target="tpu_custom_call" | custom-call | tf_op jit(solution)/shard_map/attend/pallas_call | solution.py:450
  32.9 12.2 %all_to_all.11.a_ref = bf16[32,4,768]{2,1,0:T(4,128)(2,1)S(1)} all-to-all(bf16[32,4,768]{2,1,0:T(4,128)(2,1)S(1)} %attend.1), channel_id=1, replica_groups=mesh['nhi'=8,'nlo'=8,'lat'=4] {'nhi','lat'}, dimensions={0} | all-to-all | bytes 393216 | tf_op jit(solution)/shard_map/all_to_all | solution.py:463
  45.1 1.1 %out.1 = bf16[128,768]{1,0:T(8,128)(2,1)} custom-call(bf16[32,4,768]{2,1,0:T(4,128)(2,1)S(1)} %all_to_all.11.a_ref, bf16[768,768]{1,0:T(8,128)(2,1)S(1)} %get-tuple-element.63.w_ref, bf16[128,768]{1,0:T(8,128)(2,1)S(1)} %get-tuple-element.64.mixed_ref), custom_call_target="tpu_custom_call" | custom-call | tf_op jit(solution)/shard_map/out/pallas_call | solution.py:464
  (1 shorter events, 0.0 us)
Async XLA Ops:
  1.4 5.2 %collective-permute-start.2 = (bf16[2,3072]{1,0:T(2,128)(2,1)S(1)}, bf16[2,3072]{1,0:T(2,128)(2,1)S(1)}, u32[]{:S(2)}, u32[]{:S(2)}) collective-permute-start(bf16[2,3072]{1,0:T(2,128)(2,1)S(1)} %get-tuple-element.43), channel_id=1, source_target_pairs={{0,1},{1,0},{2,3},{3,2},{4,5},{5,4},{6,7},{7,6},{8,9},{9,8},{10,11... | collective-permute-start | bytes 36872 | tf_op jit(solution)/shard_map/ppermute | solution.py:401
  4.7 3.6 %collective-permute-start.3 = (bf16[2,3072]{1,0:T(2,128)(2,1)S(1)}, bf16[2,3072]{1,0:T(2,128)(2,1)S(1)}, u32[]{:S(2)}, u32[]{:S(2)}) collective-permute-start(bf16[2,3072]{1,0:T(2,128)(2,1)S(1)} %get-tuple-element.44), channel_id=1, source_target_pairs={{0,3},{1,2},{2,1},{3,0},{4,7},{5,6},{6,5},{7,4},{8,11},{9,10},{10,... | collective-permute-start | bytes 36872 | tf_op jit(solution)/shard_map/ppermute | solution.py:402
  4.7 12.2 %collective-permute-start = (bf16[16,3072]{1,0:T(8,128)(2,1)S(1)}, bf16[16,3072]{1,0:T(8,128)(2,1)S(1)}, u32[]{:S(2)}, u32[]{:S(2)}) collective-permute-start(bf16[16,3072]{1,0:T(8,128)(2,1)S(1)} %get-tuple-element.36), channel_id=1, source_target_pairs={{0,1},{1,0},{2,3},{3,2},{4,5},{5,4},{6,7},{7,6},{8,9},{9,8},{10,11... | collective-permute-start | bytes 294920 | tf_op jit(solution)/shard_map/ppermute | solution.py:403
  4.9 12.0 %collective-permute-start.1 = (bf16[16,3072]{1,0:T(8,128)(2,1)S(1)}, bf16[16,3072]{1,0:T(8,128)(2,1)S(1)}, u32[]{:S(2)}, u32[]{:S(2)}) collective-permute-start(bf16[16,3072]{1,0:T(8,128)(2,1)S(1)} %get-tuple-element.37), channel_id=1, source_target_pairs={{0,3},{1,2},{2,1},{3,0},{4,7},{5,6},{6,5},{7,4},{8,11},{9,10},{10,... | collective-permute-start | bytes 294920 | tf_op jit(solution)/shard_map/ppermute | solution.py:404
  8.3 11.0 %collective-permute-start.4 = (bf16[8,3072]{1,0:T(8,128)(2,1)S(1)}, bf16[8,3072]{1,0:T(8,128)(2,1)S(1)}, u32[]{:S(2)}, u32[]{:S(2)}) collective-permute-start(bf16[8,3072]{1,0:T(8,128)(2,1)S(1)} %pack.2.refs_9_), channel_id=1, source_target_pairs={{0,4},{4,8},{8,12},{12,16},{16,20},{20,24},{24,28},{28,32},{32,36}... | collective-permute-start | bytes 147464 | tf_op jit(solution)/shard_map/ppermute | solution.py:413
  10.9 8.4 %collective-permute-start.5 = (bf16[8,3072]{1,0:T(8,128)(2,1)S(1)}, bf16[8,3072]{1,0:T(8,128)(2,1)S(1)}, u32[]{:S(2)}, u32[]{:S(2)}) collective-permute-start(bf16[8,3072]{1,0:T(8,128)(2,1)S(1)} %pack.3.refs_14_), channel_id=1, source_target_pairs={{0,252},{4,0},{8,4},{12,8},{16,12},{20,16},{24,20},{28,24},{32,28}... | collective-permute-start | bytes 147464 | tf_op jit(solution)/shard_map/ppermute | solution.py:420
